TPU v7x, 256 devices: a whole 4x4x8 slice. The times are simulated.
256 devices in a mesh: sx: 16 (over z, y_lo), sy: 16 (over x, y_hi, core).
Axes of the slice: x: 4, y: 4 (y_hi: 2, y_lo: 2; y = y_hi * 2 + y_lo), z: 8, core: 2. Of those that a mesh axis runs over, the one named last changes fastest.
Arguments:
- dual_ops: bfloat16 [16, 16, 2048, 2048], P('sx', 'sy'), may hold values from -0.028726213 to 1.0287262
- loads: float32 [16, 16, 2048, 128], P('sx', 'sy'), may hold values from -6 to 6
- kernel_basis: bfloat16 [16, 16, 64, 2048], P('sx', 'sy'), may hold values from -0.13183594 to 0.13183594
- coarse_inverse: bfloat16 [16, 16, 1024, 1024], P('sx', 'sy'), may hold values from -1 to 1
Outputs:
- multipliers: float32 [16, 16, 2048, 128], P('sx', 'sy')
All inputs are finite; a program needn't handle non-finite values.
Results may differ from a plain program's by a relative error of at most 0.0085.
Values may be sent and summed in bfloat16 or wider, within the bound.
No kernel may reach another device: no remote copies, remote signals or barrier semaphores. Data moves between devices by JAX's collectives and lax.ppermute only.
A program may use at most 64 MiB of HBM per device.

v0:
```python
import jax
import jax.numpy as jnp
from jax import lax
from jax.sharding import PartitionSpec as P

ITERS = 3


damping = 0.5


def with_halo(block, sides, width):
    for axis, dim in sides:
        count = lax.axis_size(axis)
        forward = [(i, i + 1) for i in range(count - 1)]
        backward = [(target, source) for source, target in forward]
        low = lax.ppermute(
            lax.slice_in_dim(block, block.shape[dim] - width, None, axis=dim), axis, forward
        )
        high = lax.ppermute(lax.slice_in_dim(block, 0, width, axis=dim), axis, backward)
        block = jnp.concatenate([low, block, high], axis=dim)
    return block


def copy_for_each(array, axis):
    devices = lax.axis_size(axis)
    return lax.all_to_all(
        jnp.broadcast_to(array[None], (devices, *array.shape)), axis, 0, 0, tiled=True
    )


def joined_along(parts, dim):
    shape = list(parts.shape[1:])
    shape[dim] *= parts.shape[0]
    return jnp.moveaxis(parts, 0, dim).reshape(shape)


def collect(array, axis, dim):
    parts = copy_for_each(array, axis)
    return joined_along(parts, dim)


def cut_along(array, dim, devices):
    before, after = (array.shape[:dim], array.shape[dim + 1 :])
    return jnp.moveaxis(array.reshape(*before, devices, -1, *after), dim, 0)


def sent_and_summed(array, axis, dim):
    devices = lax.axis_size(axis)
    parts = lax.all_to_all(cut_along(array, dim, devices), axis, 0, 0, tiled=True)
    return jnp.sum(parts, axis=0)


def combine_faces(values, vertical, beside):
    width = values.shape[0] // 4
    return jnp.concatenate(
        [
            values[:width] - vertical[0],
            values[width : 2 * width] - vertical[3],
            values[2 * width : 3 * width] - beside[0],
            values[3 * width :] - beside[3],
        ],
        axis=0,
    )


def residual_faces(values):
    width = values.shape[0] // 4
    vertical = with_halo(jnp.stack([values[:width], values[width : 2 * width]]), (("sx", 0),), 1)
    beside = with_halo(
        jnp.stack([values[2 * width : 3 * width], values[3 * width :]]), (("sy", 0),), 1
    )
    return combine_faces(values, vertical, beside)


def correction_faces(values):
    width = values.shape[0] // 4
    vertical = with_halo(
        jnp.stack([values[:width], values[width : 2 * width]]).astype(jnp.bfloat16), (("sx", 0),), 1
    ).astype(jnp.float32)
    beside = with_halo(
        jnp.stack([values[2 * width : 3 * width], values[3 * width :]]).astype(jnp.bfloat16),
        (("sy", 0),),
        1,
    ).astype(jnp.float32)
    return combine_faces(values, vertical, beside)


def spread_back(columns, weights):
    return lax.dot_general(
        columns, weights, (((0,), (0,)), ((), ())), preferred_element_type=jnp.float32
    )


def local(dual_ops, loads, kernel_basis, coarse_inverse):
    operator = dual_ops[0, 0]
    right_side = loads[0, 0]
    basis = kernel_basis[0, 0]
    tile = coarse_inverse[0, 0]
    multipliers = jnp.zeros(right_side.shape, jnp.float32)
    for step in range(ITERS):
        product = jnp.dot(
            operator, multipliers.astype(jnp.bfloat16), preferred_element_type=jnp.float32
        )
        residual = residual_faces(right_side - product)
        coarse_in = jnp.dot(
            basis, residual.astype(jnp.bfloat16), preferred_element_type=jnp.float32
        ).astype(jnp.bfloat16)
        partial_rows = jnp.dot(
            tile, collect(coarse_in, "sx", 0), preferred_element_type=jnp.float32
        )
        coarse_out = sent_and_summed(partial_rows, "sy", 0).astype(jnp.bfloat16)
        back = spread_back(basis, coarse_out)
        correction = correction_faces(back)
        multipliers = multipliers + damping * (residual - correction)
    return multipliers[None, None]


def solution(mesh):
    placed = (
        P("sx", "sy", None, None),
        P("sx", "sy", None, None),
        P("sx", "sy", None, None),
        P("sx", "sy", None, None),
    )
    return jax.shard_map(
        local, mesh=mesh, in_specs=placed, out_specs=P("sx", "sy", None, None), check_vma=False
    )
```

profile of v0, /device:TPU:10, one launch (start us, length us, event | category | flops | bytes accessed | tf_op | source)
XLA Modules:
  0.0 273.1 jit_solution(2040839877518512509)
XLA Ops:
  1.7 6.3 %fusion.21 = f32[2048,128]{0,1:T(8,128)S(1)} fusion(bf16[1,1,2048,2048]{3,2,1,0:T(8,128)(2,1)} %param.4, f32[1,1,2048,128]{2,3,1,0:T(8,128)S(1)} %copy.7), kind=kOutput, calls=%fused_computation.14 | convolution fusion | flops 1074003968 | bytes 10485760 | tf_op jit(solution)/shard_map/dot_general | solution.py:102
  8.0 3.7 %collective-permute-start = (f32[1,512,128]{1,2,0:T(8,128)S(1)}, f32[1,512,128]{1,2,0:T(8,128)S(1)}, u32[]{:S(2)}, u32[]{:S(2)}) collective-permute-start(f32[1,512,128]{1,2,0:T(8,128)S(1)} %slice_bitcast_fusion.10), channel_id=1, source_target_pairs={{0,16},{16,32},{32,48},{48,64},{64,80},{80,96},{96,112},{112,128},... | collective-permute-start | bytes 786440 | tf_op jit(solution)/shard_map/ppermute | solution.py:17
  11.7 6.2 %collective-permute-done = f32[1,512,128]{1,2,0:T(8,128)S(1)} collective-permute-done((f32[1,512,128]{1,2,0:T(8,128)S(1)}, f32[1,512,128]{1,2,0:T(8,128)S(1)}, u32[]{:S(2)}, u32[]{:S(2)}) %collective-permute-start) | collective-permute-done | bytes 262176 | tf_op jit(solution)/shard_map/ppermute | solution.py:17
  20.0 2.7 %collective-permute-start.3 = (f32[1,512,128]{1,2,0:T(8,128)S(1)}, f32[1,512,128]{1,2,0:T(8,128)S(1)}, u32[]{:S(2)}, u32[]{:S(2)}) collective-permute-start(f32[1,512,128]{1,2,0:T(8,128)S(1)} %get-tuple-element.56), channel_id=1, source_target_pairs={{1,0},{2,1},{3,2},{4,3},{5,4},{6,5},{7,6},{8,7},{9,8},{10,9},{11,1... | collective-permute-start | bytes 786440 | tf_op jit(solution)/shard_map/ppermute | solution.py:20
  24.7 6.3 %collective-permute-done.1 = f32[1,512,128]{1,2,0:T(8,128)S(1)} collective-permute-done((f32[1,512,128]{1,2,0:T(8,128)S(1)}, f32[1,512,128]{1,2,0:T(8,128)S(1)}, u32[]{:S(2)}, u32[]{:S(2)}) %collective-permute-start.1) | collective-permute-done | bytes 262176 | tf_op jit(solution)/shard_map/ppermute | solution.py:20
  34.2 23.2 %all_to_all.30 = bf16[16,64,128]{2,1,0:T(8,128)(2,1)S(1)} all-to-all(bf16[16,64,128]{2,1,0:T(8,128)(2,1)S(1)} %broadcast_in_dim.9), channel_id=1, replica_groups=mesh['sx'=16,'sy'=16] {'sx'}, dimensions={0} | all-to-all | bytes 524288 | tf_op jit(solution)/shard_map/all_to_all | solution.py:27
  61.0 14.9 %all_to_all.31 = f32[16,64,128]{2,1,0:T(8,128)} all-to-all(f32[16,64,128]{2,1,0:T(8,128)} %bitcast.263), channel_id=1, replica_groups=mesh['sx'=16,'sy'=16] {'sy'}, dimensions={0} | all-to-all | bytes 1048576 | tf_op jit(solution)/shard_map/all_to_all | solution.py:50
  80.4 6.0 %collective-permute-start.7 = (bf16[1,512,128]{1,2,0:T(8,128)(2,1)S(1)}, bf16[1,512,128]{1,2,0:T(8,128)(2,1)S(1)}, u32[]{:S(2)}, u32[]{:S(2)}) collective-permute-start(bf16[1,512,128]{1,2,0:T(8,128)(2,1)S(1)} %get-tuple-element.52), channel_id=1, source_target_pairs={{1,0},{2,1},{3,2},{4,3},{5,4},{6,5},{7,6},{8,7},{9,8},{10,9},{11,1... | collective-permute-start | bytes 393224 | tf_op jit(solution)/shard_map/ppermute | solution.py:20
  86.4 3.5 %collective-permute-start.4 = (bf16[1,512,128]{1,2,0:T(8,128)(2,1)S(1)}, bf16[1,512,128]{1,2,0:T(8,128)(2,1)S(1)}, u32[]{:S(2)}, u32[]{:S(2)}) collective-permute-start(bf16[1,512,128]{1,2,0:T(8,128)(2,1)S(1)} %get-tuple-element.50), channel_id=1, source_target_pairs={{0,16},{16,32},{32,48},{48,64},{64,80},{80,96},{96,112},{112,128},... | collective-permute-start | bytes 393224 | tf_op jit(solution)/shard_map/ppermute | solution.py:17
  94.4 3.2 %collective-permute-done.5 = bf16[1,512,128]{1,2,0:T(8,128)(2,1)S(1)} collective-permute-done((bf16[1,512,128]{1,2,0:T(8,128)(2,1)S(1)}, bf16[1,512,128]{1,2,0:T(8,128)(2,1)S(1)}, u32[]{:S(2)}, u32[]{:S(2)}) %collective-permute-start.5) | collective-permute-done | bytes 131104 | tf_op jit(solution)/shard_map/ppermute | solution.py:20
  97.7 6.7 %fusion.18 = f32[2048,128]{0,1:T(8,128)S(1)} fusion(bf16[1,1,2048,2048]{3,2,1,0:T(8,128)(2,1)} %param.4, f32[1,1,2048,128]{2,3,1,0:T(8,128)S(1)} %copy.7, f32[512,128]{0,1:T(8,128)S(1)} %get-tuple-element.16, f32[512,128]{0,1:T(8,128)S(1)} %get-tuple-element.15, f32[512,128]{0,1:T(8,128)S(1)} %get-tuple-element.14, f32[512,128]{0,1:T(8,128)S(1)} %get-tuple-element.13, ...), kind=kOutput, calls=%fused_computation.13 | convolution fusion | flops 1076363264 | bytes 12582912 | tf_op jit(solution)/shard_map/dot_general | solution.py:102
  106.4 9.1 %collective-permute-done.8 = f32[1,512,128]{1,2,0:T(8,128)S(1)} collective-permute-done((f32[1,512,128]{1,2,0:T(8,128)S(1)}, f32[1,512,128]{1,2,0:T(8,128)S(1)}, u32[]{:S(2)}, u32[]{:S(2)}) %collective-permute-start.8) | collective-permute-done | bytes 262176 | tf_op jit(solution)/shard_map/ppermute | solution.py:17
  119.6 2.4 collective-permute-start.10
  122.0 3.0 %collective-permute-done.9 = f32[1,512,128]{1,2,0:T(8,128)S(1)} collective-permute-done((f32[1,512,128]{1,2,0:T(8,128)S(1)}, f32[1,512,128]{1,2,0:T(8,128)S(1)}, u32[]{:S(2)}, u32[]{:S(2)}) %collective-permute-start.9) | collective-permute-done | bytes 262176 | tf_op jit(solution)/shard_map/ppermute | solution.py:20
  125.0 4.7 %collective-permute-done.10 = f32[1,512,128]{1,2,0:T(8,128)S(1)} collective-permute-done((f32[1,512,128]{1,2,0:T(8,128)S(1)}, f32[1,512,128]{1,2,0:T(8,128)S(1)}, u32[]{:S(2)}, u32[]{:S(2)}) %collective-permute-start.10) | collective-permute-done | bytes 262176 | tf_op jit(solution)/shard_map/ppermute | solution.py:17
  130.6 17.3 %all_to_all.32 = bf16[16,64,128]{2,1,0:T(8,128)(2,1)S(1)} all-to-all(bf16[16,64,128]{2,1,0:T(8,128)(2,1)S(1)} %broadcast_in_dim.10), channel_id=1, replica_groups=mesh['sx'=16,'sy'=16] {'sx'}, dimensions={0} | all-to-all | bytes 524288 | tf_op jit(solution)/shard_map/all_to_all | solution.py:27
  151.6 14.2 %all_to_all.33 = f32[16,64,128]{2,1,0:T(8,128)} all-to-all(f32[16,64,128]{2,1,0:T(8,128)} %bitcast.264), channel_id=1, replica_groups=mesh['sx'=16,'sy'=16] {'sy'}, dimensions={0} | all-to-all | bytes 1048576 | tf_op jit(solution)/shard_map/all_to_all | solution.py:50
  170.2 6.0 %collective-permute-start.15 = (bf16[1,512,128]{1,2,0:T(8,128)(2,1)S(1)}, bf16[1,512,128]{1,2,0:T(8,128)(2,1)S(1)}, u32[]{:S(2)}, u32[]{:S(2)}) collective-permute-start(bf16[1,512,128]{1,2,0:T(8,128)(2,1)S(1)} %get-tuple-element.41), channel_id=1, source_target_pairs={{1,0},{2,1},{3,2},{4,3},{5,4},{6,5},{7,6},{8,7},{9,8},{10,9},{11,1... | collective-permute-start | bytes 393224 | tf_op jit(solution)/shard_map/ppermute | solution.py:20
  176.2 3.5 %collective-permute-start.12 = (bf16[1,512,128]{1,2,0:T(8,128)(2,1)S(1)}, bf16[1,512,128]{1,2,0:T(8,128)(2,1)S(1)}, u32[]{:S(2)}, u32[]{:S(2)}) collective-permute-start(bf16[1,512,128]{1,2,0:T(8,128)(2,1)S(1)} %get-tuple-element.39), channel_id=1, source_target_pairs={{0,16},{16,32},{32,48},{48,64},{64,80},{80,96},{96,112},{112,128},... | collective-permute-start | bytes 393224 | tf_op jit(solution)/shard_map/ppermute | solution.py:17
  184.3 3.2 %collective-permute-done.13 = bf16[1,512,128]{1,2,0:T(8,128)(2,1)S(1)} collective-permute-done((bf16[1,512,128]{1,2,0:T(8,128)(2,1)S(1)}, bf16[1,512,128]{1,2,0:T(8,128)(2,1)S(1)}, u32[]{:S(2)}, u32[]{:S(2)}) %collective-permute-start.13) | collective-permute-done | bytes 131104 | tf_op jit(solution)/shard_map/ppermute | solution.py:20
  187.5 7.4 %fusion.15 = f32[2048,128]{0,1:T(8,128)S(1)} fusion(bf16[1,1,2048,2048]{3,2,1,0:T(8,128)(2,1)} %param.4, f32[1,1,2048,128]{2,3,1,0:T(8,128)S(1)} %copy.7, f32[512,128]{0,1:T(8,128)S(1)} %get-tuple-element.12, f32[512,128]{0,1:T(8,128)S(1)} %get-tuple-element.11, f32[512,128]{0,1:T(8,128)S(1)} %get-tuple-element.10, f32[512,128]{0,1:T(8,128)S(1)} %get-tuple-element.9, ...), kind=kOutput, calls=%fused_computation.12 | convolution fusion | flops 1078722560 | bytes 14680064 | tf_op jit(solution)/shard_map/dot_general | solution.py:102
  197.0 4.1 %collective-permute-start.17 = (f32[1,512,128]{1,2,0:T(8,128)S(1)}, f32[1,512,128]{1,2,0:T(8,128)S(1)}, u32[]{:S(2)}, u32[]{:S(2)}) collective-permute-start(f32[1,512,128]{1,2,0:T(8,128)S(1)} %get-tuple-element.36), channel_id=1, source_target_pairs={{16,0},{32,16},{48,32},{64,48},{80,64},{96,80},{112,96},{128,112},... | collective-permute-start | bytes 786440 | tf_op jit(solution)/shard_map/ppermute | solution.py:20
  203.1 2.4 collective-permute-start.18
  205.5 4.4 %collective-permute-done.16 = f32[1,512,128]{1,2,0:T(8,128)S(1)} collective-permute-done((f32[1,512,128]{1,2,0:T(8,128)S(1)}, f32[1,512,128]{1,2,0:T(8,128)S(1)}, u32[]{:S(2)}, u32[]{:S(2)}) %collective-permute-start.16) | collective-permute-done | bytes 262176 | tf_op jit(solution)/shard_map/ppermute | solution.py:17
  209.9 3.3 %collective-permute-done.18 = f32[1,512,128]{1,2,0:T(8,128)S(1)} collective-permute-done((f32[1,512,128]{1,2,0:T(8,128)S(1)}, f32[1,512,128]{1,2,0:T(8,128)S(1)}, u32[]{:S(2)}, u32[]{:S(2)}) %collective-permute-start.18) | collective-permute-done | bytes 262176 | tf_op jit(solution)/shard_map/ppermute | solution.py:17
  214.6 16.5 %all_to_all.34 = bf16[16,64,128]{2,1,0:T(8,128)(2,1)S(1)} all-to-all(bf16[16,64,128]{2,1,0:T(8,128)(2,1)S(1)} %broadcast_in_dim.11), channel_id=1, replica_groups=mesh['sx'=16,'sy'=16] {'sx'}, dimensions={0} | all-to-all | bytes 524288 | tf_op jit(solution)/shard_map/all_to_all | solution.py:27
  233.0 16.8 %all_to_all.35 = f32[16,64,128]{2,1,0:T(8,128)S(1)} all-to-all(f32[16,64,128]{2,1,0:T(8,128)} %bitcast.265), channel_id=1, replica_groups=mesh['sx'=16,'sy'=16] {'sy'}, dimensions={0} | all-to-all | bytes 1048576 | tf_op jit(solution)/shard_map/all_to_all | solution.py:50
  252.2 6.0 %collective-permute-start.23 = (bf16[1,512,128]{1,2,0:T(8,128)(2,1)S(1)}, bf16[1,512,128]{1,2,0:T(8,128)(2,1)S(1)}, u32[]{:S(2)}, u32[]{:S(2)}) collective-permute-start(bf16[1,512,128]{1,2,0:T(8,128)(2,1)S(1)} %get-tuple-element.27), channel_id=1, source_target_pairs={{1,0},{2,1},{3,2},{4,3},{5,4},{6,5},{7,6},{8,7},{9,8},{10,9},{11,1... | collective-permute-start | bytes 393224 | tf_op jit(solution)/shard_map/ppermute | solution.py:20
  258.2 3.0 %collective-permute-start.20 = (bf16[1,512,128]{1,2,0:T(8,128)(2,1)S(1)}, bf16[1,512,128]{1,2,0:T(8,128)(2,1)S(1)}, u32[]{:S(2)}, u32[]{:S(2)}) collective-permute-start(bf16[1,512,128]{1,2,0:T(8,128)(2,1)S(1)} %get-tuple-element.25), channel_id=1, source_target_pairs={{0,16},{16,32},{32,48},{48,64},{64,80},{80,96},{96,112},{112,128},... | collective-permute-start | bytes 393224 | tf_op jit(solution)/shard_map/ppermute | solution.py:17
  261.2 2.8 %collective-permute-start.21 = (bf16[1,512,128]{1,2,0:T(8,128)(2,1)S(1)}, bf16[1,512,128]{1,2,0:T(8,128)(2,1)S(1)}, u32[]{:S(2)}, u32[]{:S(2)}) collective-permute-start(bf16[1,512,128]{1,2,0:T(8,128)(2,1)S(1)} %get-tuple-element.28), channel_id=1, source_target_pairs={{16,0},{32,16},{48,32},{64,48},{80,64},{96,80},{112,96},{128,112},... | collective-permute-start | bytes 393224 | tf_op jit(solution)/shard_map/ppermute | solution.py:20
  265.8 3.2 %collective-permute-done.21 = bf16[1,512,128]{1,2,0:T(8,128)(2,1)S(1)} collective-permute-done((bf16[1,512,128]{1,2,0:T(8,128)(2,1)S(1)}, bf16[1,512,128]{1,2,0:T(8,128)(2,1)S(1)}, u32[]{:S(2)}, u32[]{:S(2)}) %collective-permute-start.21) | collective-permute-done | bytes 131104 | tf_op jit(solution)/shard_map/ppermute | solution.py:20
  269.1 2.7 fusion.44
  (103 shorter events, 53.5 us)
Async XLA Ops:
  0.0 57.4 %copy-start = (bf16[1,1,1024,1024]{3,2,1,0:T(8,128)(2,1)S(1)}, bf16[1,1,1024,1024]{3,2,1,0:T(8,128)(2,1)}, u32[]{:S(2)}) copy-start(bf16[1,1,1024,1024]{3,2,1,0:T(8,128)(2,1)} %param.7) | copy-start | bytes 6291460
  1.7 32.1 %copy-start.8 = (bf16[1,1,64,2048]{3,2,1,0:T(8,128)(2,1)S(1)}, bf16[1,1,64,2048]{3,2,1,0:T(8,128)(2,1)}, u32[]{:S(2)}) copy-start(bf16[1,1,64,2048]{3,2,1,0:T(8,128)(2,1)} %param.6) | copy-start | bytes 786436
  8.0 9.9 %collective-permute-start = (f32[1,512,128]{1,2,0:T(8,128)S(1)}, f32[1,512,128]{1,2,0:T(8,128)S(1)}, u32[]{:S(2)}, u32[]{:S(2)}) collective-permute-start(f32[1,512,128]{1,2,0:T(8,128)S(1)} %slice_bitcast_fusion.10), channel_id=1, source_target_pairs={{0,16},{16,32},{32,48},{48,64},{64,80},{80,96},{96,112},{112,128},... | collective-permute-start | bytes 786440 | tf_op jit(solution)/shard_map/ppermute | solution.py:17
  18.1 13.0 %collective-permute-start.1 = (f32[1,512,128]{1,2,0:T(8,128)S(1)}, f32[1,512,128]{1,2,0:T(8,128)S(1)}, u32[]{:S(2)}, u32[]{:S(2)}) collective-permute-start(f32[1,512,128]{1,2,0:T(8,128)S(1)} %get-tuple-element.55), channel_id=1, source_target_pairs={{16,0},{32,16},{48,32},{64,48},{80,64},{96,80},{112,96},{128,112},... | collective-permute-start | bytes 786440 | tf_op jit(solution)/shard_map/ppermute | solution.py:20
  20.0 11.0 %collective-permute-start.3 = (f32[1,512,128]{1,2,0:T(8,128)S(1)}, f32[1,512,128]{1,2,0:T(8,128)S(1)}, u32[]{:S(2)}, u32[]{:S(2)}) collective-permute-start(f32[1,512,128]{1,2,0:T(8,128)S(1)} %get-tuple-element.56), channel_id=1, source_target_pairs={{1,0},{2,1},{3,2},{4,3},{5,4},{6,5},{7,6},{8,7},{9,8},{10,9},{11,1... | collective-permute-start | bytes 786440 | tf_op jit(solution)/shard_map/ppermute | solution.py:20
  22.8 10.2 %collective-permute-start.2 = (f32[1,512,128]{1,2,0:T(8,128)S(1)}, f32[1,512,128]{1,2,0:T(8,128)S(1)}, u32[]{:S(2)}, u32[]{:S(2)}) collective-permute-start(f32[1,512,128]{1,2,0:T(8,128)S(1)} %get-tuple-element.57), channel_id=1, source_target_pairs={{0,1},{1,2},{2,3},{3,4},{4,5},{5,6},{6,7},{7,8},{8,9},{9,10},{10,1... | collective-permute-start | bytes 786440 | tf_op jit(solution)/shard_map/ppermute | solution.py:17
  78.4 13.8 %collective-permute-start.6 = (bf16[1,512,128]{1,2,0:T(8,128)(2,1)S(1)}, bf16[1,512,128]{1,2,0:T(8,128)(2,1)S(1)}, u32[]{:S(2)}, u32[]{:S(2)}) collective-permute-start(bf16[1,512,128]{1,2,0:T(8,128)(2,1)S(1)} %get-tuple-element.51), channel_id=1, source_target_pairs={{0,1},{1,2},{2,3},{3,4},{4,5},{5,6},{6,7},{7,8},{8,9},{9,10},{10,1... | collective-permute-start | bytes 393224 | tf_op jit(solution)/shard_map/ppermute | solution.py:17
  80.4 11.9 %collective-permute-start.7 = (bf16[1,512,128]{1,2,0:T(8,128)(2,1)S(1)}, bf16[1,512,128]{1,2,0:T(8,128)(2,1)S(1)}, u32[]{:S(2)}, u32[]{:S(2)}) collective-permute-start(bf16[1,512,128]{1,2,0:T(8,128)(2,1)S(1)} %get-tuple-element.52), channel_id=1, source_target_pairs={{1,0},{2,1},{3,2},{4,3},{5,4},{6,5},{7,6},{8,7},{9,8},{10,9},{11,1... | collective-permute-start | bytes 393224 | tf_op jit(solution)/shard_map/ppermute | solution.py:20
  86.4 8.0 %collective-permute-start.4 = (bf16[1,512,128]{1,2,0:T(8,128)(2,1)S(1)}, bf16[1,512,128]{1,2,0:T(8,128)(2,1)S(1)}, u32[]{:S(2)}, u32[]{:S(2)}) collective-permute-start(bf16[1,512,128]{1,2,0:T(8,128)(2,1)S(1)} %get-tuple-element.50), channel_id=1, source_target_pairs={{0,16},{16,32},{32,48},{48,64},{64,80},{80,96},{96,112},{112,128},... | collective-permute-start | bytes 393224 | tf_op jit(solution)/shard_map/ppermute | solution.py:17
  89.9 7.8 %collective-permute-start.5 = (bf16[1,512,128]{1,2,0:T(8,128)(2,1)S(1)}, bf16[1,512,128]{1,2,0:T(8,128)(2,1)S(1)}, u32[]{:S(2)}, u32[]{:S(2)}) collective-permute-start(bf16[1,512,128]{1,2,0:T(8,128)(2,1)S(1)} %get-tuple-element.53), channel_id=1, source_target_pairs={{16,0},{32,16},{48,32},{64,48},{80,64},{96,80},{112,96},{128,112},... | collective-permute-start | bytes 393224 | tf_op jit(solution)/shard_map/ppermute | solution.py:20
  97.7 32.1 %copy-start.5 = (f32[512,128]{0,1:T(8,128)}, f32[512,128]{0,1:T(8,128)S(1)}, u32[]{:S(2)}) copy-start(f32[512,128]{0,1:T(8,128)S(1)} %get-tuple-element.13) | copy-start | bytes 786436
  97.7 32.1 %copy-start.6 = (f32[512,128]{0,1:T(8,128)}, f32[512,128]{0,1:T(8,128)S(1)}, u32[]{:S(2)}) copy-start(f32[512,128]{0,1:T(8,128)S(1)} %get-tuple-element.14) | copy-start | bytes 786436
  97.7 32.2 %copy-start.9 = (bf16[1,1,64,2048]{3,2,1,0:T(8,128)(2,1)S(1)}, bf16[1,1,64,2048]{3,2,1,0:T(8,128)(2,1)}, u32[]{:S(2)}) copy-start(bf16[1,1,64,2048]{3,2,1,0:T(8,128)(2,1)} %param.6) | copy-start | bytes 786436
  104.5 11.1 %collective-permute-start.8 = (f32[1,512,128]{1,2,0:T(8,128)S(1)}, f32[1,512,128]{1,2,0:T(8,128)S(1)}, u32[]{:S(2)}, u32[]{:S(2)}) collective-permute-start(f32[1,512,128]{1,2,0:T(8,128)S(1)} %slice_bitcast_fusion.6), channel_id=1, source_target_pairs={{0,16},{16,32},{32,48},{48,64},{64,80},{80,96},{96,112},{112,128},... | collective-permute-start | bytes 786440 | tf_op jit(solution)/shard_map/ppermute | solution.py:17
  115.7 32.2 %copy-start.19 = (f32[512,128]{0,1:T(8,128)}, f32[512,128]{0,1:T(8,128)S(1)}, u32[]{:S(2)}) copy-start(f32[512,128]{0,1:T(8,128)S(1)} %get-tuple-element.43) | copy-start | bytes 786436
  115.7 9.3 %collective-permute-start.9 = (f32[1,512,128]{1,2,0:T(8,128)S(1)}, f32[1,512,128]{1,2,0:T(8,128)S(1)}, u32[]{:S(2)}, u32[]{:S(2)}) collective-permute-start(f32[1,512,128]{1,2,0:T(8,128)S(1)} %get-tuple-element.44), channel_id=1, source_target_pairs={{16,0},{32,16},{48,32},{64,48},{80,64},{96,80},{112,96},{128,112},... | collective-permute-start | bytes 786440 | tf_op jit(solution)/shard_map/ppermute | solution.py:20
  117.7 7.3 %collective-permute-start.11 = (f32[1,512,128]{1,2,0:T(8,128)S(1)}, f32[1,512,128]{1,2,0:T(8,128)S(1)}, u32[]{:S(2)}, u32[]{:S(2)}) collective-permute-start(f32[1,512,128]{1,2,0:T(8,128)S(1)} %get-tuple-element.45), channel_id=1, source_target_pairs={{1,0},{2,1},{3,2},{4,3},{5,4},{6,5},{7,6},{8,7},{9,8},{10,9},{11,1... | collective-permute-start | bytes 786440 | tf_op jit(solution)/shard_map/ppermute | solution.py:20
  119.6 10.1 %collective-permute-start.10 = (f32[1,512,128]{1,2,0:T(8,128)S(1)}, f32[1,512,128]{1,2,0:T(8,128)S(1)}, u32[]{:S(2)}, u32[]{:S(2)}) collective-permute-start(f32[1,512,128]{1,2,0:T(8,128)S(1)} %get-tuple-element.46), channel_id=1, source_target_pairs={{0,1},{1,2},{2,3},{3,4},{4,5},{5,6},{6,7},{7,8},{8,9},{9,10},{10,1... | collective-permute-start | bytes 786440 | tf_op jit(solution)/shard_map/ppermute | solution.py:17
  168.2 13.8 %collective-permute-start.14 = (bf16[1,512,128]{1,2,0:T(8,128)(2,1)S(1)}, bf16[1,512,128]{1,2,0:T(8,128)(2,1)S(1)}, u32[]{:S(2)}, u32[]{:S(2)}) collective-permute-start(bf16[1,512,128]{1,2,0:T(8,128)(2,1)S(1)} %get-tuple-element.40), channel_id=1, source_target_pairs={{0,1},{1,2},{2,3},{3,4},{4,5},{5,6},{6,7},{7,8},{8,9},{9,10},{10,1... | collective-permute-start | bytes 393224 | tf_op jit(solution)/shard_map/ppermute | solution.py:17
  170.2 11.9 %collective-permute-start.15 = (bf16[1,512,128]{1,2,0:T(8,128)(2,1)S(1)}, bf16[1,512,128]{1,2,0:T(8,128)(2,1)S(1)}, u32[]{:S(2)}, u32[]{:S(2)}) collective-permute-start(bf16[1,512,128]{1,2,0:T(8,128)(2,1)S(1)} %get-tuple-element.41), channel_id=1, source_target_pairs={{1,0},{2,1},{3,2},{4,3},{5,4},{6,5},{7,6},{8,7},{9,8},{10,9},{11,1... | collective-permute-start | bytes 393224 | tf_op jit(solution)/shard_map/ppermute | solution.py:20
  176.2 8.0 %collective-permute-start.12 = (bf16[1,512,128]{1,2,0:T(8,128)(2,1)S(1)}, bf16[1,512,128]{1,2,0:T(8,128)(2,1)S(1)}, u32[]{:S(2)}, u32[]{:S(2)}) collective-permute-start(bf16[1,512,128]{1,2,0:T(8,128)(2,1)S(1)} %get-tuple-element.39), channel_id=1, source_target_pairs={{0,16},{16,32},{32,48},{48,64},{64,80},{80,96},{96,112},{112,128},... | collective-permute-start | bytes 393224 | tf_op jit(solution)/shard_map/ppermute | solution.py:17
  179.7 7.8 %collective-permute-start.13 = (bf16[1,512,128]{1,2,0:T(8,128)(2,1)S(1)}, bf16[1,512,128]{1,2,0:T(8,128)(2,1)S(1)}, u32[]{:S(2)}, u32[]{:S(2)}) collective-permute-start(bf16[1,512,128]{1,2,0:T(8,128)(2,1)S(1)} %get-tuple-element.42), channel_id=1, source_target_pairs={{16,0},{32,16},{48,32},{64,48},{80,64},{96,80},{112,96},{128,112},... | collective-permute-start | bytes 393224 | tf_op jit(solution)/shard_map/ppermute | solution.py:20
  187.5 26.8 %copy-start.10 = (bf16[1,1,64,2048]{3,2,1,0:T(8,128)(2,1)S(1)}, bf16[1,1,64,2048]{3,2,1,0:T(8,128)(2,1)}, u32[]{:S(2)}) copy-start(bf16[1,1,64,2048]{3,2,1,0:T(8,128)(2,1)} %param.6) | copy-start | bytes 786436
  195.0 54.8 %copy-start.11 = (bf16[1,1,64,2048]{3,2,1,0:T(8,128)(2,1)S(1)}, bf16[1,1,64,2048]{3,2,1,0:T(8,128)(2,1)}, u32[]{:S(2)}) copy-start(bf16[1,1,64,2048]{3,2,1,0:T(8,128)(2,1)} %param.6) | copy-start | bytes 786436
  195.1 14.8 %collective-permute-start.16 = (f32[1,512,128]{1,2,0:T(8,128)S(1)}, f32[1,512,128]{1,2,0:T(8,128)S(1)}, u32[]{:S(2)}, u32[]{:S(2)}) collective-permute-start(f32[1,512,128]{1,2,0:T(8,128)S(1)} %get-tuple-element.35), channel_id=1, source_target_pairs={{0,16},{16,32},{32,48},{48,64},{64,80},{80,96},{96,112},{112,128},... | collective-permute-start | bytes 786440 | tf_op jit(solution)/shard_map/ppermute | solution.py:17
  197.0 12.9 %collective-permute-start.17 = (f32[1,512,128]{1,2,0:T(8,128)S(1)}, f32[1,512,128]{1,2,0:T(8,128)S(1)}, u32[]{:S(2)}, u32[]{:S(2)}) collective-permute-start(f32[1,512,128]{1,2,0:T(8,128)S(1)} %get-tuple-element.36), channel_id=1, source_target_pairs={{16,0},{32,16},{48,32},{64,48},{80,64},{96,80},{112,96},{128,112},... | collective-permute-start | bytes 786440 | tf_op jit(solution)/shard_map/ppermute | solution.py:20
  201.1 8.8 %collective-permute-start.19 = (f32[1,512,128]{1,2,0:T(8,128)S(1)}, f32[1,512,128]{1,2,0:T(8,128)S(1)}, u32[]{:S(2)}, u32[]{:S(2)}) collective-permute-start(f32[1,512,128]{1,2,0:T(8,128)S(1)} %get-tuple-element.37), channel_id=1, source_target_pairs={{1,0},{2,1},{3,2},{4,3},{5,4},{6,5},{7,6},{8,7},{9,8},{10,9},{11,1... | collective-permute-start | bytes 786440 | tf_op jit(solution)/shard_map/ppermute | solution.py:20
  203.1 10.1 %collective-permute-start.18 = (f32[1,512,128]{1,2,0:T(8,128)S(1)}, f32[1,512,128]{1,2,0:T(8,128)S(1)}, u32[]{:S(2)}, u32[]{:S(2)}) collective-permute-start(f32[1,512,128]{1,2,0:T(8,128)S(1)} %get-tuple-element.38), channel_id=1, source_target_pairs={{0,1},{1,2},{2,3},{3,4},{4,5},{5,6},{6,7},{7,8},{8,9},{9,10},{10,1... | collective-permute-start | bytes 786440 | tf_op jit(solution)/shard_map/ppermute | solution.py:17
  250.2 13.8 %collective-permute-start.22 = (bf16[1,512,128]{1,2,0:T(8,128)(2,1)S(1)}, bf16[1,512,128]{1,2,0:T(8,128)(2,1)S(1)}, u32[]{:S(2)}, u32[]{:S(2)}) collective-permute-start(bf16[1,512,128]{1,2,0:T(8,128)(2,1)S(1)} %get-tuple-element.26), channel_id=1, source_target_pairs={{0,1},{1,2},{2,3},{3,4},{4,5},{5,6},{6,7},{7,8},{8,9},{9,10},{10,1... | collective-permute-start | bytes 393224 | tf_op jit(solution)/shard_map/ppermute | solution.py:17
  252.2 11.9 %collective-permute-start.23 = (bf16[1,512,128]{1,2,0:T(8,128)(2,1)S(1)}, bf16[1,512,128]{1,2,0:T(8,128)(2,1)S(1)}, u32[]{:S(2)}, u32[]{:S(2)}) collective-permute-start(bf16[1,512,128]{1,2,0:T(8,128)(2,1)S(1)} %get-tuple-element.27), channel_id=1, source_target_pairs={{1,0},{2,1},{3,2},{4,3},{5,4},{6,5},{7,6},{8,7},{9,8},{10,9},{11,1... | collective-permute-start | bytes 393224 | tf_op jit(solution)/shard_map/ppermute | solution.py:20
  258.2 7.6 %collective-permute-start.20 = (bf16[1,512,128]{1,2,0:T(8,128)(2,1)S(1)}, bf16[1,512,128]{1,2,0:T(8,128)(2,1)S(1)}, u32[]{:S(2)}, u32[]{:S(2)}) collective-permute-start(bf16[1,512,128]{1,2,0:T(8,128)(2,1)S(1)} %get-tuple-element.25), channel_id=1, source_target_pairs={{0,16},{16,32},{32,48},{48,64},{64,80},{80,96},{96,112},{112,128},... | collective-permute-start | bytes 393224 | tf_op jit(solution)/shard_map/ppermute | solution.py:17
  261.2 7.8 %collective-permute-start.21 = (bf16[1,512,128]{1,2,0:T(8,128)(2,1)S(1)}, bf16[1,512,128]{1,2,0:T(8,128)(2,1)S(1)}, u32[]{:S(2)}, u32[]{:S(2)}) collective-permute-start(bf16[1,512,128]{1,2,0:T(8,128)(2,1)S(1)} %get-tuple-element.28), channel_id=1, source_target_pairs={{16,0},{32,16},{48,32},{64,48},{80,64},{96,80},{112,96},{128,112},... | collective-permute-start | bytes 393224 | tf_op jit(solution)/shard_map/ppermute | solution.py:20
  (12 other events, 124.7 us)
where the time goes:
time: 275 us; the launch traced here: 273 us
  blocking collectives  103 us (37%)
  starting transfers between devices  70.3 us (26%)
  waiting for transfers between devices  54.3 us (20%)
  matrix products  28.3 us (10%)
  local copies, waits for them, and re-layouts  9.69 us (4%)
  other arithmetic  6.93 us (3%)
    all_to_all x3, blocking collectives, copy_for_each(): lax.all_to_all(jnp.broadcast_to(array[None], (devices, *array.shape)), ax...  57 us
    all_to_all x3, blocking collectives, sent_and_summed(): lax.all_to_all(cut_along(array, dim, devices), axis, 0, 0, tiled=True)  45.9 us
    ppermute x12, starting transfers between devices, with_halo(): lax.ppermute(lax.slice_in_dim(block, 0, width, axis=dim), axis, backward)  40.2 us
    ppermute x12, waiting for transfers between devices, with_halo(): lax.ppermute(lax.slice_in_dim(block, block.shape[dim] - width, None, axis...  35.4 us
    ppermute x12, starting transfers between devices, with_halo(): lax.ppermute(lax.slice_in_dim(block, block.shape[dim] - width, None, axis...  30 us
    dot_general x3, matrix products, local(): jnp.dot(operator, multipliers.astype(jnp.bfloat16), preferred_element_typ...  20.4 us
    ppermute x12, waiting for transfers between devices, with_halo(): lax.ppermute(lax.slice_in_dim(block, 0, width, axis=dim), axis, backward)  18.9 us
  transfers between devices with their start and end apart: 24, of which 14 were waited for; matrix products, arithmetic and copies ran while one was open for 0% of the time, Pallas kernels for 0%

commit v1 on v0

v1 whole, which is shorter than its diff:
```python
import jax
import jax.numpy as jnp
from jax import lax
from jax.experimental import pallas as pl
from jax.experimental.pallas import tpu as pltpu
from jax.sharding import PartitionSpec as P

ITERS = 3
DAMPING = 0.5

VMEM = pl.BlockSpec(memory_space=pltpu.VMEM)
SMEM = pl.BlockSpec(memory_space=pltpu.SMEM)
BF16 = jnp.bfloat16
F32 = jnp.float32


def kernel_call(body, outs, scratch=(), flops=0, moved=0, limit=16 << 20):
    return lambda *operands: pl.pallas_call(
        body,
        out_shape=tuple(outs),
        in_specs=[SMEM] + [VMEM] * (len(operands) - 1),
        out_specs=tuple([VMEM] * len(outs)),
        scratch_shapes=list(scratch),
        compiler_params=pltpu.CompilerParams(vmem_limit_bytes=limit),
        cost_estimate=pl.CostEstimate(flops=flops, bytes_accessed=moved, transcendentals=0),
    )(*operands)


def odd_places():
    return jnp.stack([lax.rem(lax.axis_index(axis), 2) for axis in ("sx", "sy")]).astype(jnp.int32)


def face_starts(odd, width):
    starts = []
    for axis, first in enumerate((0, 2)):
        starts.append(pl.multiple_of((first + 1 - odd[axis]) * width, width))
        starts.append(pl.multiple_of((first + odd[axis]) * width, width))
    return starts


def exchange(parts):
    received = []
    for index, part in enumerate(parts):
        axis = ("sx", "sy")[index // 2]
        count = lax.axis_size(axis)
        lower = range(index % 2, count - 1, 2)
        pairs = [(i, i + 1) for i in lower] + [(i + 1, i) for i in lower]
        received.append(lax.ppermute(part, axis, pairs))
    return received


def faces_body(odd, values, *faces):
    width = values.shape[0] // 4
    for start, face in zip(face_starts(odd, width), faces):
        face[...] = values[pl.ds(start, width), :].astype(BF16)


def restrict_body(first, odd, *refs):
    values, basis, *others = refs
    held = None if first else others.pop(0)
    received = others[:4]
    stepped, coarse = others[4:]
    width = values.shape[0] // 4
    total = jnp.zeros(coarse.shape[1:], F32)
    for start, part in zip(face_starts(odd, width), received):
        rows = pl.ds(start, width)
        residual = values[rows, :] - part[...].astype(F32)
        half = DAMPING * residual
        stepped[rows, :] = half if first else held[rows, :] + half
        total += jnp.dot(basis[:, rows], residual.astype(BF16), preferred_element_type=F32)
    coarse[...] = jnp.broadcast_to(total.astype(BF16)[None], coarse.shape)


def tile_body(odd, tile, columns, partial):
    count, rows, loads = partial.shape
    whole = columns[...].reshape(tile.shape[1], loads)
    product = jnp.dot(tile[...], whole, preferred_element_type=F32)
    partial[...] = product.astype(BF16).reshape(count, rows, loads)


def sum_body(odd, parts, total):
    total[...] = jnp.sum(parts[...].astype(F32), axis=0).astype(BF16)


def sum_with_basis_body(odd, parts, basis, *messages):
    total = jnp.sum(parts[...].astype(F32), axis=0).astype(BF16)
    rows, loads = total.shape
    width = basis.shape[1] // 4
    for start, message in zip(face_starts(odd, width), messages):
        message[:rows, :] = total
        for piece in range(width // loads):
            columns = pl.ds(pl.multiple_of(start + piece * loads, loads), loads)
            message[(piece + 1) * rows : (piece + 2) * rows, :] = basis[:, columns]


def corrected(stepped, basis, own, slices, theirs, start, width):
    rows, loads = own.shape
    near = basis[:, pl.ds(start, width)]
    far = jnp.concatenate(
        [slices[(i + 1) * rows : (i + 2) * rows, :] for i in range(width // loads)], axis=1
    )
    weights = jnp.concatenate([near, far], axis=0)
    columns = jnp.concatenate([own, -theirs], axis=0)
    back = lax.dot_general(
        weights, columns, (((0,), (0,)), ((), ())), preferred_element_type=F32
    )
    return stepped[pl.ds(start, width), :] - DAMPING * back


def advance_body(odd, stepped, basis, own, operator, loads, *refs):
    slices, theirs = refs[:4], refs[4:8]
    held, values = refs[8:10]
    faces, rounded = refs[10:14], refs[14]
    width = values.shape[0] // 4
    rows = basis.shape[0]
    starts = face_starts(odd, width)
    for start, kept, other in zip(starts, slices, theirs):
        part = corrected(
            stepped, basis, own[:rows, :], kept, other[:rows, :], start, width
        )
        held[pl.ds(start, width), :] = part
        rounded[pl.ds(start, width), :] = part.astype(BF16)
    for start, face in zip(starts, faces):
        block = pl.ds(start, width)
        product = jnp.dot(operator[block, :], rounded[...], preferred_element_type=F32)
        value = loads[block, :] - product
        values[block, :] = value
        face[...] = value.astype(BF16)


def finish_body(odd, stepped, basis, own, *refs):
    slices, theirs, (out,) = refs[:4], refs[4:8], refs[8:]
    width = out.shape[0] // 4
    rows = basis.shape[0]
    for start, kept, other in zip(face_starts(odd, width), slices, theirs):
        out[pl.ds(start, width), :] = corrected(
            stepped, basis, own[:rows, :], kept, other[:rows, :], start, width
        )


def local(dual_ops, loads, kernel_basis, coarse_inverse):
    operator, right, basis, tile = dual_ops[0, 0], loads[0, 0], kernel_basis[0, 0], coarse_inverse[0, 0]
    size, columns = right.shape
    width = size // 4
    rows = basis.shape[0]
    whole = jax.ShapeDtypeStruct(right.shape, F32)
    face = jax.ShapeDtypeStruct((width, columns), BF16)
    blocks_x = jax.ShapeDtypeStruct((lax.axis_size("sx"), rows, columns), BF16)
    blocks_y = jax.ShapeDtypeStruct((lax.axis_size("sy"), rows, columns), BF16)
    coarse = jax.ShapeDtypeStruct((rows, columns), BF16)
    message = jax.ShapeDtypeStruct((rows + width * rows // columns, columns), BF16)

    odd = odd_places()
    values, held = right, None
    faces = kernel_call(faces_body, [face] * 4, moved=3 << 19)(odd, right)
    for step in range(ITERS):
        received = exchange(faces)
        first = step == 0
        stepped, sent = kernel_call(
            lambda *refs, first=first: restrict_body(first, *refs),
            [whole, blocks_x],
            flops=2 * rows * size * columns,
            moved=4 << 20,
        )(odd, values, basis, *([] if first else [held]), *received)
        gathered = lax.all_to_all(sent, "sx", 0, 0, tiled=True)
        (partial,) = kernel_call(
            tile_body, [blocks_y], flops=2 * tile.size * columns, moved=3 << 20
        )(odd, tile, gathered)
        parts = lax.all_to_all(partial, "sy", 0, 0, tiled=True)
        if first:
            messages = kernel_call(sum_with_basis_body, [message] * 4, moved=1 << 20)(odd, parts, basis)
            own = messages[0]
            theirs = exchange(messages)
            slices = theirs
        else:
            (own,) = kernel_call(sum_body, [coarse], moved=1 << 18)(odd, parts)
            theirs = exchange([own] * 4)
        if step < ITERS - 1:
            held, values, *faces = kernel_call(
                advance_body,
                [whole, whole] + [face] * 4,
                [pltpu.VMEM((size, columns), BF16)],
                flops=2 * operator.size * columns,
                moved=16 << 20,
            )(odd, stepped, basis, own, operator, right, *slices, *theirs)
        else:
            (out,) = kernel_call(finish_body, [whole], moved=2 << 20)(
                odd, stepped, basis, own, *slices, *theirs
            )
    return out[None, None]


def solution(mesh):
    placed = P("sx", "sy", None, None)
    return jax.shard_map(
        local, mesh=mesh, in_specs=(placed,) * 4, out_specs=placed, check_vma=False
    )
```

time: 275 us -> 198 us (0.72)
  waiting for transfers between devices: 54.3 us -> 25.6 us
  matrix products: 28.3 us -> 0 us
  starting transfers between devices: 70.3 us -> 51 us
  Pallas kernels: 0 us -> 17.1 us
  blocking collectives: 103 us -> 92.4 us
  other arithmetic: 6.93 us -> 0.07 us
    ppermute x24, waiting for transfers between devices: 54.3 us -> 25.6 us  [exchange(): received.append(lax.ppermute(part, axis, pairs))]
    dot_general x12 -> x0, matrix products: 28.3 us -> none  [the longest x3 20.4 us: local(): jnp.dot(operator, multipliers.astype(jnp.bfloat16), preferred_element_typ...]
    ppermute x24, starting transfers between devices: 70.3 us -> 51 us  [exchange(): received.append(lax.ppermute(part, axis, pairs))]
    pallas_call x0 -> x13, Pallas kernels: none -> 17.1 us  [kernel_call(): pl.pallas_call(body, out_shape=tuple(outs), in_specs=[SMEM] + [VMEM] * (l...]
    all_to_all x6, blocking collectives: 103 us -> 92.4 us  [the longest x3 54.3 us: local(): gathered = lax.all_to_all(sent, 'sx', 0, 0, tiled=True)]
    unnamed x41 -> x22, local copies, waits for them, and re-layouts: 2.85 us -> 10.3 us
    dot_general x3 -> x0, local copies, waits for them, and re-layouts: 5.08 us -> none  [local(): jnp.dot(tile, collect(coarse_in, 'sx', 0), preferred_element_type=jnp.flo...]
  transfers between devices with their start and end apart: 24 -> 24, of which waited for: 14 -> 9; matrix products, arithmetic and copies ran while one was open for 0% -> 0% of each run, Pallas kernels for 0% -> 0%
where the time goes in v1:
time: 198 us; the launch traced here: 197 us
  blocking collectives  92.4 us (47%)
  starting transfers between devices  51 us (26%)
  waiting for transfers between devices  25.6 us (13%)
  Pallas kernels  17.1 us (9%)
  local copies, waits for them, and re-layouts  10.3 us (5%)
    all_to_all x3, blocking collectives, local(): gathered = lax.all_to_all(sent, 'sx', 0, 0, tiled=True)  54.3 us
    ppermute x24, starting transfers between devices, exchange(): received.append(lax.ppermute(part, axis, pairs))  51 us
    all_to_all x3, blocking collectives, local(): parts = lax.all_to_all(partial, 'sy', 0, 0, tiled=True)  38.1 us
    ppermute x24, waiting for transfers between devices, exchange(): received.append(lax.ppermute(part, axis, pairs))  25.6 us
    pallas_call x13, Pallas kernels, kernel_call(): pl.pallas_call(body, out_shape=tuple(outs), in_specs=[SMEM] + [VMEM] * (l...  17.1 us
    unnamed x22, local copies, waits for them, and re-layouts  10.3 us
  transfers between devices with their start and end apart: 24, of which 9 were waited for; matrix products, arithmetic and copies ran while one was open for 0% of the time, Pallas kernels for 0%

profile of v1, /device:TPU:10, one launch (start us, length us, event | category | flops | bytes accessed | tf_op | source)
XLA Modules:
  0.0 196.8 jit_solution(9277671046518808742)
XLA Ops:
  2.4 4.8 %collective-permute-start.1 = (bf16[512,128]{1,0:T(8,128)(2,1)S(1)}, bf16[512,128]{1,0:T(8,128)(2,1)S(1)}, u32[]{:S(2)}, u32[]{:S(2)}) collective-permute-start(bf16[512,128]{1,0:T(8,128)(2,1)S(1)} %get-tuple-element.32), channel_id=1, source_target_pairs={{16,32},{48,64},{80,96},{112,128},{144,160},{176,192},{208,224},{3... | collective-permute-start | bytes 393224 | tf_op jit(solution)/shard_map/ppermute | solution.py:48
  7.4 4.3 %collective-permute-start.3 = (bf16[512,128]{1,0:T(8,128)(2,1)S(1)}, bf16[512,128]{1,0:T(8,128)(2,1)S(1)}, u32[]{:S(2)}, u32[]{:S(2)}) collective-permute-start(bf16[512,128]{1,0:T(8,128)(2,1)S(1)} %get-tuple-element.34), channel_id=1, source_target_pairs={{1,2},{3,4},{5,6},{7,8},{9,10},{11,12},{13,14},{2,1},{4,3},{6,5},{... | collective-permute-start | bytes 393224 | tf_op jit(solution)/shard_map/ppermute | solution.py:48
  11.7 4.5 %collective-permute-done.3.refs_6_ = bf16[512,128]{1,0:T(8,128)(2,1)S(1)} collective-permute-done((bf16[512,128]{1,0:T(8,128)(2,1)S(1)}, bf16[512,128]{1,0:T(8,128)(2,1)S(1)}, u32[]{:S(2)}, u32[]{:S(2)}) %collective-permute-start.3) | collective-permute-done | bytes 131104 | tf_op jit(solution)/shard_map/ppermute | solution.py:48
  18.0 20.7 %all_to_all.30.columns = bf16[16,64,128]{2,1,0:T(8,128)(2,1)S(1)} all-to-all(bf16[16,64,128]{2,1,0:T(8,128)(2,1)S(1)} %get-tuple-element.36), channel_id=1, replica_groups=mesh['sx'=16,'sy'=16] {'sx'}, dimensions={0} | all-to-all | bytes 524288 | tf_op jit(solution)/shard_map/all_to_all | solution.py:165
  38.7 1.6 copy-done.2
  40.3 1.2 shard_map.48
  41.5 12.7 %all_to_all.31.parts = bf16[16,64,128]{2,1,0:T(8,128)(2,1)S(1)} all-to-all(bf16[16,64,128]{2,1,0:T(8,128)(2,1)S(1)} %shard_map.48), channel_id=1, replica_groups=mesh['sx'=16,'sy'=16] {'sy'}, dimensions={0} | all-to-all | bytes 524288 | tf_op jit(solution)/shard_map/all_to_all | solution.py:169
  55.8 3.2 %collective-permute-start.5 = (bf16[320,128]{1,0:T(8,128)(2,1)S(1)}, bf16[320,128]{1,0:T(8,128)(2,1)S(1)}, u32[]{:S(2)}, u32[]{:S(2)}) collective-permute-start(bf16[320,128]{1,0:T(8,128)(2,1)S(1)} %get-tuple-element.38), channel_id=1, source_target_pairs={{16,32},{48,64},{80,96},{112,128},{144,160},{176,192},{208,224},{3... | collective-permute-start | bytes 245768 | tf_op jit(solution)/shard_map/ppermute | solution.py:48
  59.6 3.3 %collective-permute-start.7 = (bf16[320,128]{1,0:T(8,128)(2,1)S(1)}, bf16[320,128]{1,0:T(8,128)(2,1)S(1)}, u32[]{:S(2)}, u32[]{:S(2)}) collective-permute-start(bf16[320,128]{1,0:T(8,128)(2,1)S(1)} %get-tuple-element.40), channel_id=1, source_target_pairs={{1,2},{3,4},{5,6},{7,8},{9,10},{11,12},{13,14},{2,1},{4,3},{6,5},{... | collective-permute-start | bytes 245768 | tf_op jit(solution)/shard_map/ppermute | solution.py:48
  63.8 4.0 %collective-permute-done.7.refs_3_.refs_7_ = bf16[320,128]{1,0:T(8,128)(2,1)S(1)} collective-permute-done((bf16[320,128]{1,0:T(8,128)(2,1)S(1)}, bf16[320,128]{1,0:T(8,128)(2,1)S(1)}, u32[]{:S(2)}, u32[]{:S(2)}) %collective-permute-start.7) | collective-permute-done | bytes 81952 | tf_op jit(solution)/shard_map/ppermute | solution.py:48
  67.8 3.4 %copy-done = bf16[1,1,2048,2048]{3,2,1,0:T(8,128)(2,1)S(1)} copy-done((bf16[1,1,2048,2048]{3,2,1,0:T(8,128)(2,1)S(1)}, bf16[1,1,2048,2048]{3,2,1,0:T(8,128)(2,1)}, u32[]{:S(2)}) %copy-start) | copy-done | bytes 8388632
  73.4 3.3 %shard_map.50 = (f32[2048,128]{1,0:T(8,128)S(1)}, f32[2048,128]{1,0:T(8,128)S(1)}, bf16[512,128]{1,0:T(8,128)(2,1)S(1)}, bf16[512,128]{1,0:T(8,128)(2,1)S(1)}, b...) custom-call(s32[2]{0:T(128)S(1)} %pad_add_fusion.odd.refs_0_, f32[2048,128]{1,0:T(8,128)S(1)} %get-tuple-element.35.stepped, ...), custom_call_target="tpu_custom_call" | custom-call | flops 1073741824 | bytes 16777216 | tf_op jit(solution)/shard_map/pallas_call | solution.py:18
  77.0 4.8 %collective-permute-start.9 = (bf16[512,128]{1,0:T(8,128)(2,1)S(1)}, bf16[512,128]{1,0:T(8,128)(2,1)S(1)}, u32[]{:S(2)}, u32[]{:S(2)}) collective-permute-start(bf16[512,128]{1,0:T(8,128)(2,1)S(1)} %get-tuple-element.44), channel_id=1, source_target_pairs={{16,32},{48,64},{80,96},{112,128},{144,160},{176,192},{208,224},{3... | collective-permute-start | bytes 393224 | tf_op jit(solution)/shard_map/ppermute | solution.py:48
  81.9 4.7 %collective-permute-start.11 = (bf16[512,128]{1,0:T(8,128)(2,1)S(1)}, bf16[512,128]{1,0:T(8,128)(2,1)S(1)}, u32[]{:S(2)}, u32[]{:S(2)}) collective-permute-start(bf16[512,128]{1,0:T(8,128)(2,1)S(1)} %get-tuple-element.46), channel_id=1, source_target_pairs={{1,2},{3,4},{5,6},{7,8},{9,10},{11,12},{13,14},{2,1},{4,3},{6,5},{... | collective-permute-start | bytes 393224 | tf_op jit(solution)/shard_map/ppermute | solution.py:48
  86.6 4.0 %collective-permute-done.11.refs_7_ = bf16[512,128]{1,0:T(8,128)(2,1)S(1)} collective-permute-done((bf16[512,128]{1,0:T(8,128)(2,1)S(1)}, bf16[512,128]{1,0:T(8,128)(2,1)S(1)}, u32[]{:S(2)}, u32[]{:S(2)}) %collective-permute-start.11) | collective-permute-done | bytes 131104 | tf_op jit(solution)/shard_map/ppermute | solution.py:48
  91.6 16.7 %all_to_all.32.columns = bf16[16,64,128]{2,1,0:T(8,128)(2,1)S(1)} all-to-all(bf16[16,64,128]{2,1,0:T(8,128)(2,1)S(1)} %get-tuple-element.48), channel_id=1, replica_groups=mesh['sx'=16,'sy'=16] {'sx'}, dimensions={0} | all-to-all | bytes 524288 | tf_op jit(solution)/shard_map/all_to_all | solution.py:165
  108.2 1.2 shard_map.52
  109.5 13.2 %all_to_all.33.parts = bf16[16,64,128]{2,1,0:T(8,128)(2,1)S(1)} all-to-all(bf16[16,64,128]{2,1,0:T(8,128)(2,1)S(1)} %shard_map.52), channel_id=1, replica_groups=mesh['sx'=16,'sy'=16] {'sy'}, dimensions={0} | all-to-all | bytes 524288 | tf_op jit(solution)/shard_map/all_to_all | solution.py:169
  123.3 4.3 %collective-permute-start.15 = (bf16[64,128]{1,0:T(8,128)(2,1)S(1)}, bf16[64,128]{1,0:T(8,128)(2,1)S(1)}, u32[]{:S(2)}, u32[]{:S(2)}) collective-permute-start(bf16[64,128]{1,0:T(8,128)(2,1)S(1)} %shard_map.53.own), channel_id=1, source_target_pairs={{1,2},{3,4},{5,6},{7,8},{9,10},{11,12},{13,14},{2,1},{4,3},{6,5},{... | collective-permute-start | bytes 49160 | tf_op jit(solution)/shard_map/ppermute | solution.py:48
  127.7 3.2 %collective-permute-start.13 = (bf16[64,128]{1,0:T(8,128)(2,1)S(1)}, bf16[64,128]{1,0:T(8,128)(2,1)S(1)}, u32[]{:S(2)}, u32[]{:S(2)}) collective-permute-start(bf16[64,128]{1,0:T(8,128)(2,1)S(1)} %shard_map.53.own), channel_id=1, source_target_pairs={{16,32},{48,64},{80,96},{112,128},{144,160},{176,192},{208,224},{3... | collective-permute-start | bytes 49160 | tf_op jit(solution)/shard_map/ppermute | solution.py:48
  131.0 3.2 %collective-permute-done.13.refs_5_ = bf16[64,128]{1,0:T(8,128)(2,1)S(1)} collective-permute-done((bf16[64,128]{1,0:T(8,128)(2,1)S(1)}, bf16[64,128]{1,0:T(8,128)(2,1)S(1)}, u32[]{:S(2)}, u32[]{:S(2)}) %collective-permute-start.13) | collective-permute-done | bytes 16416 | tf_op jit(solution)/shard_map/ppermute | solution.py:48
  134.7 3.3 %shard_map.54 = (f32[2048,128]{1,0:T(8,128)S(1)}, f32[2048,128]{1,0:T(8,128)S(1)}, bf16[512,128]{1,0:T(8,128)(2,1)S(1)}, bf16[512,128]{1,0:T(8,128)(2,1)S(1)}, b...) custom-call(s32[2]{0:T(128)S(1)} %pad_add_fusion.odd.refs_0_, f32[2048,128]{1,0:T(8,128)S(1)} %get-tuple-element.47.stepped, ...), custom_call_target="tpu_custom_call" | custom-call | flops 1073741824 | bytes 16777216 | tf_op jit(solution)/shard_map/pallas_call | solution.py:18
  138.1 4.7 %collective-permute-start.17 = (bf16[512,128]{1,0:T(8,128)(2,1)S(1)}, bf16[512,128]{1,0:T(8,128)(2,1)S(1)}, u32[]{:S(2)}, u32[]{:S(2)}) collective-permute-start(bf16[512,128]{1,0:T(8,128)(2,1)S(1)} %get-tuple-element.52), channel_id=1, source_target_pairs={{16,32},{48,64},{80,96},{112,128},{144,160},{176,192},{208,224},{3... | collective-permute-start | bytes 393224 | tf_op jit(solution)/shard_map/ppermute | solution.py:48
  143.0 4.0 %collective-permute-start.19 = (bf16[512,128]{1,0:T(8,128)(2,1)S(1)}, bf16[512,128]{1,0:T(8,128)(2,1)S(1)}, u32[]{:S(2)}, u32[]{:S(2)}) collective-permute-start(bf16[512,128]{1,0:T(8,128)(2,1)S(1)} %get-tuple-element.54), channel_id=1, source_target_pairs={{1,2},{3,4},{5,6},{7,8},{9,10},{11,12},{13,14},{2,1},{4,3},{6,5},{... | collective-permute-start | bytes 393224 | tf_op jit(solution)/shard_map/ppermute | solution.py:48
  147.1 4.7 %collective-permute-done.19.refs_7_ = bf16[512,128]{1,0:T(8,128)(2,1)S(1)} collective-permute-done((bf16[512,128]{1,0:T(8,128)(2,1)S(1)}, bf16[512,128]{1,0:T(8,128)(2,1)S(1)}, u32[]{:S(2)}, u32[]{:S(2)}) %collective-permute-start.19) | collective-permute-done | bytes 131104 | tf_op jit(solution)/shard_map/ppermute | solution.py:48
  152.7 16.9 %all_to_all.34.columns = bf16[16,64,128]{2,1,0:T(8,128)(2,1)S(1)} all-to-all(bf16[16,64,128]{2,1,0:T(8,128)(2,1)S(1)} %get-tuple-element.56), channel_id=1, replica_groups=mesh['sx'=16,'sy'=16] {'sx'}, dimensions={0} | all-to-all | bytes 524288 | tf_op jit(solution)/shard_map/all_to_all | solution.py:165
  169.6 1.2 shard_map.56
  170.8 12.1 %all_to_all.35.parts = bf16[16,64,128]{2,1,0:T(8,128)(2,1)S(1)} all-to-all(bf16[16,64,128]{2,1,0:T(8,128)(2,1)S(1)} %shard_map.56), channel_id=1, replica_groups=mesh['sx'=16,'sy'=16] {'sy'}, dimensions={0} | all-to-all | bytes 524288 | tf_op jit(solution)/shard_map/all_to_all | solution.py:169
  183.5 4.3 %collective-permute-start.23 = (bf16[64,128]{1,0:T(8,128)(2,1)S(1)}, bf16[64,128]{1,0:T(8,128)(2,1)S(1)}, u32[]{:S(2)}, u32[]{:S(2)}) collective-permute-start(bf16[64,128]{1,0:T(8,128)(2,1)S(1)} %shard_map.57.own), channel_id=1, source_target_pairs={{1,2},{3,4},{5,6},{7,8},{9,10},{11,12},{13,14},{2,1},{4,3},{6,5},{... | collective-permute-start | bytes 49160 | tf_op jit(solution)/shard_map/ppermute | solution.py:48
  187.9 3.2 %collective-permute-start.21 = (bf16[64,128]{1,0:T(8,128)(2,1)S(1)}, bf16[64,128]{1,0:T(8,128)(2,1)S(1)}, u32[]{:S(2)}, u32[]{:S(2)}) collective-permute-start(bf16[64,128]{1,0:T(8,128)(2,1)S(1)} %shard_map.57.own), channel_id=1, source_target_pairs={{16,32},{48,64},{80,96},{112,128},{144,160},{176,192},{208,224},{3... | collective-permute-start | bytes 49160 | tf_op jit(solution)/shard_map/ppermute | solution.py:48
  191.2 3.2 %collective-permute-done.21.refs_5_ = bf16[64,128]{1,0:T(8,128)(2,1)S(1)} collective-permute-done((bf16[64,128]{1,0:T(8,128)(2,1)S(1)}, bf16[64,128]{1,0:T(8,128)(2,1)S(1)}, u32[]{:S(2)}, u32[]{:S(2)}) %collective-permute-start.21) | collective-permute-done | bytes 16416 | tf_op jit(solution)/shard_map/ppermute | solution.py:48
  194.9 1.9 shard_map.58
  (58 shorter events, 14.7 us)
Async XLA Ops:
  0.1 1.2 copy-start.4
  1.9 9.7 %collective-permute-start = (bf16[512,128]{1,0:T(8,128)(2,1)S(1)}, bf16[512,128]{1,0:T(8,128)(2,1)S(1)}, u32[]{:S(2)}, u32[]{:S(2)}) collective-permute-start(bf16[512,128]{1,0:T(8,128)(2,1)S(1)} %get-tuple-element.31), channel_id=1, source_target_pairs={{0,16},{32,48},{64,80},{96,112},{128,144},{160,176},{192,208},{224... | collective-permute-start | bytes 393224 | tf_op jit(solution)/shard_map/ppermute | solution.py:48
  2.4 9.2 %collective-permute-start.1 = (bf16[512,128]{1,0:T(8,128)(2,1)S(1)}, bf16[512,128]{1,0:T(8,128)(2,1)S(1)}, u32[]{:S(2)}, u32[]{:S(2)}) collective-permute-start(bf16[512,128]{1,0:T(8,128)(2,1)S(1)} %get-tuple-element.32), channel_id=1, source_target_pairs={{16,32},{48,64},{80,96},{112,128},{144,160},{176,192},{208,224},{3... | collective-permute-start | bytes 393224 | tf_op jit(solution)/shard_map/ppermute | solution.py:48
  7.3 4.4 %collective-permute-start.2 = (bf16[512,128]{1,0:T(8,128)(2,1)S(1)}, bf16[512,128]{1,0:T(8,128)(2,1)S(1)}, u32[]{:S(2)}, u32[]{:S(2)}) collective-permute-start(bf16[512,128]{1,0:T(8,128)(2,1)S(1)} %get-tuple-element.33), channel_id=1, source_target_pairs={{0,1},{2,3},{4,5},{6,7},{8,9},{10,11},{12,13},{14,15},{1,0},{3,2},... | collective-permute-start | bytes 393224 | tf_op jit(solution)/shard_map/ppermute | solution.py:48
  7.4 8.8 %collective-permute-start.3 = (bf16[512,128]{1,0:T(8,128)(2,1)S(1)}, bf16[512,128]{1,0:T(8,128)(2,1)S(1)}, u32[]{:S(2)}, u32[]{:S(2)}) collective-permute-start(bf16[512,128]{1,0:T(8,128)(2,1)S(1)} %get-tuple-element.34), channel_id=1, source_target_pairs={{1,2},{3,4},{5,6},{7,8},{9,10},{11,12},{13,14},{2,1},{4,3},{6,5},{... | collective-permute-start | bytes 393224 | tf_op jit(solution)/shard_map/ppermute | solution.py:48
  17.1 73.6 %copy-start.10 = (bf16[1,1,64,2048]{3,2,1,0:T(8,128)(2,1)S(1)}, bf16[1,1,64,2048]{3,2,1,0:T(8,128)(2,1)}, u32[]{:S(2)}) copy-start(bf16[1,1,64,2048]{3,2,1,0:T(8,128)(2,1)} %param.6) | copy-start | bytes 786436
  38.7 1.6 copy-start.2
  40.3 67.9 %copy-start.3 = (bf16[1,1,1024,1024]{3,2,1,0:T(8,128)(2,1)S(1)}, bf16[1,1,1024,1024]{3,2,1,0:T(8,128)(2,1)}, u32[]{:S(2)}) copy-start(bf16[1,1,1024,1024]{3,2,1,0:T(8,128)(2,1)} %param.7) | copy-start | bytes 6291460
  55.8 8.0 %collective-permute-start.5 = (bf16[320,128]{1,0:T(8,128)(2,1)S(1)}, bf16[320,128]{1,0:T(8,128)(2,1)S(1)}, u32[]{:S(2)}, u32[]{:S(2)}) collective-permute-start(bf16[320,128]{1,0:T(8,128)(2,1)S(1)} %get-tuple-element.38), channel_id=1, source_target_pairs={{16,32},{48,64},{80,96},{112,128},{144,160},{176,192},{208,224},{3... | collective-permute-start | bytes 245768 | tf_op jit(solution)/shard_map/ppermute | solution.py:48
  59.0 4.8 %collective-permute-start.6 = (bf16[320,128]{1,0:T(8,128)(2,1)S(1)}, bf16[320,128]{1,0:T(8,128)(2,1)S(1)}, u32[]{:S(2)}, u32[]{:S(2)}) collective-permute-start(bf16[320,128]{1,0:T(8,128)(2,1)S(1)} %get-tuple-element.39), channel_id=1, source_target_pairs={{0,1},{2,3},{4,5},{6,7},{8,9},{10,11},{12,13},{14,15},{1,0},{3,2},... | collective-permute-start | bytes 245768 | tf_op jit(solution)/shard_map/ppermute | solution.py:48
  59.6 8.3 %collective-permute-start.7 = (bf16[320,128]{1,0:T(8,128)(2,1)S(1)}, bf16[320,128]{1,0:T(8,128)(2,1)S(1)}, u32[]{:S(2)}, u32[]{:S(2)}) collective-permute-start(bf16[320,128]{1,0:T(8,128)(2,1)S(1)} %get-tuple-element.40), channel_id=1, source_target_pairs={{1,2},{3,4},{5,6},{7,8},{9,10},{11,12},{13,14},{2,1},{4,3},{6,5},{... | collective-permute-start | bytes 245768 | tf_op jit(solution)/shard_map/ppermute | solution.py:48
  62.8 5.0 %collective-permute-start.4 = (bf16[320,128]{1,0:T(8,128)(2,1)S(1)}, bf16[320,128]{1,0:T(8,128)(2,1)S(1)}, u32[]{:S(2)}, u32[]{:S(2)}) collective-permute-start(bf16[320,128]{1,0:T(8,128)(2,1)S(1)} %get-tuple-element.37.own), channel_id=1, source_target_pairs={{0,16},{32,48},{64,80},{96,112},{128,144},{160,176},{192,208},{224... | collective-permute-start | bytes 245768 | tf_op jit(solution)/shard_map/ppermute | solution.py:48
  67.8 3.4 %copy-start = (bf16[1,1,2048,2048]{3,2,1,0:T(8,128)(2,1)S(1)}, bf16[1,1,2048,2048]{3,2,1,0:T(8,128)(2,1)}, u32[]{:S(2)}) copy-start(bf16[1,1,2048,2048]{3,2,1,0:T(8,128)(2,1)} %param.4) | copy-start | bytes 25165828
  71.2 1.2 copy-start.5
  73.4 61.3 %copy-start.1 = (bf16[1,1,2048,2048]{3,2,1,0:T(8,128)(2,1)S(1)}, bf16[1,1,2048,2048]{3,2,1,0:T(8,128)(2,1)}, u32[]{:S(2)}) copy-start(bf16[1,1,2048,2048]{3,2,1,0:T(8,128)(2,1)} %param.4) | copy-start | bytes 25165828
  73.4 61.3 %copy-start.6 = (f32[1,1,2048,128]{3,2,1,0:T(8,128)S(1)}, f32[1,1,2048,128]{3,2,1,0:T(8,128)}, u32[]{:S(2)}) copy-start(f32[1,1,2048,128]{3,2,1,0:T(8,128)} %param.5) | copy-start | bytes 3145732
  76.7 9.9 %collective-permute-start.8 = (bf16[512,128]{1,0:T(8,128)(2,1)S(1)}, bf16[512,128]{1,0:T(8,128)(2,1)S(1)}, u32[]{:S(2)}, u32[]{:S(2)}) collective-permute-start(bf16[512,128]{1,0:T(8,128)(2,1)S(1)} %get-tuple-element.43), channel_id=1, source_target_pairs={{0,16},{32,48},{64,80},{96,112},{128,144},{160,176},{192,208},{224... | collective-permute-start | bytes 393224 | tf_op jit(solution)/shard_map/ppermute | solution.py:48
  77.0 9.6 %collective-permute-start.9 = (bf16[512,128]{1,0:T(8,128)(2,1)S(1)}, bf16[512,128]{1,0:T(8,128)(2,1)S(1)}, u32[]{:S(2)}, u32[]{:S(2)}) collective-permute-start(bf16[512,128]{1,0:T(8,128)(2,1)S(1)} %get-tuple-element.44), channel_id=1, source_target_pairs={{16,32},{48,64},{80,96},{112,128},{144,160},{176,192},{208,224},{3... | collective-permute-start | bytes 393224 | tf_op jit(solution)/shard_map/ppermute | solution.py:48
  81.8 4.8 %collective-permute-start.10 = (bf16[512,128]{1,0:T(8,128)(2,1)S(1)}, bf16[512,128]{1,0:T(8,128)(2,1)S(1)}, u32[]{:S(2)}, u32[]{:S(2)}) collective-permute-start(bf16[512,128]{1,0:T(8,128)(2,1)S(1)} %get-tuple-element.45), channel_id=1, source_target_pairs={{0,1},{2,3},{4,5},{6,7},{8,9},{10,11},{12,13},{14,15},{1,0},{3,2},... | collective-permute-start | bytes 393224 | tf_op jit(solution)/shard_map/ppermute | solution.py:48
  81.9 8.8 %collective-permute-start.11 = (bf16[512,128]{1,0:T(8,128)(2,1)S(1)}, bf16[512,128]{1,0:T(8,128)(2,1)S(1)}, u32[]{:S(2)}, u32[]{:S(2)}) collective-permute-start(bf16[512,128]{1,0:T(8,128)(2,1)S(1)} %get-tuple-element.46), channel_id=1, source_target_pairs={{1,2},{3,4},{5,6},{7,8},{9,10},{11,12},{13,14},{2,1},{4,3},{6,5},{... | collective-permute-start | bytes 393224 | tf_op jit(solution)/shard_map/ppermute | solution.py:48
  123.3 7.7 %collective-permute-start.15 = (bf16[64,128]{1,0:T(8,128)(2,1)S(1)}, bf16[64,128]{1,0:T(8,128)(2,1)S(1)}, u32[]{:S(2)}, u32[]{:S(2)}) collective-permute-start(bf16[64,128]{1,0:T(8,128)(2,1)S(1)} %shard_map.53.own), channel_id=1, source_target_pairs={{1,2},{3,4},{5,6},{7,8},{9,10},{11,12},{13,14},{2,1},{4,3},{6,5},{... | collective-permute-start | bytes 49160 | tf_op jit(solution)/shard_map/ppermute | solution.py:48
  127.6 3.4 %collective-permute-start.14 = (bf16[64,128]{1,0:T(8,128)(2,1)S(1)}, bf16[64,128]{1,0:T(8,128)(2,1)S(1)}, u32[]{:S(2)}, u32[]{:S(2)}) collective-permute-start(bf16[64,128]{1,0:T(8,128)(2,1)S(1)} %shard_map.53.own), channel_id=1, source_target_pairs={{0,1},{2,3},{4,5},{6,7},{8,9},{10,11},{12,13},{14,15},{1,0},{3,2},... | collective-permute-start | bytes 49160 | tf_op jit(solution)/shard_map/ppermute | solution.py:48
  127.7 6.5 %collective-permute-start.13 = (bf16[64,128]{1,0:T(8,128)(2,1)S(1)}, bf16[64,128]{1,0:T(8,128)(2,1)S(1)}, u32[]{:S(2)}, u32[]{:S(2)}) collective-permute-start(bf16[64,128]{1,0:T(8,128)(2,1)S(1)} %shard_map.53.own), channel_id=1, source_target_pairs={{16,32},{48,64},{80,96},{112,128},{144,160},{176,192},{208,224},{3... | collective-permute-start | bytes 49160 | tf_op jit(solution)/shard_map/ppermute | solution.py:48
  130.8 3.8 %collective-permute-start.12 = (bf16[64,128]{1,0:T(8,128)(2,1)S(1)}, bf16[64,128]{1,0:T(8,128)(2,1)S(1)}, u32[]{:S(2)}, u32[]{:S(2)}) collective-permute-start(bf16[64,128]{1,0:T(8,128)(2,1)S(1)} %shard_map.53.own), channel_id=1, source_target_pairs={{0,16},{32,48},{64,80},{96,112},{128,144},{160,176},{192,208},{224... | collective-permute-start | bytes 49160 | tf_op jit(solution)/shard_map/ppermute | solution.py:48
  138.0 9.1 %collective-permute-start.16 = (bf16[512,128]{1,0:T(8,128)(2,1)S(1)}, bf16[512,128]{1,0:T(8,128)(2,1)S(1)}, u32[]{:S(2)}, u32[]{:S(2)}) collective-permute-start(bf16[512,128]{1,0:T(8,128)(2,1)S(1)} %get-tuple-element.51), channel_id=1, source_target_pairs={{0,16},{32,48},{64,80},{96,112},{128,144},{160,176},{192,208},{224... | collective-permute-start | bytes 393224 | tf_op jit(solution)/shard_map/ppermute | solution.py:48
  138.1 9.0 %collective-permute-start.17 = (bf16[512,128]{1,0:T(8,128)(2,1)S(1)}, bf16[512,128]{1,0:T(8,128)(2,1)S(1)}, u32[]{:S(2)}, u32[]{:S(2)}) collective-permute-start(bf16[512,128]{1,0:T(8,128)(2,1)S(1)} %get-tuple-element.52), channel_id=1, source_target_pairs={{16,32},{48,64},{80,96},{112,128},{144,160},{176,192},{208,224},{3... | collective-permute-start | bytes 393224 | tf_op jit(solution)/shard_map/ppermute | solution.py:48
  142.7 4.3 %collective-permute-start.18 = (bf16[512,128]{1,0:T(8,128)(2,1)S(1)}, bf16[512,128]{1,0:T(8,128)(2,1)S(1)}, u32[]{:S(2)}, u32[]{:S(2)}) collective-permute-start(bf16[512,128]{1,0:T(8,128)(2,1)S(1)} %get-tuple-element.53), channel_id=1, source_target_pairs={{0,1},{2,3},{4,5},{6,7},{8,9},{10,11},{12,13},{14,15},{1,0},{3,2},... | collective-permute-start | bytes 393224 | tf_op jit(solution)/shard_map/ppermute | solution.py:48
  143.0 8.8 %collective-permute-start.19 = (bf16[512,128]{1,0:T(8,128)(2,1)S(1)}, bf16[512,128]{1,0:T(8,128)(2,1)S(1)}, u32[]{:S(2)}, u32[]{:S(2)}) collective-permute-start(bf16[512,128]{1,0:T(8,128)(2,1)S(1)} %get-tuple-element.54), channel_id=1, source_target_pairs={{1,2},{3,4},{5,6},{7,8},{9,10},{11,12},{13,14},{2,1},{4,3},{6,5},{... | collective-permute-start | bytes 393224 | tf_op jit(solution)/shard_map/ppermute | solution.py:48
  183.5 7.7 %collective-permute-start.23 = (bf16[64,128]{1,0:T(8,128)(2,1)S(1)}, bf16[64,128]{1,0:T(8,128)(2,1)S(1)}, u32[]{:S(2)}, u32[]{:S(2)}) collective-permute-start(bf16[64,128]{1,0:T(8,128)(2,1)S(1)} %shard_map.57.own), channel_id=1, source_target_pairs={{1,2},{3,4},{5,6},{7,8},{9,10},{11,12},{13,14},{2,1},{4,3},{6,5},{... | collective-permute-start | bytes 49160 | tf_op jit(solution)/shard_map/ppermute | solution.py:48
  187.8 3.4 %collective-permute-start.22 = (bf16[64,128]{1,0:T(8,128)(2,1)S(1)}, bf16[64,128]{1,0:T(8,128)(2,1)S(1)}, u32[]{:S(2)}, u32[]{:S(2)}) collective-permute-start(bf16[64,128]{1,0:T(8,128)(2,1)S(1)} %shard_map.57.own), channel_id=1, source_target_pairs={{0,1},{2,3},{4,5},{6,7},{8,9},{10,11},{12,13},{14,15},{1,0},{3,2},... | collective-permute-start | bytes 49160 | tf_op jit(solution)/shard_map/ppermute | solution.py:48
  187.9 6.5 %collective-permute-start.21 = (bf16[64,128]{1,0:T(8,128)(2,1)S(1)}, bf16[64,128]{1,0:T(8,128)(2,1)S(1)}, u32[]{:S(2)}, u32[]{:S(2)}) collective-permute-start(bf16[64,128]{1,0:T(8,128)(2,1)S(1)} %shard_map.57.own), channel_id=1, source_target_pairs={{16,32},{48,64},{80,96},{112,128},{144,160},{176,192},{208,224},{3... | collective-permute-start | bytes 49160 | tf_op jit(solution)/shard_map/ppermute | solution.py:48
  191.1 3.8 %collective-permute-start.20 = (bf16[64,128]{1,0:T(8,128)(2,1)S(1)}, bf16[64,128]{1,0:T(8,128)(2,1)S(1)}, u32[]{:S(2)}, u32[]{:S(2)}) collective-permute-start(bf16[64,128]{1,0:T(8,128)(2,1)S(1)} %shard_map.57.own), channel_id=1, source_target_pairs={{0,16},{32,48},{64,80},{96,112},{128,144},{160,176},{192,208},{224... | collective-permute-start | bytes 49160 | tf_op jit(solution)/shard_map/ppermute | solution.py:48
  (3 other events, 2.9 us)

commit v2 on v1

v2 whole, which is shorter than its diff:
```python
import functools

import jax
import jax.numpy as jnp
from jax import lax
from jax.experimental import pallas as pl
from jax.experimental.pallas import tpu as pltpu
from jax.sharding import PartitionSpec as P


ITERS = 3
DAMPING = 0.5

VMEM = pl.BlockSpec(memory_space=pltpu.VMEM)
SMEM = pl.BlockSpec(memory_space=pltpu.SMEM)
HBM = pl.BlockSpec(memory_space=pltpu.HBM)
BF16 = jnp.bfloat16
F32 = jnp.float32


def kernel_call(body, outs, scratch=(), flops=0, moved=0, limit=16 << 20, outside=()):
    return lambda *operands: pl.pallas_call(
        body,
        out_shape=tuple(outs),
        in_specs=[SMEM] + [HBM if i in outside else VMEM for i in range(1, len(operands))],
        out_specs=tuple([VMEM] * len(outs)),
        scratch_shapes=list(scratch),
        compiler_params=pltpu.CompilerParams(vmem_limit_bytes=limit),
        cost_estimate=pl.CostEstimate(flops=flops, bytes_accessed=moved, transcendentals=0),
    )(*operands)


def place_facts():
    places = [(lax.axis_index(axis), lax.axis_size(axis)) for axis in ("sx", "sy")]
    odd = [lax.rem(place, 2) for place, count in places]
    ends = [((place == 0) | (place == count - 1)).astype(jnp.int32) for place, count in places]
    return jnp.stack(odd + ends)


EXCHANGES = ((1, True), (0, True), (0, False), (1, False))


def face_starts(facts, width):
    starts = []
    for axis, far in EXCHANGES:
        odd = facts[axis]
        starts.append(pl.multiple_of((2 * axis + (odd if far else 1 - odd)) * width, width))
    return starts


def from_neighbours(facts, received):
    arrays = []
    for (axis, far), array in zip(EXCHANGES, received):
        arrays.append(jnp.where(facts[2 + axis] == 1, jnp.zeros_like(array), array) if far else array)
    return arrays


def exchange(parts):
    received = []
    for (axis, far), part in zip(EXCHANGES, parts):
        name = ("sx", "sy")[axis]
        count = lax.axis_size(name)
        lower = range(1 if far else 0, count, 2)
        pairs = [(i, (i + 1) % count) for i in lower] + [((i + 1) % count, i) for i in lower]
        received.append(lax.ppermute(part, name, pairs))
    return received


def faces_body(facts, loads, basis, tile, *refs):
    faces, right, basis_here, tile_here, arrived = refs[:4], *refs[4:]
    width = loads.shape[0] // 4
    blocks = [pl.ds(start, width) for start in face_starts(facts, width)]
    pairs = [(loads.at[block, :], right.at[block, :]) for block in blocks]
    pairs += [(basis, basis_here), (tile, tile_here)]
    copies = [
        pltpu.make_async_copy(source, target, arrived.at[index])
        for index, (source, target) in enumerate(pairs)
    ]
    for copy in copies:
        copy.start()
    for copy, block, face in zip(copies, blocks, faces):
        copy.wait()
        face[...] = right[block, :].astype(BF16)
    for copy in copies[4:]:
        copy.wait()


def restrict_body(first, facts, *refs):
    values, basis, *others = refs
    held = None if first else others.pop(0)
    received = others[:4]
    stepped, coarse = others[4:]
    width = values.shape[0] // 4
    total = jnp.zeros(coarse.shape[1:], F32)
    sides = from_neighbours(facts, [part[...].astype(F32) for part in received])
    for start, side in zip(face_starts(facts, width), sides):
        rows = pl.ds(start, width)
        residual = values[rows, :] - side
        half = DAMPING * residual
        stepped[rows, :] = half if first else held[rows, :] + half
        total += jnp.dot(basis[:, rows], residual.astype(BF16), preferred_element_type=F32)
    coarse[...] = jnp.broadcast_to(total.astype(BF16)[None], coarse.shape)


def tile_body(facts, tile, columns, partial):
    count, rows, loads = partial.shape
    whole = columns[...].reshape(tile.shape[1], loads)
    product = jnp.dot(tile[...], whole, preferred_element_type=F32)
    partial[...] = product.astype(BF16).reshape(count, rows, loads)


def sum_body(facts, parts, total):
    total[...] = jnp.sum(parts[...].astype(F32), axis=0).astype(BF16)


def sum_with_basis_body(facts, parts, basis, *messages):
    total = jnp.sum(parts[...].astype(F32), axis=0).astype(BF16)
    rows, loads = total.shape
    width = basis.shape[1] // 4
    for start, message in zip(face_starts(facts, width), messages):
        message[:rows, :] = total
        for piece in range(width // loads):
            columns = pl.ds(pl.multiple_of(start + piece * loads, loads), loads)
            message[(piece + 1) * rows : (piece + 2) * rows, :] = basis[:, columns]


def corrected(stepped, basis, own, slices, theirs, start, width):
    rows, loads = own.shape
    near = basis[:, pl.ds(start, width)]
    far = jnp.concatenate(
        [slices[(i + 1) * rows : (i + 2) * rows, :] for i in range(width // loads)], axis=1
    )
    weights = jnp.concatenate([near, far], axis=0)
    columns = jnp.concatenate([own, -theirs], axis=0)
    back = lax.dot_general(
        weights, columns, (((0,), (0,)), ((), ())), preferred_element_type=F32
    )
    return stepped[pl.ds(start, width), :] - DAMPING * back


def advance_body(load, facts, stepped, basis, own, operator, right, *refs):
    slices, theirs = refs[:4], refs[4:8]
    held, values = refs[8:10]
    faces, others = refs[10:14], refs[14:]
    width = values.shape[0] // 4
    rows = basis.shape[0]
    starts = face_starts(facts, width)
    copies = []
    if load:
        source, operator, rounded, arrived = operator, *others
        for index, start in enumerate(starts):
            block = pl.ds(start, width)
            copies.append(
                pltpu.make_async_copy(
                    source.at[block, :], operator.at[block, :], arrived.at[index]
                )
            )
            copies[-1].start()
    else:
        (rounded,) = others
    corrections = from_neighbours(facts, [part[:rows, :] for part in theirs])
    for start, kept, other in zip(starts, slices, corrections):
        part = corrected(stepped, basis, own[:rows, :], kept, other, start, width)
        held[pl.ds(start, width), :] = part
        rounded[pl.ds(start, width), :] = part.astype(BF16)
    for index, (start, face) in enumerate(zip(starts, faces)):
        block = pl.ds(start, width)
        if load:
            copies[index].wait()
        product = jnp.dot(operator[block, :], rounded[...], preferred_element_type=F32)
        value = right[block, :] - product
        values[block, :] = value
        face[...] = value.astype(BF16)


def finish_body(facts, stepped, basis, own, *refs):
    slices, theirs, (out,) = refs[:4], refs[4:8], refs[8:]
    width = out.shape[0] // 4
    rows = basis.shape[0]
    others = from_neighbours(facts, [part[:rows, :] for part in theirs])
    for start, kept, other in zip(face_starts(facts, width), slices, others):
        out[pl.ds(start, width), :] = corrected(
            stepped, basis, own[:rows, :], kept, other, start, width
        )


def local(dual_ops, loads, kernel_basis, coarse_inverse):
    operator, right, basis, tile = dual_ops[0, 0], loads[0, 0], kernel_basis[0, 0], coarse_inverse[0, 0]
    size, columns = right.shape
    width = size // 4
    rows = basis.shape[0]
    whole = jax.ShapeDtypeStruct(right.shape, F32)
    face = jax.ShapeDtypeStruct((width, columns), BF16)
    blocks_x = jax.ShapeDtypeStruct((lax.axis_size("sx"), rows, columns), BF16)
    blocks_y = jax.ShapeDtypeStruct((lax.axis_size("sy"), rows, columns), BF16)
    coarse = jax.ShapeDtypeStruct((rows, columns), BF16)
    message = jax.ShapeDtypeStruct((rows + width * rows // columns, columns), BF16)

    facts = place_facts()
    *faces, right, basis, tile = kernel_call(
        faces_body,
        [face] * 4 + [jax.ShapeDtypeStruct(x.shape, x.dtype) for x in (right, basis, tile)],
        [pltpu.SemaphoreType.DMA((7,))],
        moved=8 << 20,
        outside=(1, 2, 3),
    )(facts, right, basis, tile)
    values, held = right, None
    for step in range(ITERS):
        received = exchange(faces)
        first = step == 0
        stepped, sent = kernel_call(
            functools.partial(restrict_body, first),
            [whole, blocks_x],
            flops=2 * rows * size * columns,
            moved=4 << 20,
        )(facts, values, basis, *([] if first else [held]), *received)
        gathered = lax.all_to_all(sent, "sx", 0, 0, tiled=True)
        (partial,) = kernel_call(
            tile_body, [blocks_y], flops=2 * tile.size * columns, moved=3 << 20
        )(facts, tile, gathered)
        parts = lax.all_to_all(partial, "sy", 0, 0, tiled=True)
        if first:
            messages = kernel_call(sum_with_basis_body, [message] * 4, moved=1 << 20)(facts, parts, basis)
            own = messages[0]
            theirs = exchange(messages)
            slices = theirs
        else:
            (own,) = kernel_call(sum_body, [coarse], moved=1 << 18)(facts, parts)
            theirs = exchange([own] * 4)
        if step < ITERS - 1:
            outs, scratch = [whole, whole] + [face] * 4, [pltpu.VMEM((size, columns), BF16)]
            if first:
                outs.append(jax.ShapeDtypeStruct(operator.shape, BF16))
                scratch.append(pltpu.SemaphoreType.DMA((4,)))
            held, values, *faces = kernel_call(
                functools.partial(advance_body, first),
                outs,
                scratch,
                flops=2 * operator.size * columns,
                moved=16 << 20,
                outside=(4,) if first else (),
            )(facts, stepped, basis, own, operator, right, *slices, *theirs)
            if first:
                operator = faces.pop()
        else:
            (out,) = kernel_call(finish_body, [whole], moved=2 << 20)(
                facts, stepped, basis, own, *slices, *theirs
            )
    return out[None, None]


def solution(mesh):
    placed = P("sx", "sy", None, None)
    return jax.shard_map(
        local, mesh=mesh, in_specs=(placed,) * 4, out_specs=placed, check_vma=False
    )
```

time: 198 us -> 182 us (0.919)
  the two profiles are of different devices: /device:TPU:10 before, /device:TPU:32 now
where the time goes in v2:
time: 182 us; the launch traced here: 181 us
  blocking collectives  94.8 us (52%)
  waiting for transfers between devices  37.4 us (21%)
  starting transfers between devices  24.1 us (13%)
  Pallas kernels  20.6 us (11%)
  local copies, waits for them, and re-layouts  4.2 us (2%)
    all_to_all x3, blocking collectives, local(): gathered = lax.all_to_all(sent, 'sx', 0, 0, tiled=True)  53 us
    all_to_all x3, blocking collectives, local(): parts = lax.all_to_all(partial, 'sy', 0, 0, tiled=True)  41.8 us
    ppermute x24, waiting for transfers between devices, exchange(): received.append(lax.ppermute(part, name, pairs))  37.4 us
    ppermute x24, starting transfers between devices, exchange(): received.append(lax.ppermute(part, name, pairs))  24.1 us
    pallas_call x13, Pallas kernels, kernel_call(): pl.pallas_call(body, out_shape=tuple(outs), in_specs=[SMEM] + [HBM if i i...  20.6 us
    unnamed x8, local copies, waits for them, and re-layouts  4.2 us
  transfers between devices with their start and end apart: 24, of which 15 were waited for; matrix products, arithmetic and copies ran while one was open for 0% of the time, Pallas kernels for 0%

profile of v2, /device:TPU:32, one launch (start us, length us, event | category | flops | bytes accessed | tf_op | source)
XLA Modules:
  0.0 181.3 jit_solution(16575789446344087489)
XLA Ops:
  0.1 1.7 copy-done.1
  1.8 1.5 copy-done.2
  5.2 4.9 %collective-permute-start = (bf16[512,128]{1,0:T(8,128)(2,1)S(1)}, bf16[512,128]{1,0:T(8,128)(2,1)S(1)}, u32[]{:S(2)}, u32[]{:S(2)}) collective-permute-start(bf16[512,128]{1,0:T(8,128)(2,1)S(1)} %get-tuple-element.37), channel_id=1, source_target_pairs={{1,2},{3,4},{5,6},{7,8},{9,10},{11,12},{13,14},{15,0},{2,1},{4,3},... | collective-permute-start | bytes 393224 | tf_op jit(solution)/shard_map/ppermute | solution.py:65
  10.3 3.2 %collective-permute-start.2 = (bf16[512,128]{1,0:T(8,128)(2,1)S(1)}, bf16[512,128]{1,0:T(8,128)(2,1)S(1)}, u32[]{:S(2)}, u32[]{:S(2)}) collective-permute-start(bf16[512,128]{1,0:T(8,128)(2,1)S(1)} %get-tuple-element.39), channel_id=1, source_target_pairs={{0,16},{32,48},{64,80},{96,112},{128,144},{160,176},{192,208},{224... | collective-permute-start | bytes 393224 | tf_op jit(solution)/shard_map/ppermute | solution.py:65
  13.7 2.4 %collective-permute-done.1.refs_3_ = bf16[512,128]{1,0:T(8,128)(2,1)S(1)} collective-permute-done((bf16[512,128]{1,0:T(8,128)(2,1)S(1)}, bf16[512,128]{1,0:T(8,128)(2,1)S(1)}, u32[]{:S(2)}, u32[]{:S(2)}) %collective-permute-start.1) | collective-permute-done | bytes 131104 | tf_op jit(solution)/shard_map/ppermute | solution.py:65
  16.1 2.5 %collective-permute-done.2.refs_4_ = bf16[512,128]{1,0:T(8,128)(2,1)S(1)} collective-permute-done((bf16[512,128]{1,0:T(8,128)(2,1)S(1)}, bf16[512,128]{1,0:T(8,128)(2,1)S(1)}, u32[]{:S(2)}, u32[]{:S(2)}) %collective-permute-start.2) | collective-permute-done | bytes 131104 | tf_op jit(solution)/shard_map/ppermute | solution.py:65
  19.4 19.8 %all_to_all.30.columns = bf16[16,64,128]{2,1,0:T(8,128)(2,1)S(1)} all-to-all(bf16[16,64,128]{2,1,0:T(8,128)(2,1)S(1)} %get-tuple-element.43), channel_id=1, replica_groups=mesh['sx'=16,'sy'=16] {'sx'}, dimensions={0} | all-to-all | bytes 524288 | tf_op jit(solution)/shard_map/all_to_all | solution.py:217
  39.2 1.2 shard_map.48
  40.4 13.7 %all_to_all.31.parts = bf16[16,64,128]{2,1,0:T(8,128)(2,1)S(1)} all-to-all(bf16[16,64,128]{2,1,0:T(8,128)(2,1)S(1)} %shard_map.48), channel_id=1, replica_groups=mesh['sx'=16,'sy'=16] {'sy'}, dimensions={0} | all-to-all | bytes 524288 | tf_op jit(solution)/shard_map/all_to_all | solution.py:221
  54.8 1.1 collective-permute-start.5
  55.9 1.6 collective-permute-start.6
  58.1 2.2 %collective-permute-done.5.refs_1_.refs_5_ = bf16[320,128]{1,0:T(8,128)(2,1)S(1)} collective-permute-done((bf16[320,128]{1,0:T(8,128)(2,1)S(1)}, bf16[320,128]{1,0:T(8,128)(2,1)S(1)}, u32[]{:S(2)}, u32[]{:S(2)}) %collective-permute-start.5) | collective-permute-done | bytes 81952 | tf_op jit(solution)/shard_map/ppermute | solution.py:65
  60.3 2.6 %collective-permute-done.6.refs_2_.refs_6_ = bf16[320,128]{1,0:T(8,128)(2,1)S(1)} collective-permute-done((bf16[320,128]{1,0:T(8,128)(2,1)S(1)}, bf16[320,128]{1,0:T(8,128)(2,1)S(1)}, u32[]{:S(2)}, u32[]{:S(2)}) %collective-permute-start.6) | collective-permute-done | bytes 81952 | tf_op jit(solution)/shard_map/ppermute | solution.py:65
  63.0 1.9 %collective-permute-done.4.refs_0_.refs_4_ = bf16[320,128]{1,0:T(8,128)(2,1)S(1)} collective-permute-done((bf16[320,128]{1,0:T(8,128)(2,1)S(1)}, bf16[320,128]{1,0:T(8,128)(2,1)S(1)}, u32[]{:S(2)}, u32[]{:S(2)}) %collective-permute-start.4) | collective-permute-done | bytes 81952 | tf_op jit(solution)/shard_map/ppermute | solution.py:65
  64.9 6.5 %shard_map.50 = (f32[2048,128]{1,0:T(8,128)S(1)}, f32[2048,128]{1,0:T(8,128)S(1)}, bf16[512,128]{1,0:T(8,128)(2,1)S(1)}, bf16[512,128]{1,0:T(8,128)(2,1)S(1)}, b...) custom-call(s32[4]{0:T(128)S(1)} %pad_add_fusion.facts, ...), custom_call_target="tpu_custom_call" | custom-call | flops 1073741824 | bytes 16777216 | tf_op jit(solution)/shard_map/pallas_call | solution.py:22
  72.9 1.5 collective-permute-start.10
  74.4 5.8 %collective-permute-done.8.refs_3_ = bf16[512,128]{1,0:T(8,128)(2,1)S(1)} collective-permute-done((bf16[512,128]{1,0:T(8,128)(2,1)S(1)}, bf16[512,128]{1,0:T(8,128)(2,1)S(1)}, u32[]{:S(2)}, u32[]{:S(2)}) %collective-permute-start.8) | collective-permute-done | bytes 131104 | tf_op jit(solution)/shard_map/ppermute | solution.py:65
  82.1 16.8 %all_to_all.32.columns = bf16[16,64,128]{2,1,0:T(8,128)(2,1)S(1)} all-to-all(bf16[16,64,128]{2,1,0:T(8,128)(2,1)S(1)} %get-tuple-element.55), channel_id=1, replica_groups=mesh['sx'=16,'sy'=16] {'sx'}, dimensions={0} | all-to-all | bytes 524288 | tf_op jit(solution)/shard_map/all_to_all | solution.py:217
  99.0 1.2 shard_map.52
  100.2 13.9 %all_to_all.33.parts = bf16[16,64,128]{2,1,0:T(8,128)(2,1)S(1)} all-to-all(bf16[16,64,128]{2,1,0:T(8,128)(2,1)S(1)} %shard_map.52), channel_id=1, replica_groups=mesh['sx'=16,'sy'=16] {'sy'}, dimensions={0} | all-to-all | bytes 524288 | tf_op jit(solution)/shard_map/all_to_all | solution.py:221
  115.0 3.0 %collective-permute-start.13 = (bf16[64,128]{1,0:T(8,128)(2,1)S(1)}, bf16[64,128]{1,0:T(8,128)(2,1)S(1)}, u32[]{:S(2)}, u32[]{:S(2)}) collective-permute-start(bf16[64,128]{1,0:T(8,128)(2,1)S(1)} %shard_map.53.own), channel_id=1, source_target_pairs={{16,32},{48,64},{80,96},{112,128},{144,160},{176,192},{208,224},{2... | collective-permute-start | bytes 49160 | tf_op jit(solution)/shard_map/ppermute | solution.py:65
  119.7 5.1 %collective-permute-done.12.refs_4_ = bf16[64,128]{1,0:T(8,128)(2,1)S(1)} collective-permute-done((bf16[64,128]{1,0:T(8,128)(2,1)S(1)}, bf16[64,128]{1,0:T(8,128)(2,1)S(1)}, u32[]{:S(2)}, u32[]{:S(2)}) %collective-permute-start.12) | collective-permute-done | bytes 16416 | tf_op jit(solution)/shard_map/ppermute | solution.py:65
  124.7 3.3 %shard_map.54 = (f32[2048,128]{1,0:T(8,128)S(1)}, f32[2048,128]{1,0:T(8,128)S(1)}, bf16[512,128]{1,0:T(8,128)(2,1)S(1)}, bf16[512,128]{1,0:T(8,128)(2,1)S(1)}, b...) custom-call(s32[4]{0:T(128)S(1)} %pad_add_fusion.facts, f32[2048,128]{1,0:T(8,128)S(1)} %get-tuple-element.54.stepped, ...), custom_call_target="tpu_custom_call" | custom-call | flops 1073741824 | bytes 16777216 | tf_op jit(solution)/shard_map/pallas_call | solution.py:22
  128.4 1.9 %collective-permute-start.18 = (bf16[512,128]{1,0:T(8,128)(2,1)S(1)}, bf16[512,128]{1,0:T(8,128)(2,1)S(1)}, u32[]{:S(2)}, u32[]{:S(2)}) collective-permute-start(bf16[512,128]{1,0:T(8,128)(2,1)S(1)} %get-tuple-element.61), channel_id=1, source_target_pairs={{0,16},{32,48},{64,80},{96,112},{128,144},{160,176},{192,208},{224... | collective-permute-start | bytes 393224 | tf_op jit(solution)/shard_map/ppermute | solution.py:65
  130.3 5.8 %collective-permute-done.16.refs_3_ = bf16[512,128]{1,0:T(8,128)(2,1)S(1)} collective-permute-done((bf16[512,128]{1,0:T(8,128)(2,1)S(1)}, bf16[512,128]{1,0:T(8,128)(2,1)S(1)}, u32[]{:S(2)}, u32[]{:S(2)}) %collective-permute-start.16) | collective-permute-done | bytes 131104 | tf_op jit(solution)/shard_map/ppermute | solution.py:65
  137.0 16.4 %all_to_all.34.columns = bf16[16,64,128]{2,1,0:T(8,128)(2,1)S(1)} all-to-all(bf16[16,64,128]{2,1,0:T(8,128)(2,1)S(1)} %get-tuple-element.64), channel_id=1, replica_groups=mesh['sx'=16,'sy'=16] {'sx'}, dimensions={0} | all-to-all | bytes 524288 | tf_op jit(solution)/shard_map/all_to_all | solution.py:217
  153.4 1.2 shard_map.56
  154.6 14.1 %all_to_all.35.parts = bf16[16,64,128]{2,1,0:T(8,128)(2,1)S(1)} all-to-all(bf16[16,64,128]{2,1,0:T(8,128)(2,1)S(1)} %shard_map.56), channel_id=1, replica_groups=mesh['sx'=16,'sy'=16] {'sy'}, dimensions={0} | all-to-all | bytes 524288 | tf_op jit(solution)/shard_map/all_to_all | solution.py:221
  169.5 3.1 %collective-permute-start.21 = (bf16[64,128]{1,0:T(8,128)(2,1)S(1)}, bf16[64,128]{1,0:T(8,128)(2,1)S(1)}, u32[]{:S(2)}, u32[]{:S(2)}) collective-permute-start(bf16[64,128]{1,0:T(8,128)(2,1)S(1)} %shard_map.57.own), channel_id=1, source_target_pairs={{16,32},{48,64},{80,96},{112,128},{144,160},{176,192},{208,224},{2... | collective-permute-start | bytes 49160 | tf_op jit(solution)/shard_map/ppermute | solution.py:65
  173.3 1.1 collective-permute-done.21.refs_5_
  174.3 5.1 %collective-permute-done.20.refs_4_ = bf16[64,128]{1,0:T(8,128)(2,1)S(1)} collective-permute-done((bf16[64,128]{1,0:T(8,128)(2,1)S(1)}, bf16[64,128]{1,0:T(8,128)(2,1)S(1)}, u32[]{:S(2)}, u32[]{:S(2)}) %collective-permute-start.20) | collective-permute-done | bytes 16416 | tf_op jit(solution)/shard_map/ppermute | solution.py:65
  179.4 1.9 %shard_map.58 = f32[2048,128]{1,0:T(8,128)} custom-call(s32[4]{0:T(128)S(1)} %pad_add_fusion.facts, f32[2048,128]{1,0:T(8,128)S(1)} %get-tuple-element.63.stepped, bf16[64,2048]{1,0:T(8,128)(2,1)S(1)} %get-tuple-element.36.refs_1_.basis, bf16[64,128]{1,0:T(8,128)(2,1)S(1)} %shard_map.57.own, bf16[320,128]{1,0:T(8,128)(2,1)S(1)} %collective-permute-done.4.refs_0_.refs_4_, ...), custom_call_target="tpu_custom_call" | custom-call | bytes 2097152 | tf_op jit(solution)/shard_map/pallas_call | solution.py:22
  (44 shorter events, 13.2 us)
Async XLA Ops:
  0.0 64.9 %copy-start = (bf16[1,1,2048,2048]{3,2,1,0:T(8,128)(2,1)S(1)}, bf16[1,1,2048,2048]{3,2,1,0:T(8,128)(2,1)}, u32[]{:S(2)}) copy-start(bf16[1,1,2048,2048]{3,2,1,0:T(8,128)(2,1)} %param.4) | copy-start | bytes 25165828
  0.1 1.7 copy-start.1
  1.8 1.5 copy-start.2
  3.3 1.0 copy-start.3
  5.2 8.5 %collective-permute-start = (bf16[512,128]{1,0:T(8,128)(2,1)S(1)}, bf16[512,128]{1,0:T(8,128)(2,1)S(1)}, u32[]{:S(2)}, u32[]{:S(2)}) collective-permute-start(bf16[512,128]{1,0:T(8,128)(2,1)S(1)} %get-tuple-element.37), channel_id=1, source_target_pairs={{1,2},{3,4},{5,6},{7,8},{9,10},{11,12},{13,14},{15,0},{2,1},{4,3},... | collective-permute-start | bytes 393224 | tf_op jit(solution)/shard_map/ppermute | solution.py:65
  10.1 6.0 %collective-permute-start.1 = (bf16[512,128]{1,0:T(8,128)(2,1)S(1)}, bf16[512,128]{1,0:T(8,128)(2,1)S(1)}, u32[]{:S(2)}, u32[]{:S(2)}) collective-permute-start(bf16[512,128]{1,0:T(8,128)(2,1)S(1)} %get-tuple-element.38), channel_id=1, source_target_pairs={{16,32},{48,64},{80,96},{112,128},{144,160},{176,192},{208,224},{2... | collective-permute-start | bytes 393224 | tf_op jit(solution)/shard_map/ppermute | solution.py:65
  10.3 8.2 %collective-permute-start.2 = (bf16[512,128]{1,0:T(8,128)(2,1)S(1)}, bf16[512,128]{1,0:T(8,128)(2,1)S(1)}, u32[]{:S(2)}, u32[]{:S(2)}) collective-permute-start(bf16[512,128]{1,0:T(8,128)(2,1)S(1)} %get-tuple-element.39), channel_id=1, source_target_pairs={{0,16},{32,48},{64,80},{96,112},{128,144},{160,176},{192,208},{224... | collective-permute-start | bytes 393224 | tf_op jit(solution)/shard_map/ppermute | solution.py:65
  13.5 5.1 %collective-permute-start.3 = (bf16[512,128]{1,0:T(8,128)(2,1)S(1)}, bf16[512,128]{1,0:T(8,128)(2,1)S(1)}, u32[]{:S(2)}, u32[]{:S(2)}) collective-permute-start(bf16[512,128]{1,0:T(8,128)(2,1)S(1)} %get-tuple-element.40), channel_id=1, source_target_pairs={{0,1},{2,3},{4,5},{6,7},{8,9},{10,11},{12,13},{14,15},{1,0},{3,2},... | collective-permute-start | bytes 393224 | tf_op jit(solution)/shard_map/ppermute | solution.py:65
  54.8 5.5 %collective-permute-start.5 = (bf16[320,128]{1,0:T(8,128)(2,1)S(1)}, bf16[320,128]{1,0:T(8,128)(2,1)S(1)}, u32[]{:S(2)}, u32[]{:S(2)}) collective-permute-start(bf16[320,128]{1,0:T(8,128)(2,1)S(1)} %get-tuple-element.45), channel_id=1, source_target_pairs={{16,32},{48,64},{80,96},{112,128},{144,160},{176,192},{208,224},{2... | collective-permute-start | bytes 245768 | tf_op jit(solution)/shard_map/ppermute | solution.py:65
  55.9 7.1 %collective-permute-start.6 = (bf16[320,128]{1,0:T(8,128)(2,1)S(1)}, bf16[320,128]{1,0:T(8,128)(2,1)S(1)}, u32[]{:S(2)}, u32[]{:S(2)}) collective-permute-start(bf16[320,128]{1,0:T(8,128)(2,1)S(1)} %get-tuple-element.46), channel_id=1, source_target_pairs={{0,16},{32,48},{64,80},{96,112},{128,144},{160,176},{192,208},{224... | collective-permute-start | bytes 245768 | tf_op jit(solution)/shard_map/ppermute | solution.py:65
  57.4 5.5 %collective-permute-start.7 = (bf16[320,128]{1,0:T(8,128)(2,1)S(1)}, bf16[320,128]{1,0:T(8,128)(2,1)S(1)}, u32[]{:S(2)}, u32[]{:S(2)}) collective-permute-start(bf16[320,128]{1,0:T(8,128)(2,1)S(1)} %get-tuple-element.47), channel_id=1, source_target_pairs={{0,1},{2,3},{4,5},{6,7},{8,9},{10,11},{12,13},{14,15},{1,0},{3,2},... | collective-permute-start | bytes 245768 | tf_op jit(solution)/shard_map/ppermute | solution.py:65
  57.4 7.5 %collective-permute-start.4 = (bf16[320,128]{1,0:T(8,128)(2,1)S(1)}, bf16[320,128]{1,0:T(8,128)(2,1)S(1)}, u32[]{:S(2)}, u32[]{:S(2)}) collective-permute-start(bf16[320,128]{1,0:T(8,128)(2,1)S(1)} %get-tuple-element.44.own), channel_id=1, source_target_pairs={{1,2},{3,4},{5,6},{7,8},{9,10},{11,12},{13,14},{15,0},{2,1},{4,3},... | collective-permute-start | bytes 245768 | tf_op jit(solution)/shard_map/ppermute | solution.py:65
  71.4 8.9 %collective-permute-start.8 = (bf16[512,128]{1,0:T(8,128)(2,1)S(1)}, bf16[512,128]{1,0:T(8,128)(2,1)S(1)}, u32[]{:S(2)}, u32[]{:S(2)}) collective-permute-start(bf16[512,128]{1,0:T(8,128)(2,1)S(1)} %get-tuple-element.50), channel_id=1, source_target_pairs={{1,2},{3,4},{5,6},{7,8},{9,10},{11,12},{13,14},{15,0},{2,1},{4,3},... | collective-permute-start | bytes 393224 | tf_op jit(solution)/shard_map/ppermute | solution.py:65
  72.1 8.1 %collective-permute-start.9 = (bf16[512,128]{1,0:T(8,128)(2,1)S(1)}, bf16[512,128]{1,0:T(8,128)(2,1)S(1)}, u32[]{:S(2)}, u32[]{:S(2)}) collective-permute-start(bf16[512,128]{1,0:T(8,128)(2,1)S(1)} %get-tuple-element.51), channel_id=1, source_target_pairs={{16,32},{48,64},{80,96},{112,128},{144,160},{176,192},{208,224},{2... | collective-permute-start | bytes 393224 | tf_op jit(solution)/shard_map/ppermute | solution.py:65
  72.9 8.3 %collective-permute-start.10 = (bf16[512,128]{1,0:T(8,128)(2,1)S(1)}, bf16[512,128]{1,0:T(8,128)(2,1)S(1)}, u32[]{:S(2)}, u32[]{:S(2)}) collective-permute-start(bf16[512,128]{1,0:T(8,128)(2,1)S(1)} %get-tuple-element.52), channel_id=1, source_target_pairs={{0,16},{32,48},{64,80},{96,112},{128,144},{160,176},{192,208},{224... | collective-permute-start | bytes 393224 | tf_op jit(solution)/shard_map/ppermute | solution.py:65
  74.4 6.8 %collective-permute-start.11 = (bf16[512,128]{1,0:T(8,128)(2,1)S(1)}, bf16[512,128]{1,0:T(8,128)(2,1)S(1)}, u32[]{:S(2)}, u32[]{:S(2)}) collective-permute-start(bf16[512,128]{1,0:T(8,128)(2,1)S(1)} %get-tuple-element.53), channel_id=1, source_target_pairs={{0,1},{2,3},{4,5},{6,7},{8,9},{10,11},{12,13},{14,15},{1,0},{3,2},... | collective-permute-start | bytes 393224 | tf_op jit(solution)/shard_map/ppermute | solution.py:65
  114.7 3.5 %collective-permute-start.15 = (bf16[64,128]{1,0:T(8,128)(2,1)S(1)}, bf16[64,128]{1,0:T(8,128)(2,1)S(1)}, u32[]{:S(2)}, u32[]{:S(2)}) collective-permute-start(bf16[64,128]{1,0:T(8,128)(2,1)S(1)} %shard_map.53.own), channel_id=1, source_target_pairs={{0,1},{2,3},{4,5},{6,7},{8,9},{10,11},{12,13},{14,15},{1,0},{3,2},... | collective-permute-start | bytes 49160 | tf_op jit(solution)/shard_map/ppermute | solution.py:65
  114.9 3.7 %collective-permute-start.14 = (bf16[64,128]{1,0:T(8,128)(2,1)S(1)}, bf16[64,128]{1,0:T(8,128)(2,1)S(1)}, u32[]{:S(2)}, u32[]{:S(2)}) collective-permute-start(bf16[64,128]{1,0:T(8,128)(2,1)S(1)} %shard_map.53.own), channel_id=1, source_target_pairs={{0,16},{32,48},{64,80},{96,112},{128,144},{160,176},{192,208},{224... | collective-permute-start | bytes 49160 | tf_op jit(solution)/shard_map/ppermute | solution.py:65
  115.0 4.7 %collective-permute-start.13 = (bf16[64,128]{1,0:T(8,128)(2,1)S(1)}, bf16[64,128]{1,0:T(8,128)(2,1)S(1)}, u32[]{:S(2)}, u32[]{:S(2)}) collective-permute-start(bf16[64,128]{1,0:T(8,128)(2,1)S(1)} %shard_map.53.own), channel_id=1, source_target_pairs={{16,32},{48,64},{80,96},{112,128},{144,160},{176,192},{208,224},{2... | collective-permute-start | bytes 49160 | tf_op jit(solution)/shard_map/ppermute | solution.py:65
  117.9 6.8 %collective-permute-start.12 = (bf16[64,128]{1,0:T(8,128)(2,1)S(1)}, bf16[64,128]{1,0:T(8,128)(2,1)S(1)}, u32[]{:S(2)}, u32[]{:S(2)}) collective-permute-start(bf16[64,128]{1,0:T(8,128)(2,1)S(1)} %shard_map.53.own), channel_id=1, source_target_pairs={{1,2},{3,4},{5,6},{7,8},{9,10},{11,12},{13,14},{15,0},{2,1},{4,3},... | collective-permute-start | bytes 49160 | tf_op jit(solution)/shard_map/ppermute | solution.py:65
  128.0 8.1 %collective-permute-start.16 = (bf16[512,128]{1,0:T(8,128)(2,1)S(1)}, bf16[512,128]{1,0:T(8,128)(2,1)S(1)}, u32[]{:S(2)}, u32[]{:S(2)}) collective-permute-start(bf16[512,128]{1,0:T(8,128)(2,1)S(1)} %get-tuple-element.59), channel_id=1, source_target_pairs={{1,2},{3,4},{5,6},{7,8},{9,10},{11,12},{13,14},{15,0},{2,1},{4,3},... | collective-permute-start | bytes 393224 | tf_op jit(solution)/shard_map/ppermute | solution.py:65
  128.4 7.7 %collective-permute-start.17 = (bf16[512,128]{1,0:T(8,128)(2,1)S(1)}, bf16[512,128]{1,0:T(8,128)(2,1)S(1)}, u32[]{:S(2)}, u32[]{:S(2)}) collective-permute-start(bf16[512,128]{1,0:T(8,128)(2,1)S(1)} %get-tuple-element.60), channel_id=1, source_target_pairs={{16,32},{48,64},{80,96},{112,128},{144,160},{176,192},{208,224},{2... | collective-permute-start | bytes 393224 | tf_op jit(solution)/shard_map/ppermute | solution.py:65
  128.4 7.7 %collective-permute-start.18 = (bf16[512,128]{1,0:T(8,128)(2,1)S(1)}, bf16[512,128]{1,0:T(8,128)(2,1)S(1)}, u32[]{:S(2)}, u32[]{:S(2)}) collective-permute-start(bf16[512,128]{1,0:T(8,128)(2,1)S(1)} %get-tuple-element.61), channel_id=1, source_target_pairs={{0,16},{32,48},{64,80},{96,112},{128,144},{160,176},{192,208},{224... | collective-permute-start | bytes 393224 | tf_op jit(solution)/shard_map/ppermute | solution.py:65
  130.3 5.8 %collective-permute-start.19 = (bf16[512,128]{1,0:T(8,128)(2,1)S(1)}, bf16[512,128]{1,0:T(8,128)(2,1)S(1)}, u32[]{:S(2)}, u32[]{:S(2)}) collective-permute-start(bf16[512,128]{1,0:T(8,128)(2,1)S(1)} %get-tuple-element.62), channel_id=1, source_target_pairs={{0,1},{2,3},{4,5},{6,7},{8,9},{10,11},{12,13},{14,15},{1,0},{3,2},... | collective-permute-start | bytes 393224 | tf_op jit(solution)/shard_map/ppermute | solution.py:65
  169.3 3.6 %collective-permute-start.23 = (bf16[64,128]{1,0:T(8,128)(2,1)S(1)}, bf16[64,128]{1,0:T(8,128)(2,1)S(1)}, u32[]{:S(2)}, u32[]{:S(2)}) collective-permute-start(bf16[64,128]{1,0:T(8,128)(2,1)S(1)} %shard_map.57.own), channel_id=1, source_target_pairs={{0,1},{2,3},{4,5},{6,7},{8,9},{10,11},{12,13},{14,15},{1,0},{3,2},... | collective-permute-start | bytes 49160 | tf_op jit(solution)/shard_map/ppermute | solution.py:65
  169.5 3.7 %collective-permute-start.22 = (bf16[64,128]{1,0:T(8,128)(2,1)S(1)}, bf16[64,128]{1,0:T(8,128)(2,1)S(1)}, u32[]{:S(2)}, u32[]{:S(2)}) collective-permute-start(bf16[64,128]{1,0:T(8,128)(2,1)S(1)} %shard_map.57.own), channel_id=1, source_target_pairs={{0,16},{32,48},{64,80},{96,112},{128,144},{160,176},{192,208},{224... | collective-permute-start | bytes 49160 | tf_op jit(solution)/shard_map/ppermute | solution.py:65
  169.5 4.8 %collective-permute-start.21 = (bf16[64,128]{1,0:T(8,128)(2,1)S(1)}, bf16[64,128]{1,0:T(8,128)(2,1)S(1)}, u32[]{:S(2)}, u32[]{:S(2)}) collective-permute-start(bf16[64,128]{1,0:T(8,128)(2,1)S(1)} %shard_map.57.own), channel_id=1, source_target_pairs={{16,32},{48,64},{80,96},{112,128},{144,160},{176,192},{208,224},{2... | collective-permute-start | bytes 49160 | tf_op jit(solution)/shard_map/ppermute | solution.py:65
  172.6 6.8 %collective-permute-start.20 = (bf16[64,128]{1,0:T(8,128)(2,1)S(1)}, bf16[64,128]{1,0:T(8,128)(2,1)S(1)}, u32[]{:S(2)}, u32[]{:S(2)}) collective-permute-start(bf16[64,128]{1,0:T(8,128)(2,1)S(1)} %shard_map.57.own), channel_id=1, source_target_pairs={{1,2},{3,4},{5,6},{7,8},{9,10},{11,12},{13,14},{15,0},{2,1},{4,3},... | collective-permute-start | bytes 49160 | tf_op jit(solution)/shard_map/ppermute | solution.py:65

commit v3 on v2

v3 whole, which is shorter than its diff:
```python
import functools

import jax
import jax.numpy as jnp
from jax import lax
from jax.experimental import pallas as pl
from jax.experimental.pallas import tpu as pltpu
from jax.sharding import PartitionSpec as P


ITERS = 3
DAMPING = 0.5

VMEM = pl.BlockSpec(memory_space=pltpu.VMEM)
SMEM = pl.BlockSpec(memory_space=pltpu.SMEM)
HBM = pl.BlockSpec(memory_space=pltpu.HBM)
BF16 = jnp.bfloat16
F32 = jnp.float32


def kernel_call(body, outs, scratch=(), flops=0, moved=0, limit=16 << 20, outside=(), out_space=VMEM):
    return lambda *operands: pl.pallas_call(
        body,
        out_shape=tuple(outs),
        in_specs=[SMEM] + [HBM if i in outside else VMEM for i in range(1, len(operands))],
        out_specs=tuple([out_space] * len(outs)),
        scratch_shapes=list(scratch),
        compiler_params=pltpu.CompilerParams(vmem_limit_bytes=limit),
        cost_estimate=pl.CostEstimate(flops=flops, bytes_accessed=moved, transcendentals=0),
    )(*operands)


def place_facts():
    places = [(lax.axis_index(axis), lax.axis_size(axis)) for axis in ("sx", "sy")]
    odd = [lax.rem(place, 2) for place, count in places]
    ends = [((place == 0) | (place == count - 1)).astype(jnp.int32) for place, count in places]
    return jnp.stack(odd + ends)


EXCHANGES = ((1, True), (0, True), (0, False), (1, False))


def face_starts(facts, width):
    starts = []
    for axis, far in EXCHANGES:
        odd = facts[axis]
        starts.append(pl.multiple_of((2 * axis + (odd if far else 1 - odd)) * width, width))
    return starts


def from_neighbours(facts, received):
    arrays = []
    for (axis, far), array in zip(EXCHANGES, received):
        arrays.append(jnp.where(facts[2 + axis] == 1, jnp.zeros_like(array), array) if far else array)
    return arrays


def exchange(parts):
    received = []
    for (axis, far), part in zip(EXCHANGES, parts):
        name = ("sx", "sy")[axis]
        count = lax.axis_size(name)
        lower = range(1 if far else 0, count, 2)
        pairs = [(i, (i + 1) % count) for i in lower] + [((i + 1) % count, i) for i in lower]
        received.append(lax.ppermute(part, name, pairs))
    return received


def faces_body(facts, loads, tile, operator, *refs):
    del tile, operator
    faces, (right, arrived) = refs[:4], refs[4:]
    width = loads.shape[0] // 4
    blocks = [pl.ds(start, width) for start in face_starts(facts, width)]
    copies = [
        pltpu.make_async_copy(loads.at[block, :], right.at[block, :], arrived.at[index])
        for index, block in enumerate(blocks)
    ]
    for copy in copies:
        copy.start()
    for copy, block, face in zip(copies, blocks, faces):
        copy.wait()
        face[...] = right[block, :].astype(BF16)


def restrict_body(first, facts, basis, *refs):
    if first:
        (values,), refs = refs[:1], refs[1:]
    else:
        values, held, refs = refs[:4], refs[4], refs[5:]
    received, (stepped, coarse) = refs[:4], refs[4:]
    width = stepped.shape[0] // 4
    total = jnp.zeros(coarse.shape[1:], F32)
    sides = from_neighbours(facts, [part[...].astype(F32) for part in received])
    for index, (start, side) in enumerate(zip(face_starts(facts, width), sides)):
        rows = pl.ds(start, width)
        residual = (values[rows, :] if first else values[index][...]) - side
        half = DAMPING * residual
        stepped[rows, :] = half if first else held[rows, :] + half
        total += jnp.dot(basis[:, rows], residual.astype(BF16), preferred_element_type=F32)
    coarse[...] = jnp.broadcast_to(total.astype(BF16)[None], coarse.shape)


def tile_body(facts, tile, columns, *others):
    partial = others[-1]
    count, rows, loads = partial.shape
    whole = columns[...].reshape(tile.shape[1], loads)
    product = jnp.dot(tile[...], whole, preferred_element_type=F32)
    partial[...] = product.astype(BF16).reshape(count, rows, loads)


def sum_body(facts, parts, total):
    total[...] = jnp.sum(parts[...].astype(F32), axis=0).astype(BF16)


def sum_with_basis_body(facts, parts, basis, *messages):
    total = jnp.sum(parts[...].astype(F32), axis=0).astype(BF16)
    rows, loads = total.shape
    width = basis.shape[1] // 4
    for start, message in zip(face_starts(facts, width), messages):
        message[:rows, :] = total
        for piece in range(width // loads):
            columns = pl.ds(pl.multiple_of(start + piece * loads, loads), loads)
            message[(piece + 1) * rows : (piece + 2) * rows, :] = basis[:, columns]


def corrected(stepped, basis, own, slices, theirs, start, width):
    rows, loads = own.shape
    near = basis[:, pl.ds(start, width)]
    far = jnp.concatenate(
        [slices[(i + 1) * rows : (i + 2) * rows, :] for i in range(width // loads)], axis=1
    )
    weights = jnp.concatenate([near, far], axis=0)
    columns = jnp.concatenate([own, -theirs], axis=0)
    back = lax.dot_general(
        weights, columns, (((0,), (0,)), ((), ())), preferred_element_type=F32
    )
    return stepped[pl.ds(start, width), :] - DAMPING * back


def multiplied(facts, which, operator, right, rounded, values, faces):
    width = operator.shape[0] // 4
    for start, value, face in zip(face_starts(facts, width)[which], values, faces):
        block = pl.ds(start, width)
        product = jnp.dot(operator[block, :], rounded[...], preferred_element_type=F32)
        difference = right[block, :] - product
        value[...] = difference
        face[...] = difference.astype(BF16)


def advance_body(facts, stepped, basis, own, operator, right, *refs):
    slices, theirs = refs[:4], refs[4:8]
    held, rounded = refs[8:10]
    values, faces = refs[10:12], refs[12:14]
    width = held.shape[0] // 4
    rows = basis.shape[0]
    starts = face_starts(facts, width)
    corrections = from_neighbours(facts, [part[:rows, :] for part in theirs])
    for start, kept, other in zip(starts, slices, corrections):
        part = corrected(stepped, basis, own[:rows, :], kept, other, start, width)
        held[pl.ds(start, width), :] = part
        rounded[pl.ds(start, width), :] = part.astype(BF16)
    multiplied(facts, slice(0, 2), operator, right, rounded, values, faces)


def advance_near_body(facts, operator, right, rounded, *refs):
    multiplied(facts, slice(2, 4), operator, right, rounded, refs[:2], refs[2:])


def finish_body(facts, stepped, basis, own, *refs):
    slices, theirs, (out, block, leaving) = refs[:4], refs[4:8], refs[8:]
    width = out.shape[0] // 4
    rows = basis.shape[0]
    others = from_neighbours(facts, [part[:rows, :] for part in theirs])
    copies = []
    for index, (start, kept, other) in enumerate(
        zip(face_starts(facts, width), slices, others)
    ):
        block[index] = corrected(stepped, basis, own[:rows, :], kept, other, start, width)
        copies.append(
            pltpu.make_async_copy(
                block.at[index], out.at[pl.ds(start, width), :], leaving.at[index]
            )
        )
        copies[-1].start()
    for copy in copies:
        copy.wait()


def local(dual_ops, loads, kernel_basis, coarse_inverse):
    operator, right, basis, tile = dual_ops[0, 0], loads[0, 0], kernel_basis[0, 0], coarse_inverse[0, 0]
    size, columns = right.shape
    width = size // 4
    rows = basis.shape[0]
    whole = jax.ShapeDtypeStruct(right.shape, F32)
    face = jax.ShapeDtypeStruct((width, columns), BF16)
    blocks_x = jax.ShapeDtypeStruct((lax.axis_size("sx"), rows, columns), BF16)
    blocks_y = jax.ShapeDtypeStruct((lax.axis_size("sy"), rows, columns), BF16)
    coarse = jax.ShapeDtypeStruct((rows, columns), BF16)
    message = jax.ShapeDtypeStruct((rows + width * rows // columns, columns), BF16)

    facts = place_facts()
    *faces, right = kernel_call(
        faces_body,
        [face] * 4 + [whole],
        [pltpu.SemaphoreType.DMA((4,))],
        moved=3 << 20,
        limit=52 << 20,
        outside=(1, 2, 3),
    )(facts, right, tile, operator)
    for step in range(ITERS):
        received = exchange(faces)
        first = step == 0
        stepped, sent = kernel_call(
            functools.partial(restrict_body, first),
            [whole, blocks_x],
            flops=2 * rows * size * columns,
            moved=4 << 20,
        )(facts, basis, *([right] if first else [*values, held]), *received)
        gathered = lax.all_to_all(sent, "sx", 0, 0, tiled=True)
        (partial,) = kernel_call(
            tile_body,
            [blocks_y],
            flops=2 * tile.size * columns,
            moved=3 << 20,
            outside=(3,) if first else (),
        )(facts, tile, gathered, *([operator] if first else []))
        parts = lax.all_to_all(partial, "sy", 0, 0, tiled=True)
        if first:
            messages = kernel_call(sum_with_basis_body, [message] * 4, moved=1 << 20)(
                facts, parts, basis
            )
            own = messages[0]
            theirs = exchange(messages)
            slices = theirs
        else:
            (own,) = kernel_call(sum_body, [coarse], moved=1 << 18)(facts, parts)
            theirs = exchange([own] * 4)
        if step < ITERS - 1:
            part = jax.ShapeDtypeStruct((width, columns), F32)
            held, rounded, *others = kernel_call(
                advance_body,
                [whole, jax.ShapeDtypeStruct(whole.shape, BF16)] + [part] * 2 + [face] * 2,
                flops=operator.size * columns,
                moved=12 << 20,
            )(facts, stepped, basis, own, operator, right, *slices, *theirs)
            more = kernel_call(
                advance_near_body,
                [part] * 2 + [face] * 2,
                flops=operator.size * columns,
                moved=8 << 20,
            )(facts, operator, right, rounded)
            values, faces = [*others[:2], *more[:2]], [*others[2:], *more[2:]]
        else:
            (out,) = kernel_call(
                finish_body,
                [whole],
                [pltpu.VMEM((4, width, columns), F32), pltpu.SemaphoreType.DMA((4,))],
                moved=2 << 20,
                out_space=HBM,
            )(facts, stepped, basis, own, *slices, *theirs)
    return out[None, None]


def solution(mesh):
    placed = P("sx", "sy", None, None)
    return jax.shard_map(
        local, mesh=mesh, in_specs=(placed,) * 4, out_specs=placed, check_vma=False
    )
```

time: 182 us -> 175 us (0.962)
  local copies, waits for them, and re-layouts: 4.2 us -> 0.01 us
    unnamed x8 -> x6, local copies, waits for them, and re-layouts: 4.2 us -> 0.01 us
    all_to_all x3, blocking collectives: 41.8 us -> 39.4 us  [local(): parts = lax.all_to_all(partial, 'sy', 0, 0, tiled=True)]
    pallas_call x13 -> x15, Pallas kernels: 20.6 us -> 19.9 us  [kernel_call(): pl.pallas_call(body, out_shape=tuple(outs), in_specs=[SMEM] + [HBM if i i...]
  transfers between devices with their start and end apart: 24 -> 24, of which waited for: 15 -> 15; matrix products, arithmetic and copies ran while one was open for 0% -> 0% of each run, Pallas kernels for 0% -> 1%
where the time goes in v3:
time: 175 us
  blocking collectives  93.3 us (53%)
  waiting for transfers between devices  37.6 us (21%)
  starting transfers between devices  24 us (14%)
  Pallas kernels  19.9 us (11%)
    all_to_all x3, blocking collectives, local(): gathered = lax.all_to_all(sent, 'sx', 0, 0, tiled=True)  53.9 us
    all_to_all x3, blocking collectives, local(): parts = lax.all_to_all(partial, 'sy', 0, 0, tiled=True)  39.4 us
    ppermute x24, waiting for transfers between devices, exchange(): received.append(lax.ppermute(part, name, pairs))  37.6 us
    ppermute x24, starting transfers between devices, exchange(): received.append(lax.ppermute(part, name, pairs))  24 us
    pallas_call x15, Pallas kernels, kernel_call(): pl.pallas_call(body, out_shape=tuple(outs), in_specs=[SMEM] + [HBM if i i...  19.9 us
  transfers between devices with their start and end apart: 24, of which 15 were waited for; matrix products, arithmetic and copies ran while one was open for 0% of the time, Pallas kernels for 1%

profile of v3, /device:TPU:32, one launch (start us, length us, event | category | flops | bytes accessed | tf_op | source)
XLA Modules:
  0.0 175.2 jit_solution(307196238741871805)
XLA Ops:
  0.1 2.1 %shard_map.46 = (bf16[512,128]{1,0:T(8,128)(2,1)S(1)}, bf16[512,128]{1,0:T(8,128)(2,1)S(1)}, bf16[512,128]{1,0:T(8,128)(2,1)S(1)}, bf16[512,128]{1,0:T(8,128)(2,1)S(1)}, f32[2048,128]{1,0:T(8,128)S(1)}) custom-call(s32[4]{0:T(128)S(1)} %pad_add_fusion.facts, f32[2048,128]{1,0:T(8,128)} %bitcast.26, bf16[1024,1024]{1,0:T(8,128)(2,1)} %bitcast.15, ...), custom_call_target="tpu_custom_call" | custom-call | bytes 3145728 | tf_op jit(solution)/shard_map/pallas_call | solution.py:22
  2.2 4.9 %collective-permute-start = (bf16[512,128]{1,0:T(8,128)(2,1)S(1)}, bf16[512,128]{1,0:T(8,128)(2,1)S(1)}, u32[]{:S(2)}, u32[]{:S(2)}) collective-permute-start(bf16[512,128]{1,0:T(8,128)(2,1)S(1)} %get-tuple-element.41), channel_id=1, source_target_pairs={{1,2},{3,4},{5,6},{7,8},{9,10},{11,12},{13,14},{15,0},{2,1},{4,3},... | collective-permute-start | bytes 393224 | tf_op jit(solution)/shard_map/ppermute | solution.py:65
  7.3 3.2 %collective-permute-start.2 = (bf16[512,128]{1,0:T(8,128)(2,1)S(1)}, bf16[512,128]{1,0:T(8,128)(2,1)S(1)}, u32[]{:S(2)}, u32[]{:S(2)}) collective-permute-start(bf16[512,128]{1,0:T(8,128)(2,1)S(1)} %get-tuple-element.43), channel_id=1, source_target_pairs={{0,16},{32,48},{64,80},{96,112},{128,144},{160,176},{192,208},{224... | collective-permute-start | bytes 393224 | tf_op jit(solution)/shard_map/ppermute | solution.py:65
  10.7 2.4 %collective-permute-done.1.refs_2_ = bf16[512,128]{1,0:T(8,128)(2,1)S(1)} collective-permute-done((bf16[512,128]{1,0:T(8,128)(2,1)S(1)}, bf16[512,128]{1,0:T(8,128)(2,1)S(1)}, u32[]{:S(2)}, u32[]{:S(2)}) %collective-permute-start.1) | collective-permute-done | bytes 131104 | tf_op jit(solution)/shard_map/ppermute | solution.py:65
  13.1 2.5 %collective-permute-done.2.refs_3_ = bf16[512,128]{1,0:T(8,128)(2,1)S(1)} collective-permute-done((bf16[512,128]{1,0:T(8,128)(2,1)S(1)}, bf16[512,128]{1,0:T(8,128)(2,1)S(1)}, u32[]{:S(2)}, u32[]{:S(2)}) %collective-permute-start.2) | collective-permute-done | bytes 131104 | tf_op jit(solution)/shard_map/ppermute | solution.py:65
  16.4 19.8 %all_to_all.30.columns = bf16[16,64,128]{2,1,0:T(8,128)(2,1)S(1)} all-to-all(bf16[16,64,128]{2,1,0:T(8,128)(2,1)S(1)} %get-tuple-element.46), channel_id=1, replica_groups=mesh['sx'=16,'sy'=16] {'sx'}, dimensions={0} | all-to-all | bytes 524288 | tf_op jit(solution)/shard_map/all_to_all | solution.py:219
  36.2 1.2 shard_map.48
  37.4 13.7 %all_to_all.31.parts = bf16[16,64,128]{2,1,0:T(8,128)(2,1)S(1)} all-to-all(bf16[16,64,128]{2,1,0:T(8,128)(2,1)S(1)} %shard_map.48), channel_id=1, replica_groups=mesh['sx'=16,'sy'=16] {'sy'}, dimensions={0} | all-to-all | bytes 524288 | tf_op jit(solution)/shard_map/all_to_all | solution.py:227
  52.9 1.6 collective-permute-start.6
  55.1 2.2 %collective-permute-done.5.refs_1_.refs_5_ = bf16[320,128]{1,0:T(8,128)(2,1)S(1)} collective-permute-done((bf16[320,128]{1,0:T(8,128)(2,1)S(1)}, bf16[320,128]{1,0:T(8,128)(2,1)S(1)}, u32[]{:S(2)}, u32[]{:S(2)}) %collective-permute-start.5) | collective-permute-done | bytes 81952 | tf_op jit(solution)/shard_map/ppermute | solution.py:65
  57.3 2.6 %collective-permute-done.6.refs_2_.refs_6_ = bf16[320,128]{1,0:T(8,128)(2,1)S(1)} collective-permute-done((bf16[320,128]{1,0:T(8,128)(2,1)S(1)}, bf16[320,128]{1,0:T(8,128)(2,1)S(1)}, u32[]{:S(2)}, u32[]{:S(2)}) %collective-permute-start.6) | collective-permute-done | bytes 81952 | tf_op jit(solution)/shard_map/ppermute | solution.py:65
  60.0 1.9 %collective-permute-done.4.refs_0_.refs_4_ = bf16[320,128]{1,0:T(8,128)(2,1)S(1)} collective-permute-done((bf16[320,128]{1,0:T(8,128)(2,1)S(1)}, bf16[320,128]{1,0:T(8,128)(2,1)S(1)}, u32[]{:S(2)}, u32[]{:S(2)}) %collective-permute-start.4) | collective-permute-done | bytes 81952 | tf_op jit(solution)/shard_map/ppermute | solution.py:65
  61.9 2.2 %shard_map.50 = (f32[2048,128]{1,0:T(8,128)S(1)}, bf16[2048,128]{1,0:T(8,128)(2,1)S(1)}, f32[512,128]{1,0:T(8,128)S(1)}, f32[512,128]{1,0:T(8,128)S(1)}, bf16[51...) custom-call(s32[4]{0:T(128)S(1)} %pad_add_fusion.facts, f32[2048,128]{1,0:T(8,128)S(1)} %get-tuple-element.45.stepped, ...), custom_call_target="tpu_custom_call" | custom-call | flops 536870912 | bytes 12582912 | tf_op jit(solution)/shard_map/pallas_call | solution.py:22
  65.6 1.8 %shard_map.51 = (f32[512,128]{1,0:T(8,128)S(1)}, f32[512,128]{1,0:T(8,128)S(1)}, bf16[512,128]{1,0:T(8,128)(2,1)S(1)}, bf16[512,128]{1,0:T(8,128)(2,1)S(1)}) custom-call(s32[4]{0:T(128)S(1)} %pad_add_fusion.facts, bf16[2048,2048]{1,0:T(8,128)(2,1)S(1)} %bitcast.12, f32[2048,128]{1,0:T(8,128)S(1)} %get-tuple-element.40.refs_0_.right, ...), custom_call_target="tpu_custom_call" | custom-call | flops 536870912 | bytes 8388608 | tf_op jit(solution)/shard_map/pallas_call | solution.py:22
  67.4 1.6 collective-permute-start.10
  69.0 3.9 %collective-permute-done.8.refs_5_ = bf16[512,128]{1,0:T(8,128)(2,1)S(1)} collective-permute-done((bf16[512,128]{1,0:T(8,128)(2,1)S(1)}, bf16[512,128]{1,0:T(8,128)(2,1)S(1)}, u32[]{:S(2)}, u32[]{:S(2)}) %collective-permute-start.8) | collective-permute-done | bytes 131104 | tf_op jit(solution)/shard_map/ppermute | solution.py:65
  74.8 17.0 %all_to_all.32.columns = bf16[16,64,128]{2,1,0:T(8,128)(2,1)S(1)} all-to-all(bf16[16,64,128]{2,1,0:T(8,128)(2,1)S(1)} %get-tuple-element.62), channel_id=1, replica_groups=mesh['sx'=16,'sy'=16] {'sx'}, dimensions={0} | all-to-all | bytes 524288 | tf_op jit(solution)/shard_map/all_to_all | solution.py:219
  91.8 1.2 shard_map.53
  93.0 13.8 %all_to_all.33.parts = bf16[16,64,128]{2,1,0:T(8,128)(2,1)S(1)} all-to-all(bf16[16,64,128]{2,1,0:T(8,128)(2,1)S(1)} %shard_map.53), channel_id=1, replica_groups=mesh['sx'=16,'sy'=16] {'sy'}, dimensions={0} | all-to-all | bytes 524288 | tf_op jit(solution)/shard_map/all_to_all | solution.py:227
  107.7 3.0 %collective-permute-start.13 = (bf16[64,128]{1,0:T(8,128)(2,1)S(1)}, bf16[64,128]{1,0:T(8,128)(2,1)S(1)}, u32[]{:S(2)}, u32[]{:S(2)}) collective-permute-start(bf16[64,128]{1,0:T(8,128)(2,1)S(1)} %shard_map.54.own), channel_id=1, source_target_pairs={{16,32},{48,64},{80,96},{112,128},{144,160},{176,192},{208,224},{2... | collective-permute-start | bytes 49160 | tf_op jit(solution)/shard_map/ppermute | solution.py:65
  112.5 5.0 %collective-permute-done.12.refs_4_ = bf16[64,128]{1,0:T(8,128)(2,1)S(1)} collective-permute-done((bf16[64,128]{1,0:T(8,128)(2,1)S(1)}, bf16[64,128]{1,0:T(8,128)(2,1)S(1)}, u32[]{:S(2)}, u32[]{:S(2)}) %collective-permute-start.12) | collective-permute-done | bytes 16416 | tf_op jit(solution)/shard_map/ppermute | solution.py:65
  117.5 2.2 %shard_map.55 = (f32[2048,128]{1,0:T(8,128)S(1)}, bf16[2048,128]{1,0:T(8,128)(2,1)S(1)}, f32[512,128]{1,0:T(8,128)S(1)}, f32[512,128]{1,0:T(8,128)S(1)}, bf16[51...) custom-call(s32[4]{0:T(128)S(1)} %pad_add_fusion.facts, f32[2048,128]{1,0:T(8,128)S(1)} %get-tuple-element.61.stepped, ...), custom_call_target="tpu_custom_call" | custom-call | flops 536870912 | bytes 12582912 | tf_op jit(solution)/shard_map/pallas_call | solution.py:22
  119.6 1.8 %shard_map.56 = (f32[512,128]{1,0:T(8,128)S(1)}, f32[512,128]{1,0:T(8,128)S(1)}, bf16[512,128]{1,0:T(8,128)(2,1)S(1)}, bf16[512,128]{1,0:T(8,128)(2,1)S(1)}) custom-call(s32[4]{0:T(128)S(1)} %pad_add_fusion.facts, bf16[2048,2048]{1,0:T(8,128)(2,1)S(1)} %bitcast.14, f32[2048,128]{1,0:T(8,128)S(1)} %get-tuple-element.40.refs_0_.right, ...), custom_call_target="tpu_custom_call" | custom-call | flops 536870912 | bytes 8388608 | tf_op jit(solution)/shard_map/pallas_call | solution.py:22
  122.1 1.2 collective-permute-start.17
  123.3 7.9 %collective-permute-done.18.refs_7_ = bf16[512,128]{1,0:T(8,128)(2,1)S(1)} collective-permute-done((bf16[512,128]{1,0:T(8,128)(2,1)S(1)}, bf16[512,128]{1,0:T(8,128)(2,1)S(1)}, u32[]{:S(2)}, u32[]{:S(2)}) %collective-permute-start.18) | collective-permute-done | bytes 131104 | tf_op jit(solution)/shard_map/ppermute | solution.py:65
  132.1 17.2 %all_to_all.34.columns = bf16[16,64,128]{2,1,0:T(8,128)(2,1)S(1)} all-to-all(bf16[16,64,128]{2,1,0:T(8,128)(2,1)S(1)} %get-tuple-element.74), channel_id=1, replica_groups=mesh['sx'=16,'sy'=16] {'sx'}, dimensions={0} | all-to-all | bytes 524288 | tf_op jit(solution)/shard_map/all_to_all | solution.py:219
  149.3 1.2 shard_map.58
  150.5 11.9 %all_to_all.35.parts = bf16[16,64,128]{2,1,0:T(8,128)(2,1)S(1)} all-to-all(bf16[16,64,128]{2,1,0:T(8,128)(2,1)S(1)} %shard_map.58), channel_id=1, replica_groups=mesh['sx'=16,'sy'=16] {'sy'}, dimensions={0} | all-to-all | bytes 524288 | tf_op jit(solution)/shard_map/all_to_all | solution.py:227
  163.7 2.7 %collective-permute-start.21 = (bf16[64,128]{1,0:T(8,128)(2,1)S(1)}, bf16[64,128]{1,0:T(8,128)(2,1)S(1)}, u32[]{:S(2)}, u32[]{:S(2)}) collective-permute-start(bf16[64,128]{1,0:T(8,128)(2,1)S(1)} %shard_map.59.own), channel_id=1, source_target_pairs={{16,32},{48,64},{80,96},{112,128},{144,160},{176,192},{208,224},{2... | collective-permute-start | bytes 49160 | tf_op jit(solution)/shard_map/ppermute | solution.py:65
  166.9 1.5 collective-permute-done.21.refs_5_
  168.4 4.8 %collective-permute-done.20.refs_4_ = bf16[64,128]{1,0:T(8,128)(2,1)S(1)} collective-permute-done((bf16[64,128]{1,0:T(8,128)(2,1)S(1)}, bf16[64,128]{1,0:T(8,128)(2,1)S(1)}, u32[]{:S(2)}, u32[]{:S(2)}) %collective-permute-start.20) | collective-permute-done | bytes 16416 | tf_op jit(solution)/shard_map/ppermute | solution.py:65
  173.2 1.8 %shard_map.60 = f32[2048,128]{1,0:T(8,128)} custom-call(s32[4]{0:T(128)S(1)} %pad_add_fusion.facts, f32[2048,128]{1,0:T(8,128)S(1)} %get-tuple-element.73.stepped, bf16[64,2048]{1,0:T(8,128)(2,1)S(1)} %bitcast.25, bf16[64,128]{1,0:T(8,128)(2,1)S(1)} %shard_map.59.own, bf16[320,128]{1,0:T(8,128)(2,1)S(1)} %collective-permute-done.4.refs_0_.refs_4_, ...), custom_call_target="tpu_custom_call" | custom-call | bytes 2097152 | tf_op jit(solution)/shard_map/pallas_call | solution.py:22
  (44 shorter events, 13.2 us)
Async XLA Ops:
  0.0 36.2 %copy-start.1 = (bf16[1,1,1024,1024]{3,2,1,0:T(8,128)(2,1)S(1)}, bf16[1,1,1024,1024]{3,2,1,0:T(8,128)(2,1)}, u32[]{:S(2)}) copy-start(bf16[1,1,1024,1024]{3,2,1,0:T(8,128)(2,1)} %param.7) | copy-start | bytes 6291460
  0.0 15.5 %copy-start.2 = (bf16[1,1,64,2048]{3,2,1,0:T(8,128)(2,1)S(1)}, bf16[1,1,64,2048]{3,2,1,0:T(8,128)(2,1)}, u32[]{:S(2)}) copy-start(bf16[1,1,64,2048]{3,2,1,0:T(8,128)(2,1)} %param.6) | copy-start | bytes 786436
  0.0 36.2 %copy-start = (bf16[1,1,2048,2048]{3,2,1,0:T(8,128)(2,1)S(1)}, bf16[1,1,2048,2048]{3,2,1,0:T(8,128)(2,1)}, u32[]{:S(2)}) copy-start(bf16[1,1,2048,2048]{3,2,1,0:T(8,128)(2,1)} %param.4) | copy-start | bytes 25165828
  2.2 8.5 %collective-permute-start = (bf16[512,128]{1,0:T(8,128)(2,1)S(1)}, bf16[512,128]{1,0:T(8,128)(2,1)S(1)}, u32[]{:S(2)}, u32[]{:S(2)}) collective-permute-start(bf16[512,128]{1,0:T(8,128)(2,1)S(1)} %get-tuple-element.41), channel_id=1, source_target_pairs={{1,2},{3,4},{5,6},{7,8},{9,10},{11,12},{13,14},{15,0},{2,1},{4,3},... | collective-permute-start | bytes 393224 | tf_op jit(solution)/shard_map/ppermute | solution.py:65
  7.1 6.0 %collective-permute-start.1 = (bf16[512,128]{1,0:T(8,128)(2,1)S(1)}, bf16[512,128]{1,0:T(8,128)(2,1)S(1)}, u32[]{:S(2)}, u32[]{:S(2)}) collective-permute-start(bf16[512,128]{1,0:T(8,128)(2,1)S(1)} %get-tuple-element.42), channel_id=1, source_target_pairs={{16,32},{48,64},{80,96},{112,128},{144,160},{176,192},{208,224},{2... | collective-permute-start | bytes 393224 | tf_op jit(solution)/shard_map/ppermute | solution.py:65
  7.3 8.2 %collective-permute-start.2 = (bf16[512,128]{1,0:T(8,128)(2,1)S(1)}, bf16[512,128]{1,0:T(8,128)(2,1)S(1)}, u32[]{:S(2)}, u32[]{:S(2)}) collective-permute-start(bf16[512,128]{1,0:T(8,128)(2,1)S(1)} %get-tuple-element.43), channel_id=1, source_target_pairs={{0,16},{32,48},{64,80},{96,112},{128,144},{160,176},{192,208},{224... | collective-permute-start | bytes 393224 | tf_op jit(solution)/shard_map/ppermute | solution.py:65
  10.5 5.1 %collective-permute-start.3 = (bf16[512,128]{1,0:T(8,128)(2,1)S(1)}, bf16[512,128]{1,0:T(8,128)(2,1)S(1)}, u32[]{:S(2)}, u32[]{:S(2)}) collective-permute-start(bf16[512,128]{1,0:T(8,128)(2,1)S(1)} %get-tuple-element.44), channel_id=1, source_target_pairs={{0,1},{2,3},{4,5},{6,7},{8,9},{10,11},{12,13},{14,15},{1,0},{3,2},... | collective-permute-start | bytes 393224 | tf_op jit(solution)/shard_map/ppermute | solution.py:65
  51.8 5.5 %collective-permute-start.5 = (bf16[320,128]{1,0:T(8,128)(2,1)S(1)}, bf16[320,128]{1,0:T(8,128)(2,1)S(1)}, u32[]{:S(2)}, u32[]{:S(2)}) collective-permute-start(bf16[320,128]{1,0:T(8,128)(2,1)S(1)} %get-tuple-element.48), channel_id=1, source_target_pairs={{16,32},{48,64},{80,96},{112,128},{144,160},{176,192},{208,224},{2... | collective-permute-start | bytes 245768 | tf_op jit(solution)/shard_map/ppermute | solution.py:65
  52.9 7.1 %collective-permute-start.6 = (bf16[320,128]{1,0:T(8,128)(2,1)S(1)}, bf16[320,128]{1,0:T(8,128)(2,1)S(1)}, u32[]{:S(2)}, u32[]{:S(2)}) collective-permute-start(bf16[320,128]{1,0:T(8,128)(2,1)S(1)} %get-tuple-element.49), channel_id=1, source_target_pairs={{0,16},{32,48},{64,80},{96,112},{128,144},{160,176},{192,208},{224... | collective-permute-start | bytes 245768 | tf_op jit(solution)/shard_map/ppermute | solution.py:65
  54.4 5.5 %collective-permute-start.7 = (bf16[320,128]{1,0:T(8,128)(2,1)S(1)}, bf16[320,128]{1,0:T(8,128)(2,1)S(1)}, u32[]{:S(2)}, u32[]{:S(2)}) collective-permute-start(bf16[320,128]{1,0:T(8,128)(2,1)S(1)} %get-tuple-element.50), channel_id=1, source_target_pairs={{0,1},{2,3},{4,5},{6,7},{8,9},{10,11},{12,13},{14,15},{1,0},{3,2},... | collective-permute-start | bytes 245768 | tf_op jit(solution)/shard_map/ppermute | solution.py:65
  54.4 7.5 %collective-permute-start.4 = (bf16[320,128]{1,0:T(8,128)(2,1)S(1)}, bf16[320,128]{1,0:T(8,128)(2,1)S(1)}, u32[]{:S(2)}, u32[]{:S(2)}) collective-permute-start(bf16[320,128]{1,0:T(8,128)(2,1)S(1)} %get-tuple-element.47.own), channel_id=1, source_target_pairs={{1,2},{3,4},{5,6},{7,8},{9,10},{11,12},{13,14},{15,0},{2,1},{4,3},... | collective-permute-start | bytes 245768 | tf_op jit(solution)/shard_map/ppermute | solution.py:65
  64.1 8.9 %collective-permute-start.8 = (bf16[512,128]{1,0:T(8,128)(2,1)S(1)}, bf16[512,128]{1,0:T(8,128)(2,1)S(1)}, u32[]{:S(2)}, u32[]{:S(2)}) collective-permute-start(bf16[512,128]{1,0:T(8,128)(2,1)S(1)} %get-tuple-element.57), channel_id=1, source_target_pairs={{1,2},{3,4},{5,6},{7,8},{9,10},{11,12},{13,14},{15,0},{2,1},{4,3},... | collective-permute-start | bytes 393224 | tf_op jit(solution)/shard_map/ppermute | solution.py:65
  64.8 8.1 %collective-permute-start.9 = (bf16[512,128]{1,0:T(8,128)(2,1)S(1)}, bf16[512,128]{1,0:T(8,128)(2,1)S(1)}, u32[]{:S(2)}, u32[]{:S(2)}) collective-permute-start(bf16[512,128]{1,0:T(8,128)(2,1)S(1)} %get-tuple-element.58), channel_id=1, source_target_pairs={{16,32},{48,64},{80,96},{112,128},{144,160},{176,192},{208,224},{2... | collective-permute-start | bytes 393224 | tf_op jit(solution)/shard_map/ppermute | solution.py:65
  67.4 6.5 %collective-permute-start.10 = (bf16[512,128]{1,0:T(8,128)(2,1)S(1)}, bf16[512,128]{1,0:T(8,128)(2,1)S(1)}, u32[]{:S(2)}, u32[]{:S(2)}) collective-permute-start(bf16[512,128]{1,0:T(8,128)(2,1)S(1)} %get-tuple-element.59), channel_id=1, source_target_pairs={{0,16},{32,48},{64,80},{96,112},{128,144},{160,176},{192,208},{224... | collective-permute-start | bytes 393224 | tf_op jit(solution)/shard_map/ppermute | solution.py:65
  69.0 4.9 %collective-permute-start.11 = (bf16[512,128]{1,0:T(8,128)(2,1)S(1)}, bf16[512,128]{1,0:T(8,128)(2,1)S(1)}, u32[]{:S(2)}, u32[]{:S(2)}) collective-permute-start(bf16[512,128]{1,0:T(8,128)(2,1)S(1)} %get-tuple-element.60), channel_id=1, source_target_pairs={{0,1},{2,3},{4,5},{6,7},{8,9},{10,11},{12,13},{14,15},{1,0},{3,2},... | collective-permute-start | bytes 393224 | tf_op jit(solution)/shard_map/ppermute | solution.py:65
  107.3 3.7 %collective-permute-start.15 = (bf16[64,128]{1,0:T(8,128)(2,1)S(1)}, bf16[64,128]{1,0:T(8,128)(2,1)S(1)}, u32[]{:S(2)}, u32[]{:S(2)}) collective-permute-start(bf16[64,128]{1,0:T(8,128)(2,1)S(1)} %shard_map.54.own), channel_id=1, source_target_pairs={{0,1},{2,3},{4,5},{6,7},{8,9},{10,11},{12,13},{14,15},{1,0},{3,2},... | collective-permute-start | bytes 49160 | tf_op jit(solution)/shard_map/ppermute | solution.py:65
  107.5 3.9 %collective-permute-start.14 = (bf16[64,128]{1,0:T(8,128)(2,1)S(1)}, bf16[64,128]{1,0:T(8,128)(2,1)S(1)}, u32[]{:S(2)}, u32[]{:S(2)}) collective-permute-start(bf16[64,128]{1,0:T(8,128)(2,1)S(1)} %shard_map.54.own), channel_id=1, source_target_pairs={{0,16},{32,48},{64,80},{96,112},{128,144},{160,176},{192,208},{224... | collective-permute-start | bytes 49160 | tf_op jit(solution)/shard_map/ppermute | solution.py:65
  107.7 4.7 %collective-permute-start.13 = (bf16[64,128]{1,0:T(8,128)(2,1)S(1)}, bf16[64,128]{1,0:T(8,128)(2,1)S(1)}, u32[]{:S(2)}, u32[]{:S(2)}) collective-permute-start(bf16[64,128]{1,0:T(8,128)(2,1)S(1)} %shard_map.54.own), channel_id=1, source_target_pairs={{16,32},{48,64},{80,96},{112,128},{144,160},{176,192},{208,224},{2... | collective-permute-start | bytes 49160 | tf_op jit(solution)/shard_map/ppermute | solution.py:65
  110.7 6.8 %collective-permute-start.12 = (bf16[64,128]{1,0:T(8,128)(2,1)S(1)}, bf16[64,128]{1,0:T(8,128)(2,1)S(1)}, u32[]{:S(2)}, u32[]{:S(2)}) collective-permute-start(bf16[64,128]{1,0:T(8,128)(2,1)S(1)} %shard_map.54.own), channel_id=1, source_target_pairs={{1,2},{3,4},{5,6},{7,8},{9,10},{11,12},{13,14},{15,0},{2,1},{4,3},... | collective-permute-start | bytes 49160 | tf_op jit(solution)/shard_map/ppermute | solution.py:65
  121.4 9.7 %collective-permute-start.18 = (bf16[512,128]{1,0:T(8,128)(2,1)S(1)}, bf16[512,128]{1,0:T(8,128)(2,1)S(1)}, u32[]{:S(2)}, u32[]{:S(2)}) collective-permute-start(bf16[512,128]{1,0:T(8,128)(2,1)S(1)} %get-tuple-element.71), channel_id=1, source_target_pairs={{0,16},{32,48},{64,80},{96,112},{128,144},{160,176},{192,208},{224... | collective-permute-start | bytes 393224 | tf_op jit(solution)/shard_map/ppermute | solution.py:65
  121.5 9.6 %collective-permute-start.19 = (bf16[512,128]{1,0:T(8,128)(2,1)S(1)}, bf16[512,128]{1,0:T(8,128)(2,1)S(1)}, u32[]{:S(2)}, u32[]{:S(2)}) collective-permute-start(bf16[512,128]{1,0:T(8,128)(2,1)S(1)} %get-tuple-element.72), channel_id=1, source_target_pairs={{0,1},{2,3},{4,5},{6,7},{8,9},{10,11},{12,13},{14,15},{1,0},{3,2},... | collective-permute-start | bytes 393224 | tf_op jit(solution)/shard_map/ppermute | solution.py:65
  121.6 9.5 %collective-permute-start.16 = (bf16[512,128]{1,0:T(8,128)(2,1)S(1)}, bf16[512,128]{1,0:T(8,128)(2,1)S(1)}, u32[]{:S(2)}, u32[]{:S(2)}) collective-permute-start(bf16[512,128]{1,0:T(8,128)(2,1)S(1)} %get-tuple-element.69), channel_id=1, source_target_pairs={{1,2},{3,4},{5,6},{7,8},{9,10},{11,12},{13,14},{15,0},{2,1},{4,3},... | collective-permute-start | bytes 393224 | tf_op jit(solution)/shard_map/ppermute | solution.py:65
  122.1 9.1 %collective-permute-start.17 = (bf16[512,128]{1,0:T(8,128)(2,1)S(1)}, bf16[512,128]{1,0:T(8,128)(2,1)S(1)}, u32[]{:S(2)}, u32[]{:S(2)}) collective-permute-start(bf16[512,128]{1,0:T(8,128)(2,1)S(1)} %get-tuple-element.70), channel_id=1, source_target_pairs={{16,32},{48,64},{80,96},{112,128},{144,160},{176,192},{208,224},{2... | collective-permute-start | bytes 393224 | tf_op jit(solution)/shard_map/ppermute | solution.py:65
  162.9 3.8 %collective-permute-start.23 = (bf16[64,128]{1,0:T(8,128)(2,1)S(1)}, bf16[64,128]{1,0:T(8,128)(2,1)S(1)}, u32[]{:S(2)}, u32[]{:S(2)}) collective-permute-start(bf16[64,128]{1,0:T(8,128)(2,1)S(1)} %shard_map.59.own), channel_id=1, source_target_pairs={{0,1},{2,3},{4,5},{6,7},{8,9},{10,11},{12,13},{14,15},{1,0},{3,2},... | collective-permute-start | bytes 49160 | tf_op jit(solution)/shard_map/ppermute | solution.py:65
  163.1 3.7 %collective-permute-start.22 = (bf16[64,128]{1,0:T(8,128)(2,1)S(1)}, bf16[64,128]{1,0:T(8,128)(2,1)S(1)}, u32[]{:S(2)}, u32[]{:S(2)}) collective-permute-start(bf16[64,128]{1,0:T(8,128)(2,1)S(1)} %shard_map.59.own), channel_id=1, source_target_pairs={{0,16},{32,48},{64,80},{96,112},{128,144},{160,176},{192,208},{224... | collective-permute-start | bytes 49160 | tf_op jit(solution)/shard_map/ppermute | solution.py:65
  163.7 4.7 %collective-permute-start.21 = (bf16[64,128]{1,0:T(8,128)(2,1)S(1)}, bf16[64,128]{1,0:T(8,128)(2,1)S(1)}, u32[]{:S(2)}, u32[]{:S(2)}) collective-permute-start(bf16[64,128]{1,0:T(8,128)(2,1)S(1)} %shard_map.59.own), channel_id=1, source_target_pairs={{16,32},{48,64},{80,96},{112,128},{144,160},{176,192},{208,224},{2... | collective-permute-start | bytes 49160 | tf_op jit(solution)/shard_map/ppermute | solution.py:65
  166.4 6.8 %collective-permute-start.20 = (bf16[64,128]{1,0:T(8,128)(2,1)S(1)}, bf16[64,128]{1,0:T(8,128)(2,1)S(1)}, u32[]{:S(2)}, u32[]{:S(2)}) collective-permute-start(bf16[64,128]{1,0:T(8,128)(2,1)S(1)} %shard_map.59.own), channel_id=1, source_target_pairs={{1,2},{3,4},{5,6},{7,8},{9,10},{11,12},{13,14},{15,0},{2,1},{4,3},... | collective-permute-start | bytes 49160 | tf_op jit(solution)/shard_map/ppermute | solution.py:65

commit v4 on v3

--- a/solution.py
+++ b/solution.py
@@ -12,7 +12,6 @@
 DAMPING = 0.5
 
 VMEM = pl.BlockSpec(memory_space=pltpu.VMEM)
-SMEM = pl.BlockSpec(memory_space=pltpu.SMEM)
 HBM = pl.BlockSpec(memory_space=pltpu.HBM)
 BF16 = jnp.bfloat16
 F32 = jnp.float32
@@ -22,7 +21,7 @@
     return lambda *operands: pl.pallas_call(
         body,
         out_shape=tuple(outs),
-        in_specs=[SMEM] + [HBM if i in outside else VMEM for i in range(1, len(operands))],
+        in_specs=[HBM if i in outside else VMEM for i in range(len(operands))],
         out_specs=tuple([out_space] * len(outs)),
         scratch_shapes=list(scratch),
         compiler_params=pltpu.CompilerParams(vmem_limit_bytes=limit),
@@ -34,7 +33,12 @@
     places = [(lax.axis_index(axis), lax.axis_size(axis)) for axis in ("sx", "sy")]
     odd = [lax.rem(place, 2) for place, count in places]
     ends = [((place == 0) | (place == count - 1)).astype(jnp.int32) for place, count in places]
-    return jnp.stack(odd + ends)
+    return jnp.broadcast_to(jnp.stack(odd + ends)[:, None], (4, 128))
+
+
+def scalars(facts):
+    rows = facts[...]
+    return [rows[row, 0] for row in range(4)]
 
 
 EXCHANGES = ((1, True), (0, True), (0, False), (1, False))
@@ -67,6 +71,7 @@
 
 
 def faces_body(facts, loads, tile, operator, *refs):
+    facts = scalars(facts)
     del tile, operator
     faces, (right, arrived) = refs[:4], refs[4:]
     width = loads.shape[0] // 4
@@ -83,6 +88,7 @@
 
 
 def restrict_body(first, facts, basis, *refs):
+    facts = scalars(facts)
     if first:
         (values,), refs = refs[:1], refs[1:]
     else:
@@ -100,7 +106,7 @@
     coarse[...] = jnp.broadcast_to(total.astype(BF16)[None], coarse.shape)
 
 
-def tile_body(facts, tile, columns, *others):
+def tile_body(tile, columns, *others):
     partial = others[-1]
     count, rows, loads = partial.shape
     whole = columns[...].reshape(tile.shape[1], loads)
@@ -108,11 +114,12 @@
     partial[...] = product.astype(BF16).reshape(count, rows, loads)
 
 
-def sum_body(facts, parts, total):
+def sum_body(parts, total):
     total[...] = jnp.sum(parts[...].astype(F32), axis=0).astype(BF16)
 
 
 def sum_with_basis_body(facts, parts, basis, *messages):
+    facts = scalars(facts)
     total = jnp.sum(parts[...].astype(F32), axis=0).astype(BF16)
     rows, loads = total.shape
     width = basis.shape[1] // 4
@@ -148,6 +155,7 @@
 
 
 def advance_body(facts, stepped, basis, own, operator, right, *refs):
+    facts = scalars(facts)
     slices, theirs = refs[:4], refs[4:8]
     held, rounded = refs[8:10]
     values, faces = refs[10:12], refs[12:14]
@@ -163,10 +171,12 @@
 
 
 def advance_near_body(facts, operator, right, rounded, *refs):
+    facts = scalars(facts)
     multiplied(facts, slice(2, 4), operator, right, rounded, refs[:2], refs[2:])
 
 
 def finish_body(facts, stepped, basis, own, *refs):
+    facts = scalars(facts)
     slices, theirs, (out, block, leaving) = refs[:4], refs[4:8], refs[8:]
     width = out.shape[0] // 4
     rows = basis.shape[0]
@@ -222,8 +232,8 @@
             [blocks_y],
             flops=2 * tile.size * columns,
             moved=3 << 20,
-            outside=(3,) if first else (),
-        )(facts, tile, gathered, *([operator] if first else []))
+            outside=(2,) if first else (),
+        )(tile, gathered, *([operator] if first else []))
         parts = lax.all_to_all(partial, "sy", 0, 0, tiled=True)
         if first:
             messages = kernel_call(sum_with_basis_body, [message] * 4, moved=1 << 20)(
@@ -233,7 +243,7 @@
             theirs = exchange(messages)
             slices = theirs
         else:
-            (own,) = kernel_call(sum_body, [coarse], moved=1 << 18)(facts, parts)
+            (own,) = kernel_call(sum_body, [coarse], moved=1 << 18)(parts)
             theirs = exchange([own] * 4)
         if step < ITERS - 1:
             part = jax.ShapeDtypeStruct((width, columns), F32)

time: 175 us -> 169 us (0.966)
  Pallas kernels: 19.9 us -> 12.6 us
    pallas_call x15, Pallas kernels: 19.9 us -> 12.6 us  [kernel_call(): pl.pallas_call(body, out_shape=tuple(outs), in_specs=[HBM if i in outside...]
where the time goes in v4:
time: 169 us
  blocking collectives  93.3 us (55%)
  waiting for transfers between devices  38.3 us (23%)
  starting transfers between devices  24 us (14%)
  Pallas kernels  12.6 us (7%)
    all_to_all x3, blocking collectives, local(): gathered = lax.all_to_all(sent, 'sx', 0, 0, tiled=True)  53.9 us
    all_to_all x3, blocking collectives, local(): parts = lax.all_to_all(partial, 'sy', 0, 0, tiled=True)  39.4 us
    ppermute x24, waiting for transfers between devices, exchange(): received.append(lax.ppermute(part, name, pairs))  38.3 us
    ppermute x24, starting transfers between devices, exchange(): received.append(lax.ppermute(part, name, pairs))  24 us
    pallas_call x15, Pallas kernels, kernel_call(): pl.pallas_call(body, out_shape=tuple(outs), in_specs=[HBM if i in outside...  12.6 us
  transfers between devices with their start and end apart: 24, of which 15 were waited for; matrix products, arithmetic and copies ran while one was open for 0% of the time, Pallas kernels for 1%

profile of v4, /device:TPU:32, one launch (start us, length us, event | category | flops | bytes accessed | tf_op | source)
XLA Modules:
  0.0 168.7 jit_solution(12632497207649013015)
XLA Ops:
  0.2 2.1 %shard_map.46 = (bf16[512,128]{1,0:T(8,128)(2,1)}, bf16[512,128]{1,0:T(8,128)(2,1)S(1)}, bf16[512,128]{1,0:T(8,128)(2,1)S(1)}, bf16[512,128]{1,0:T(8,128)(2,1)S(1)}, f32[2048,128]{1,0:T(8,128)S(1)}) custom-call(s32[4,128]{1,0:T(4,128)S(1)} %broadcast_in_dim.4.facts, f32[2048,128]{1,0:T(8,128)} %bitcast.26, bf16[1024,1024]{1,0:T(8,128)(2,1)} %bitcast.15, ...), custom_call_target="tpu_custom_call" | custom-call | bytes 3145728 | tf_op jit(solution)/shard_map/pallas_call | solution.py:21
  2.2 4.9 %collective-permute-start = (bf16[512,128]{1,0:T(8,128)(2,1)}, bf16[512,128]{1,0:T(8,128)(2,1)S(1)}, u32[]{:S(2)}, u32[]{:S(2)}) collective-permute-start(bf16[512,128]{1,0:T(8,128)(2,1)} %get-tuple-element.41), channel_id=1, source_target_pairs={{1,2},{3,4},{5,6},{7,8},{9,10},{11,12},{13,14},{15,0},{2,1},{4,3},... | collective-permute-start | bytes 393224 | tf_op jit(solution)/shard_map/ppermute | solution.py:69
  7.4 3.2 %collective-permute-start.2 = (bf16[512,128]{1,0:T(8,128)(2,1)S(1)}, bf16[512,128]{1,0:T(8,128)(2,1)S(1)}, u32[]{:S(2)}, u32[]{:S(2)}) collective-permute-start(bf16[512,128]{1,0:T(8,128)(2,1)S(1)} %get-tuple-element.43), channel_id=1, source_target_pairs={{0,16},{32,48},{64,80},{96,112},{128,144},{160,176},{192,208},{224... | collective-permute-start | bytes 393224 | tf_op jit(solution)/shard_map/ppermute | solution.py:69
  11.2 1.8 %collective-permute-done.1.refs_2_ = bf16[512,128]{1,0:T(8,128)(2,1)S(1)} collective-permute-done((bf16[512,128]{1,0:T(8,128)(2,1)S(1)}, bf16[512,128]{1,0:T(8,128)(2,1)S(1)}, u32[]{:S(2)}, u32[]{:S(2)}) %collective-permute-start.1) | collective-permute-done | bytes 131104 | tf_op jit(solution)/shard_map/ppermute | solution.py:69
  13.0 2.8 %collective-permute-done.2.refs_3_ = bf16[512,128]{1,0:T(8,128)(2,1)S(1)} collective-permute-done((bf16[512,128]{1,0:T(8,128)(2,1)S(1)}, bf16[512,128]{1,0:T(8,128)(2,1)S(1)}, u32[]{:S(2)}, u32[]{:S(2)}) %collective-permute-start.2) | collective-permute-done | bytes 131104 | tf_op jit(solution)/shard_map/ppermute | solution.py:69
  16.2 19.8 %all_to_all.30.columns = bf16[16,64,128]{2,1,0:T(8,128)(2,1)S(1)} all-to-all(bf16[16,64,128]{2,1,0:T(8,128)(2,1)S(1)} %get-tuple-element.46), channel_id=1, replica_groups=mesh['sx'=16,'sy'=16] {'sx'}, dimensions={0} | all-to-all | bytes 524288 | tf_op jit(solution)/shard_map/all_to_all | solution.py:229
  36.6 13.7 %all_to_all.31.parts = bf16[16,64,128]{2,1,0:T(8,128)(2,1)S(1)} all-to-all(bf16[16,64,128]{2,1,0:T(8,128)(2,1)S(1)} %shard_map.48), channel_id=1, replica_groups=mesh['sx'=16,'sy'=16] {'sy'}, dimensions={0} | all-to-all | bytes 524288 | tf_op jit(solution)/shard_map/all_to_all | solution.py:237
  50.5 1.1 collective-permute-start.5
  51.6 1.6 collective-permute-start.6
  53.8 2.2 %collective-permute-done.5.refs_1_.refs_5_ = bf16[320,128]{1,0:T(8,128)(2,1)S(1)} collective-permute-done((bf16[320,128]{1,0:T(8,128)(2,1)S(1)}, bf16[320,128]{1,0:T(8,128)(2,1)S(1)}, u32[]{:S(2)}, u32[]{:S(2)}) %collective-permute-start.5) | collective-permute-done | bytes 81952 | tf_op jit(solution)/shard_map/ppermute | solution.py:69
  56.1 2.6 %collective-permute-done.6.refs_2_.refs_6_ = bf16[320,128]{1,0:T(8,128)(2,1)S(1)} collective-permute-done((bf16[320,128]{1,0:T(8,128)(2,1)S(1)}, bf16[320,128]{1,0:T(8,128)(2,1)S(1)}, u32[]{:S(2)}, u32[]{:S(2)}) %collective-permute-start.6) | collective-permute-done | bytes 81952 | tf_op jit(solution)/shard_map/ppermute | solution.py:69
  58.7 1.9 %collective-permute-done.4.refs_0_.refs_4_ = bf16[320,128]{1,0:T(8,128)(2,1)S(1)} collective-permute-done((bf16[320,128]{1,0:T(8,128)(2,1)S(1)}, bf16[320,128]{1,0:T(8,128)(2,1)S(1)}, u32[]{:S(2)}, u32[]{:S(2)}) %collective-permute-start.4) | collective-permute-done | bytes 81952 | tf_op jit(solution)/shard_map/ppermute | solution.py:69
  60.6 1.7 shard_map.50
  63.9 1.3 shard_map.51
  65.1 1.6 collective-permute-start.10
  66.7 4.4 %collective-permute-done.8.refs_5_ = bf16[512,128]{1,0:T(8,128)(2,1)S(1)} collective-permute-done((bf16[512,128]{1,0:T(8,128)(2,1)S(1)}, bf16[512,128]{1,0:T(8,128)(2,1)S(1)}, u32[]{:S(2)}, u32[]{:S(2)}) %collective-permute-start.8) | collective-permute-done | bytes 131104 | tf_op jit(solution)/shard_map/ppermute | solution.py:69
  71.1 1.0 collective-permute-done.10.refs_7_
  72.5 16.9 %all_to_all.32.columns = bf16[16,64,128]{2,1,0:T(8,128)(2,1)S(1)} all-to-all(bf16[16,64,128]{2,1,0:T(8,128)(2,1)S(1)} %get-tuple-element.62), channel_id=1, replica_groups=mesh['sx'=16,'sy'=16] {'sx'}, dimensions={0} | all-to-all | bytes 524288 | tf_op jit(solution)/shard_map/all_to_all | solution.py:229
  90.2 13.8 %all_to_all.33.parts = bf16[16,64,128]{2,1,0:T(8,128)(2,1)S(1)} all-to-all(bf16[16,64,128]{2,1,0:T(8,128)(2,1)S(1)} %shard_map.53), channel_id=1, replica_groups=mesh['sx'=16,'sy'=16] {'sy'}, dimensions={0} | all-to-all | bytes 524288 | tf_op jit(solution)/shard_map/all_to_all | solution.py:237
  104.4 3.0 %collective-permute-start.13 = (bf16[64,128]{1,0:T(8,128)(2,1)S(1)}, bf16[64,128]{1,0:T(8,128)(2,1)S(1)}, u32[]{:S(2)}, u32[]{:S(2)}) collective-permute-start(bf16[64,128]{1,0:T(8,128)(2,1)S(1)} %shard_map.54.own), channel_id=1, source_target_pairs={{16,32},{48,64},{80,96},{112,128},{144,160},{176,192},{208,224},{2... | collective-permute-start | bytes 49160 | tf_op jit(solution)/shard_map/ppermute | solution.py:69
  108.1 1.0 collective-permute-done.13.refs_5_
  109.1 5.0 %collective-permute-done.12.refs_4_ = bf16[64,128]{1,0:T(8,128)(2,1)S(1)} collective-permute-done((bf16[64,128]{1,0:T(8,128)(2,1)S(1)}, bf16[64,128]{1,0:T(8,128)(2,1)S(1)}, u32[]{:S(2)}, u32[]{:S(2)}) %collective-permute-start.12) | collective-permute-done | bytes 16416 | tf_op jit(solution)/shard_map/ppermute | solution.py:69
  114.1 1.7 shard_map.55
  115.8 1.3 shard_map.56
  117.7 1.2 collective-permute-start.17
  118.9 7.9 %collective-permute-done.18.refs_7_ = bf16[512,128]{1,0:T(8,128)(2,1)S(1)} collective-permute-done((bf16[512,128]{1,0:T(8,128)(2,1)S(1)}, bf16[512,128]{1,0:T(8,128)(2,1)S(1)}, u32[]{:S(2)}, u32[]{:S(2)}) %collective-permute-start.18) | collective-permute-done | bytes 131104 | tf_op jit(solution)/shard_map/ppermute | solution.py:69
  127.2 17.2 %all_to_all.34.columns = bf16[16,64,128]{2,1,0:T(8,128)(2,1)S(1)} all-to-all(bf16[16,64,128]{2,1,0:T(8,128)(2,1)S(1)} %get-tuple-element.74), channel_id=1, replica_groups=mesh['sx'=16,'sy'=16] {'sx'}, dimensions={0} | all-to-all | bytes 524288 | tf_op jit(solution)/shard_map/all_to_all | solution.py:229
  145.1 11.9 %all_to_all.35.parts = bf16[16,64,128]{2,1,0:T(8,128)(2,1)S(1)} all-to-all(bf16[16,64,128]{2,1,0:T(8,128)(2,1)S(1)} %shard_map.58), channel_id=1, replica_groups=mesh['sx'=16,'sy'=16] {'sy'}, dimensions={0} | all-to-all | bytes 524288 | tf_op jit(solution)/shard_map/all_to_all | solution.py:237
  157.7 2.7 %collective-permute-start.21 = (bf16[64,128]{1,0:T(8,128)(2,1)S(1)}, bf16[64,128]{1,0:T(8,128)(2,1)S(1)}, u32[]{:S(2)}, u32[]{:S(2)}) collective-permute-start(bf16[64,128]{1,0:T(8,128)(2,1)S(1)} %shard_map.59.own), channel_id=1, source_target_pairs={{16,32},{48,64},{80,96},{112,128},{144,160},{176,192},{208,224},{2... | collective-permute-start | bytes 49160 | tf_op jit(solution)/shard_map/ppermute | solution.py:69
  160.9 1.5 collective-permute-done.21.refs_5_
  162.5 4.8 %collective-permute-done.20.refs_4_ = bf16[64,128]{1,0:T(8,128)(2,1)S(1)} collective-permute-done((bf16[64,128]{1,0:T(8,128)(2,1)S(1)}, bf16[64,128]{1,0:T(8,128)(2,1)S(1)}, u32[]{:S(2)}, u32[]{:S(2)}) %collective-permute-start.20) | collective-permute-done | bytes 16416 | tf_op jit(solution)/shard_map/ppermute | solution.py:69
  167.2 1.3 shard_map.60
  (45 shorter events, 9.7 us)
Async XLA Ops:
  0.0 35.9 %copy-start.1 = (bf16[1,1,1024,1024]{3,2,1,0:T(8,128)(2,1)S(1)}, bf16[1,1,1024,1024]{3,2,1,0:T(8,128)(2,1)}, u32[]{:S(2)}) copy-start(bf16[1,1,1024,1024]{3,2,1,0:T(8,128)(2,1)} %param.7) | copy-start | bytes 6291460
  0.0 15.8 %copy-start.2 = (bf16[1,1,64,2048]{3,2,1,0:T(8,128)(2,1)S(1)}, bf16[1,1,64,2048]{3,2,1,0:T(8,128)(2,1)}, u32[]{:S(2)}) copy-start(bf16[1,1,64,2048]{3,2,1,0:T(8,128)(2,1)} %param.6) | copy-start | bytes 786436
  0.0 35.9 %copy-start = (bf16[1,1,2048,2048]{3,2,1,0:T(8,128)(2,1)S(1)}, bf16[1,1,2048,2048]{3,2,1,0:T(8,128)(2,1)}, u32[]{:S(2)}) copy-start(bf16[1,1,2048,2048]{3,2,1,0:T(8,128)(2,1)} %param.4) | copy-start | bytes 25165828
  2.2 9.0 %collective-permute-start = (bf16[512,128]{1,0:T(8,128)(2,1)}, bf16[512,128]{1,0:T(8,128)(2,1)S(1)}, u32[]{:S(2)}, u32[]{:S(2)}) collective-permute-start(bf16[512,128]{1,0:T(8,128)(2,1)} %get-tuple-element.41), channel_id=1, source_target_pairs={{1,2},{3,4},{5,6},{7,8},{9,10},{11,12},{13,14},{15,0},{2,1},{4,3},... | collective-permute-start | bytes 393224 | tf_op jit(solution)/shard_map/ppermute | solution.py:69
  7.2 5.9 %collective-permute-start.1 = (bf16[512,128]{1,0:T(8,128)(2,1)S(1)}, bf16[512,128]{1,0:T(8,128)(2,1)S(1)}, u32[]{:S(2)}, u32[]{:S(2)}) collective-permute-start(bf16[512,128]{1,0:T(8,128)(2,1)S(1)} %get-tuple-element.42), channel_id=1, source_target_pairs={{16,32},{48,64},{80,96},{112,128},{144,160},{176,192},{208,224},{2... | collective-permute-start | bytes 393224 | tf_op jit(solution)/shard_map/ppermute | solution.py:69
  7.4 8.4 %collective-permute-start.2 = (bf16[512,128]{1,0:T(8,128)(2,1)S(1)}, bf16[512,128]{1,0:T(8,128)(2,1)S(1)}, u32[]{:S(2)}, u32[]{:S(2)}) collective-permute-start(bf16[512,128]{1,0:T(8,128)(2,1)S(1)} %get-tuple-element.43), channel_id=1, source_target_pairs={{0,16},{32,48},{64,80},{96,112},{128,144},{160,176},{192,208},{224... | collective-permute-start | bytes 393224 | tf_op jit(solution)/shard_map/ppermute | solution.py:69
  10.5 5.3 %collective-permute-start.3 = (bf16[512,128]{1,0:T(8,128)(2,1)S(1)}, bf16[512,128]{1,0:T(8,128)(2,1)S(1)}, u32[]{:S(2)}, u32[]{:S(2)}) collective-permute-start(bf16[512,128]{1,0:T(8,128)(2,1)S(1)} %get-tuple-element.44), channel_id=1, source_target_pairs={{0,1},{2,3},{4,5},{6,7},{8,9},{10,11},{12,13},{14,15},{1,0},{3,2},... | collective-permute-start | bytes 393224 | tf_op jit(solution)/shard_map/ppermute | solution.py:69
  50.5 5.5 %collective-permute-start.5 = (bf16[320,128]{1,0:T(8,128)(2,1)S(1)}, bf16[320,128]{1,0:T(8,128)(2,1)S(1)}, u32[]{:S(2)}, u32[]{:S(2)}) collective-permute-start(bf16[320,128]{1,0:T(8,128)(2,1)S(1)} %get-tuple-element.48), channel_id=1, source_target_pairs={{16,32},{48,64},{80,96},{112,128},{144,160},{176,192},{208,224},{2... | collective-permute-start | bytes 245768 | tf_op jit(solution)/shard_map/ppermute | solution.py:69
  51.6 7.1 %collective-permute-start.6 = (bf16[320,128]{1,0:T(8,128)(2,1)S(1)}, bf16[320,128]{1,0:T(8,128)(2,1)S(1)}, u32[]{:S(2)}, u32[]{:S(2)}) collective-permute-start(bf16[320,128]{1,0:T(8,128)(2,1)S(1)} %get-tuple-element.49), channel_id=1, source_target_pairs={{0,16},{32,48},{64,80},{96,112},{128,144},{160,176},{192,208},{224... | collective-permute-start | bytes 245768 | tf_op jit(solution)/shard_map/ppermute | solution.py:69
  53.2 5.5 %collective-permute-start.7 = (bf16[320,128]{1,0:T(8,128)(2,1)S(1)}, bf16[320,128]{1,0:T(8,128)(2,1)S(1)}, u32[]{:S(2)}, u32[]{:S(2)}) collective-permute-start(bf16[320,128]{1,0:T(8,128)(2,1)S(1)} %get-tuple-element.50), channel_id=1, source_target_pairs={{0,1},{2,3},{4,5},{6,7},{8,9},{10,11},{12,13},{14,15},{1,0},{3,2},... | collective-permute-start | bytes 245768 | tf_op jit(solution)/shard_map/ppermute | solution.py:69
  53.2 7.5 %collective-permute-start.4 = (bf16[320,128]{1,0:T(8,128)(2,1)S(1)}, bf16[320,128]{1,0:T(8,128)(2,1)S(1)}, u32[]{:S(2)}, u32[]{:S(2)}) collective-permute-start(bf16[320,128]{1,0:T(8,128)(2,1)S(1)} %get-tuple-element.47.own), channel_id=1, source_target_pairs={{1,2},{3,4},{5,6},{7,8},{9,10},{11,12},{13,14},{15,0},{2,1},{4,3},... | collective-permute-start | bytes 245768 | tf_op jit(solution)/shard_map/ppermute | solution.py:69
  62.3 8.8 %collective-permute-start.8 = (bf16[512,128]{1,0:T(8,128)(2,1)S(1)}, bf16[512,128]{1,0:T(8,128)(2,1)S(1)}, u32[]{:S(2)}, u32[]{:S(2)}) collective-permute-start(bf16[512,128]{1,0:T(8,128)(2,1)S(1)} %get-tuple-element.57), channel_id=1, source_target_pairs={{1,2},{3,4},{5,6},{7,8},{9,10},{11,12},{13,14},{15,0},{2,1},{4,3},... | collective-permute-start | bytes 393224 | tf_op jit(solution)/shard_map/ppermute | solution.py:69
  63.1 8.1 %collective-permute-start.9 = (bf16[512,128]{1,0:T(8,128)(2,1)S(1)}, bf16[512,128]{1,0:T(8,128)(2,1)S(1)}, u32[]{:S(2)}, u32[]{:S(2)}) collective-permute-start(bf16[512,128]{1,0:T(8,128)(2,1)S(1)} %get-tuple-element.58), channel_id=1, source_target_pairs={{16,32},{48,64},{80,96},{112,128},{144,160},{176,192},{208,224},{2... | collective-permute-start | bytes 393224 | tf_op jit(solution)/shard_map/ppermute | solution.py:69
  65.1 7.0 %collective-permute-start.10 = (bf16[512,128]{1,0:T(8,128)(2,1)S(1)}, bf16[512,128]{1,0:T(8,128)(2,1)S(1)}, u32[]{:S(2)}, u32[]{:S(2)}) collective-permute-start(bf16[512,128]{1,0:T(8,128)(2,1)S(1)} %get-tuple-element.59), channel_id=1, source_target_pairs={{0,16},{32,48},{64,80},{96,112},{128,144},{160,176},{192,208},{224... | collective-permute-start | bytes 393224 | tf_op jit(solution)/shard_map/ppermute | solution.py:69
  66.7 5.5 %collective-permute-start.11 = (bf16[512,128]{1,0:T(8,128)(2,1)S(1)}, bf16[512,128]{1,0:T(8,128)(2,1)S(1)}, u32[]{:S(2)}, u32[]{:S(2)}) collective-permute-start(bf16[512,128]{1,0:T(8,128)(2,1)S(1)} %get-tuple-element.60), channel_id=1, source_target_pairs={{0,1},{2,3},{4,5},{6,7},{8,9},{10,11},{12,13},{14,15},{1,0},{3,2},... | collective-permute-start | bytes 393224 | tf_op jit(solution)/shard_map/ppermute | solution.py:69
  104.0 3.7 %collective-permute-start.15 = (bf16[64,128]{1,0:T(8,128)(2,1)S(1)}, bf16[64,128]{1,0:T(8,128)(2,1)S(1)}, u32[]{:S(2)}, u32[]{:S(2)}) collective-permute-start(bf16[64,128]{1,0:T(8,128)(2,1)S(1)} %shard_map.54.own), channel_id=1, source_target_pairs={{0,1},{2,3},{4,5},{6,7},{8,9},{10,11},{12,13},{14,15},{1,0},{3,2},... | collective-permute-start | bytes 49160 | tf_op jit(solution)/shard_map/ppermute | solution.py:69
  104.2 3.9 %collective-permute-start.14 = (bf16[64,128]{1,0:T(8,128)(2,1)S(1)}, bf16[64,128]{1,0:T(8,128)(2,1)S(1)}, u32[]{:S(2)}, u32[]{:S(2)}) collective-permute-start(bf16[64,128]{1,0:T(8,128)(2,1)S(1)} %shard_map.54.own), channel_id=1, source_target_pairs={{0,16},{32,48},{64,80},{96,112},{128,144},{160,176},{192,208},{224... | collective-permute-start | bytes 49160 | tf_op jit(solution)/shard_map/ppermute | solution.py:69
  104.4 4.7 %collective-permute-start.13 = (bf16[64,128]{1,0:T(8,128)(2,1)S(1)}, bf16[64,128]{1,0:T(8,128)(2,1)S(1)}, u32[]{:S(2)}, u32[]{:S(2)}) collective-permute-start(bf16[64,128]{1,0:T(8,128)(2,1)S(1)} %shard_map.54.own), channel_id=1, source_target_pairs={{16,32},{48,64},{80,96},{112,128},{144,160},{176,192},{208,224},{2... | collective-permute-start | bytes 49160 | tf_op jit(solution)/shard_map/ppermute | solution.py:69
  107.4 6.8 %collective-permute-start.12 = (bf16[64,128]{1,0:T(8,128)(2,1)S(1)}, bf16[64,128]{1,0:T(8,128)(2,1)S(1)}, u32[]{:S(2)}, u32[]{:S(2)}) collective-permute-start(bf16[64,128]{1,0:T(8,128)(2,1)S(1)} %shard_map.54.own), channel_id=1, source_target_pairs={{1,2},{3,4},{5,6},{7,8},{9,10},{11,12},{13,14},{15,0},{2,1},{4,3},... | collective-permute-start | bytes 49160 | tf_op jit(solution)/shard_map/ppermute | solution.py:69
  117.1 9.7 %collective-permute-start.18 = (bf16[512,128]{1,0:T(8,128)(2,1)S(1)}, bf16[512,128]{1,0:T(8,128)(2,1)S(1)}, u32[]{:S(2)}, u32[]{:S(2)}) collective-permute-start(bf16[512,128]{1,0:T(8,128)(2,1)S(1)} %get-tuple-element.71), channel_id=1, source_target_pairs={{0,16},{32,48},{64,80},{96,112},{128,144},{160,176},{192,208},{224... | collective-permute-start | bytes 393224 | tf_op jit(solution)/shard_map/ppermute | solution.py:69
  117.2 9.6 %collective-permute-start.19 = (bf16[512,128]{1,0:T(8,128)(2,1)S(1)}, bf16[512,128]{1,0:T(8,128)(2,1)S(1)}, u32[]{:S(2)}, u32[]{:S(2)}) collective-permute-start(bf16[512,128]{1,0:T(8,128)(2,1)S(1)} %get-tuple-element.72), channel_id=1, source_target_pairs={{0,1},{2,3},{4,5},{6,7},{8,9},{10,11},{12,13},{14,15},{1,0},{3,2},... | collective-permute-start | bytes 393224 | tf_op jit(solution)/shard_map/ppermute | solution.py:69
  117.3 9.5 %collective-permute-start.16 = (bf16[512,128]{1,0:T(8,128)(2,1)S(1)}, bf16[512,128]{1,0:T(8,128)(2,1)S(1)}, u32[]{:S(2)}, u32[]{:S(2)}) collective-permute-start(bf16[512,128]{1,0:T(8,128)(2,1)S(1)} %get-tuple-element.69), channel_id=1, source_target_pairs={{1,2},{3,4},{5,6},{7,8},{9,10},{11,12},{13,14},{15,0},{2,1},{4,3},... | collective-permute-start | bytes 393224 | tf_op jit(solution)/shard_map/ppermute | solution.py:69
  117.7 9.1 %collective-permute-start.17 = (bf16[512,128]{1,0:T(8,128)(2,1)S(1)}, bf16[512,128]{1,0:T(8,128)(2,1)S(1)}, u32[]{:S(2)}, u32[]{:S(2)}) collective-permute-start(bf16[512,128]{1,0:T(8,128)(2,1)S(1)} %get-tuple-element.70), channel_id=1, source_target_pairs={{16,32},{48,64},{80,96},{112,128},{144,160},{176,192},{208,224},{2... | collective-permute-start | bytes 393224 | tf_op jit(solution)/shard_map/ppermute | solution.py:69
  157.0 3.8 %collective-permute-start.23 = (bf16[64,128]{1,0:T(8,128)(2,1)S(1)}, bf16[64,128]{1,0:T(8,128)(2,1)S(1)}, u32[]{:S(2)}, u32[]{:S(2)}) collective-permute-start(bf16[64,128]{1,0:T(8,128)(2,1)S(1)} %shard_map.59.own), channel_id=1, source_target_pairs={{0,1},{2,3},{4,5},{6,7},{8,9},{10,11},{12,13},{14,15},{1,0},{3,2},... | collective-permute-start | bytes 49160 | tf_op jit(solution)/shard_map/ppermute | solution.py:69
  157.2 3.7 %collective-permute-start.22 = (bf16[64,128]{1,0:T(8,128)(2,1)S(1)}, bf16[64,128]{1,0:T(8,128)(2,1)S(1)}, u32[]{:S(2)}, u32[]{:S(2)}) collective-permute-start(bf16[64,128]{1,0:T(8,128)(2,1)S(1)} %shard_map.59.own), channel_id=1, source_target_pairs={{0,16},{32,48},{64,80},{96,112},{128,144},{160,176},{192,208},{224... | collective-permute-start | bytes 49160 | tf_op jit(solution)/shard_map/ppermute | solution.py:69
  157.7 4.7 %collective-permute-start.21 = (bf16[64,128]{1,0:T(8,128)(2,1)S(1)}, bf16[64,128]{1,0:T(8,128)(2,1)S(1)}, u32[]{:S(2)}, u32[]{:S(2)}) collective-permute-start(bf16[64,128]{1,0:T(8,128)(2,1)S(1)} %shard_map.59.own), channel_id=1, source_target_pairs={{16,32},{48,64},{80,96},{112,128},{144,160},{176,192},{208,224},{2... | collective-permute-start | bytes 49160 | tf_op jit(solution)/shard_map/ppermute | solution.py:69
  160.5 6.8 %collective-permute-start.20 = (bf16[64,128]{1,0:T(8,128)(2,1)S(1)}, bf16[64,128]{1,0:T(8,128)(2,1)S(1)}, u32[]{:S(2)}, u32[]{:S(2)}) collective-permute-start(bf16[64,128]{1,0:T(8,128)(2,1)S(1)} %shard_map.59.own), channel_id=1, source_target_pairs={{1,2},{3,4},{5,6},{7,8},{9,10},{11,12},{13,14},{15,0},{2,1},{4,3},... | collective-permute-start | bytes 49160 | tf_op jit(solution)/shard_map/ppermute | solution.py:69

commit v5 on v4

--- a/solution.py
+++ b/solution.py
@@ -41,7 +41,7 @@
     return [rows[row, 0] for row in range(4)]
 
 
-EXCHANGES = ((1, True), (0, True), (0, False), (1, False))
+EXCHANGES = ((0, False), (0, True), (1, True), (1, False))
 
 
 def face_starts(facts, width):
@@ -70,36 +70,35 @@
     return received
 
 
-def faces_body(facts, loads, tile, operator, *refs):
-    facts = scalars(facts)
-    del tile, operator
-    faces, (right, arrived) = refs[:4], refs[4:]
+def faces_body(which, facts, loads, *refs):
+    facts = scalars(facts)
+    count = which.stop - which.start
+    arrived, refs = refs[-1], refs[-1 - 2 * count : -1]
+    faces, rights = refs[:count], refs[count:]
     width = loads.shape[0] // 4
-    blocks = [pl.ds(start, width) for start in face_starts(facts, width)]
     copies = [
-        pltpu.make_async_copy(loads.at[block, :], right.at[block, :], arrived.at[index])
-        for index, block in enumerate(blocks)
+        pltpu.make_async_copy(loads.at[pl.ds(start, width), :], right, arrived.at[index])
+        for index, (start, right) in enumerate(zip(face_starts(facts, width)[which], rights))
     ]
     for copy in copies:
         copy.start()
-    for copy, block, face in zip(copies, blocks, faces):
+    for copy, right, face in zip(copies, rights, faces):
         copy.wait()
-        face[...] = right[block, :].astype(BF16)
+        face[...] = right[...].astype(BF16)
 
 
 def restrict_body(first, facts, basis, *refs):
     facts = scalars(facts)
-    if first:
-        (values,), refs = refs[:1], refs[1:]
-    else:
-        values, held, refs = refs[:4], refs[4], refs[5:]
+    values, refs = refs[:4], refs[4:]
+    if not first:
+        held, refs = refs[0], refs[1:]
     received, (stepped, coarse) = refs[:4], refs[4:]
     width = stepped.shape[0] // 4
     total = jnp.zeros(coarse.shape[1:], F32)
     sides = from_neighbours(facts, [part[...].astype(F32) for part in received])
     for index, (start, side) in enumerate(zip(face_starts(facts, width), sides)):
         rows = pl.ds(start, width)
-        residual = (values[rows, :] if first else values[index][...]) - side
+        residual = values[index][...] - side
         half = DAMPING * residual
         stepped[rows, :] = half if first else held[rows, :] + half
         total += jnp.dot(basis[:, rows], residual.astype(BF16), preferred_element_type=F32)
@@ -144,35 +143,35 @@
     return stepped[pl.ds(start, width), :] - DAMPING * back
 
 
-def multiplied(facts, which, operator, right, rounded, values, faces):
+def multiplied(which, facts, operator, rounded, refs):
     width = operator.shape[0] // 4
-    for start, value, face in zip(face_starts(facts, width)[which], values, faces):
-        block = pl.ds(start, width)
-        product = jnp.dot(operator[block, :], rounded[...], preferred_element_type=F32)
-        difference = right[block, :] - product
+    count = which.stop - which.start
+    starts = face_starts(facts, width)[which]
+    rights, values, faces = refs[:count], refs[count : 2 * count], refs[2 * count :]
+    for start, right, value, face in zip(starts, rights, values, faces):
+        product = jnp.dot(
+            operator[pl.ds(start, width), :], rounded[...], preferred_element_type=F32
+        )
+        difference = right[...] - product
         value[...] = difference
         face[...] = difference.astype(BF16)
 
 
 def advance_body(facts, stepped, basis, own, operator, right, *refs):
     facts = scalars(facts)
-    slices, theirs = refs[:4], refs[4:8]
-    held, rounded = refs[8:10]
-    values, faces = refs[10:12], refs[12:14]
+    slices, theirs, (held, rounded), outs = refs[:4], refs[4:8], refs[8:10], refs[10:]
     width = held.shape[0] // 4
     rows = basis.shape[0]
-    starts = face_starts(facts, width)
     corrections = from_neighbours(facts, [part[:rows, :] for part in theirs])
-    for start, kept, other in zip(starts, slices, corrections):
+    for start, kept, other in zip(face_starts(facts, width), slices, corrections):
         part = corrected(stepped, basis, own[:rows, :], kept, other, start, width)
         held[pl.ds(start, width), :] = part
         rounded[pl.ds(start, width), :] = part.astype(BF16)
-    multiplied(facts, slice(0, 2), operator, right, rounded, values, faces)
-
-
-def advance_near_body(facts, operator, right, rounded, *refs):
-    facts = scalars(facts)
-    multiplied(facts, slice(2, 4), operator, right, rounded, refs[:2], refs[2:])
+    multiplied(slice(0, 1), facts, operator, rounded, [right, *outs])
+
+
+def more_body(which, facts, operator, rounded, *refs):
+    multiplied(which, scalars(facts), operator, rounded, refs)
 
 
 def finish_body(facts, stepped, basis, own, *refs):
@@ -209,14 +208,19 @@
     message = jax.ShapeDtypeStruct((rows + width * rows // columns, columns), BF16)
 
     facts = place_facts()
-    *faces, right = kernel_call(
-        faces_body,
-        [face] * 4 + [whole],
-        [pltpu.SemaphoreType.DMA((4,))],
-        moved=3 << 20,
-        limit=52 << 20,
-        outside=(1, 2, 3),
-    )(facts, right, tile, operator)
+    part = jax.ShapeDtypeStruct((width, columns), F32)
+    faces, rights = [], []
+    for which, others in ((slice(0, 2), (tile, operator)), (slice(2, 4), ())):
+        made = kernel_call(
+            functools.partial(faces_body, which),
+            [face] * 2 + [part] * 2,
+            [pltpu.SemaphoreType.DMA((2,))],
+            moved=2 << 20,
+            limit=(54016 if which.start == 0 else 51968) << 10,
+            outside=(1, 2, 3),
+        )(facts, right, *others)
+        faces += made[:2]
+        rights += made[2:]
     for step in range(ITERS):
         received = exchange(faces)
         first = step == 0
@@ -225,7 +229,7 @@
             [whole, blocks_x],
             flops=2 * rows * size * columns,
             moved=4 << 20,
-        )(facts, basis, *([right] if first else [*values, held]), *received)
+        )(facts, basis, *(rights if first else [*values, held]), *received)
         gathered = lax.all_to_all(sent, "sx", 0, 0, tiled=True)
         (partial,) = kernel_call(
             tile_body,
@@ -246,20 +250,23 @@
             (own,) = kernel_call(sum_body, [coarse], moved=1 << 18)(parts)
             theirs = exchange([own] * 4)
         if step < ITERS - 1:
-            part = jax.ShapeDtypeStruct((width, columns), F32)
             held, rounded, *others = kernel_call(
                 advance_body,
-                [whole, jax.ShapeDtypeStruct(whole.shape, BF16)] + [part] * 2 + [face] * 2,
-                flops=operator.size * columns,
-                moved=12 << 20,
-            )(facts, stepped, basis, own, operator, right, *slices, *theirs)
-            more = kernel_call(
-                advance_near_body,
-                [part] * 2 + [face] * 2,
-                flops=operator.size * columns,
+                [whole, jax.ShapeDtypeStruct(whole.shape, BF16), part, face],
+                flops=operator.size * columns // 2,
                 moved=8 << 20,
-            )(facts, operator, right, rounded)
-            values, faces = [*others[:2], *more[:2]], [*others[2:], *more[2:]]
+            )(facts, stepped, basis, own, operator, rights[0], *slices, *theirs)
+            values, faces = [others[0]], [others[1]]
+            for which in (slice(1, 2), slice(2, 3), slice(3, 4)):
+                count = which.stop - which.start
+                made = kernel_call(
+                    functools.partial(more_body, which),
+                    [part] * count + [face] * count,
+                    flops=operator.size * columns * count // 2,
+                    moved=count << 22,
+                )(facts, operator, rounded, *rights[which])
+                values += made[:count]
+                faces += made[count:]
         else:
             (out,) = kernel_call(
                 finish_body,
@@ -273,6 +280,4 @@
 
 def solution(mesh):
     placed = P("sx", "sy", None, None)
-    return jax.shard_map(
-        local, mesh=mesh, in_specs=(placed,) * 4, out_specs=placed, check_vma=False
-    )
+    return jax.shard_map(local, mesh=mesh, in_specs=(placed,) * 4, out_specs=placed, check_vma=False)

time: 169 us -> 172 us (1.018)
  the two profiles are of different devices: /device:TPU:32 before, /device:TPU:10 now
where the time goes in v5:
time: 172 us; the launch traced here: 169 us
  blocking collectives  89.5 us (52%)
  starting transfers between devices  31.7 us (18%)
  waiting for transfers between devices  28.2 us (16%)
  Pallas kernels  14.1 us (8%)
  local copies, waits for them, and re-layouts  4.77 us (3%)
    all_to_all x3, blocking collectives, local(): gathered = lax.all_to_all(sent, 'sx', 0, 0, tiled=True)  54.1 us
    all_to_all x3, blocking collectives, local(): parts = lax.all_to_all(partial, 'sy', 0, 0, tiled=True)  35.4 us
    ppermute x24, starting transfers between devices, exchange(): received.append(lax.ppermute(part, name, pairs))  31.7 us
    ppermute x24, waiting for transfers between devices, exchange(): received.append(lax.ppermute(part, name, pairs))  28.2 us
    pallas_call x20, Pallas kernels, kernel_call(): pl.pallas_call(body, out_shape=tuple(outs), in_specs=[HBM if i in outside...  14.1 us
    unnamed x20, local copies, waits for them, and re-layouts  4.7 us
  transfers between devices with their start and end apart: 24, of which 16 were waited for; matrix products, arithmetic and copies ran while one was open for 0% of the time, Pallas kernels for 1%

profile of v5, /device:TPU:10, one launch (start us, length us, event | category | flops | bytes accessed | tf_op | source)
XLA Modules:
  0.0 168.6 jit_solution(6788315032089655821)
XLA Ops:
  0.2 1.4 copy-done.3
  3.8 1.7 %collective-permute-start.2 = (bf16[512,128]{1,0:T(8,128)(2,1)}, bf16[512,128]{1,0:T(8,128)(2,1)S(1)}, u32[]{:S(2)}, u32[]{:S(2)}) collective-permute-start(bf16[512,128]{1,0:T(8,128)(2,1)} %get-tuple-element.49), channel_id=1, source_target_pairs={{1,2},{3,4},{5,6},{7,8},{9,10},{11,12},{13,14},{15,0},{2,1},{4,3},... | collective-permute-start | bytes 393224 | tf_op jit(solution)/shard_map/ppermute | solution.py:69
  7.3 1.4 collective-permute-start
  8.7 2.0 %collective-permute-start.1 = (bf16[512,128]{1,0:T(8,128)(2,1)S(1)}, bf16[512,128]{1,0:T(8,128)(2,1)S(1)}, u32[]{:S(2)}, u32[]{:S(2)}) collective-permute-start(bf16[512,128]{1,0:T(8,128)(2,1)S(1)} %get-tuple-element.48), channel_id=1, source_target_pairs={{16,32},{48,64},{80,96},{112,128},{144,160},{176,192},{208,224},{2... | collective-permute-start | bytes 393224 | tf_op jit(solution)/shard_map/ppermute | solution.py:69
  10.9 5.7 %collective-permute-done.refs_4_ = bf16[512,128]{1,0:T(8,128)(2,1)S(1)} collective-permute-done((bf16[512,128]{1,0:T(8,128)(2,1)S(1)}, bf16[512,128]{1,0:T(8,128)(2,1)S(1)}, u32[]{:S(2)}, u32[]{:S(2)}) %collective-permute-start) | collective-permute-done | bytes 131104 | tf_op jit(solution)/shard_map/ppermute | solution.py:69
  18.5 1.3 shard_map.48
  19.8 20.6 %all_to_all.30.columns = bf16[16,64,128]{2,1,0:T(8,128)(2,1)S(1)} all-to-all(bf16[16,64,128]{2,1,0:T(8,128)(2,1)S(1)} %get-tuple-element.52), channel_id=1, replica_groups=mesh['sx'=16,'sy'=16] {'sx'}, dimensions={0} | all-to-all | bytes 524288 | tf_op jit(solution)/shard_map/all_to_all | solution.py:233
  41.2 11.7 %all_to_all.31.parts = bf16[16,64,128]{2,1,0:T(8,128)(2,1)S(1)} all-to-all(bf16[16,64,128]{2,1,0:T(8,128)(2,1)S(1)} %shard_map.49), channel_id=1, replica_groups=mesh['sx'=16,'sy'=16] {'sy'}, dimensions={0} | all-to-all | bytes 524288 | tf_op jit(solution)/shard_map/all_to_all | solution.py:241
  53.0 1.8 %collective-permute-start.5 = (bf16[320,128]{1,0:T(8,128)(2,1)S(1)}, bf16[320,128]{1,0:T(8,128)(2,1)S(1)}, u32[]{:S(2)}, u32[]{:S(2)}) collective-permute-start(bf16[320,128]{1,0:T(8,128)(2,1)S(1)} %get-tuple-element.54), channel_id=1, source_target_pairs={{16,32},{48,64},{80,96},{112,128},{144,160},{176,192},{208,224},{2... | collective-permute-start | bytes 245768 | tf_op jit(solution)/shard_map/ppermute | solution.py:69
  54.8 1.5 collective-permute-start.6
  57.4 2.5 %collective-permute-done.5.refs_1_.refs_5_ = bf16[320,128]{1,0:T(8,128)(2,1)S(1)} collective-permute-done((bf16[320,128]{1,0:T(8,128)(2,1)S(1)}, bf16[320,128]{1,0:T(8,128)(2,1)S(1)}, u32[]{:S(2)}, u32[]{:S(2)}) %collective-permute-start.5) | collective-permute-done | bytes 81952 | tf_op jit(solution)/shard_map/ppermute | solution.py:69
  59.9 1.3 collective-permute-done.6.refs_2_.refs_6_
  65.2 2.1 %collective-permute-start.8 = (bf16[512,128]{1,0:T(8,128)(2,1)S(1)}, bf16[512,128]{1,0:T(8,128)(2,1)S(1)}, u32[]{:S(2)}, u32[]{:S(2)}) collective-permute-start(bf16[512,128]{1,0:T(8,128)(2,1)S(1)} %get-tuple-element.63), channel_id=1, source_target_pairs={{0,16},{32,48},{64,80},{96,112},{128,144},{160,176},{192,208},{224... | collective-permute-start | bytes 393224 | tf_op jit(solution)/shard_map/ppermute | solution.py:69
  67.3 3.2 %collective-permute-start.10 = (bf16[512,128]{1,0:T(8,128)(2,1)S(1)}, bf16[512,128]{1,0:T(8,128)(2,1)S(1)}, u32[]{:S(2)}, u32[]{:S(2)}) collective-permute-start(bf16[512,128]{1,0:T(8,128)(2,1)S(1)} %get-tuple-element.65), channel_id=1, source_target_pairs={{1,2},{3,4},{5,6},{7,8},{9,10},{11,12},{13,14},{15,0},{2,1},{4,3},... | collective-permute-start | bytes 393224 | tf_op jit(solution)/shard_map/ppermute | solution.py:69
  70.5 1.3 collective-permute-start.9
  71.8 2.7 %collective-permute-done.10.refs_7_ = bf16[512,128]{1,0:T(8,128)(2,1)S(1)} collective-permute-done((bf16[512,128]{1,0:T(8,128)(2,1)S(1)}, bf16[512,128]{1,0:T(8,128)(2,1)S(1)}, u32[]{:S(2)}, u32[]{:S(2)}) %collective-permute-start.10) | collective-permute-done | bytes 131104 | tf_op jit(solution)/shard_map/ppermute | solution.py:69
  74.5 2.2 %collective-permute-done.9.refs_6_ = bf16[512,128]{1,0:T(8,128)(2,1)S(1)} collective-permute-done((bf16[512,128]{1,0:T(8,128)(2,1)S(1)}, bf16[512,128]{1,0:T(8,128)(2,1)S(1)}, u32[]{:S(2)}, u32[]{:S(2)}) %collective-permute-start.9) | collective-permute-done | bytes 131104 | tf_op jit(solution)/shard_map/ppermute | solution.py:69
  77.1 17.0 %all_to_all.32.columns = bf16[16,64,128]{2,1,0:T(8,128)(2,1)S(1)} all-to-all(bf16[16,64,128]{2,1,0:T(8,128)(2,1)S(1)} %get-tuple-element.68), channel_id=1, replica_groups=mesh['sx'=16,'sy'=16] {'sx'}, dimensions={0} | all-to-all | bytes 524288 | tf_op jit(solution)/shard_map/all_to_all | solution.py:233
  94.8 12.1 %all_to_all.33.parts = bf16[16,64,128]{2,1,0:T(8,128)(2,1)S(1)} all-to-all(bf16[16,64,128]{2,1,0:T(8,128)(2,1)S(1)} %shard_map.56), channel_id=1, replica_groups=mesh['sx'=16,'sy'=16] {'sy'}, dimensions={0} | all-to-all | bytes 524288 | tf_op jit(solution)/shard_map/all_to_all | solution.py:241
  108.0 1.7 collective-permute-start.14
  109.6 1.3 collective-permute-start.13
  111.6 2.0 %collective-permute-done.14.refs_6_ = bf16[64,128]{1,0:T(8,128)(2,1)S(1)} collective-permute-done((bf16[64,128]{1,0:T(8,128)(2,1)S(1)}, bf16[64,128]{1,0:T(8,128)(2,1)S(1)}, u32[]{:S(2)}, u32[]{:S(2)}) %collective-permute-start.14) | collective-permute-done | bytes 16416 | tf_op jit(solution)/shard_map/ppermute | solution.py:69
  119.0 2.6 %collective-permute-start.17 = (bf16[512,128]{1,0:T(8,128)(2,1)S(1)}, bf16[512,128]{1,0:T(8,128)(2,1)S(1)}, u32[]{:S(2)}, u32[]{:S(2)}) collective-permute-start(bf16[512,128]{1,0:T(8,128)(2,1)S(1)} %get-tuple-element.76), channel_id=1, source_target_pairs={{16,32},{48,64},{80,96},{112,128},{144,160},{176,192},{208,224},{2... | collective-permute-start | bytes 393224 | tf_op jit(solution)/shard_map/ppermute | solution.py:69
  121.7 1.9 %collective-permute-start.16 = (bf16[512,128]{1,0:T(8,128)(2,1)S(1)}, bf16[512,128]{1,0:T(8,128)(2,1)S(1)}, u32[]{:S(2)}, u32[]{:S(2)}) collective-permute-start(bf16[512,128]{1,0:T(8,128)(2,1)S(1)} %get-tuple-element.75), channel_id=1, source_target_pairs={{0,16},{32,48},{64,80},{96,112},{128,144},{160,176},{192,208},{224... | collective-permute-start | bytes 393224 | tf_op jit(solution)/shard_map/ppermute | solution.py:69
  124.8 2.4 %collective-permute-done.17.refs_6_ = bf16[512,128]{1,0:T(8,128)(2,1)S(1)} collective-permute-done((bf16[512,128]{1,0:T(8,128)(2,1)S(1)}, bf16[512,128]{1,0:T(8,128)(2,1)S(1)}, u32[]{:S(2)}, u32[]{:S(2)}) %collective-permute-start.17) | collective-permute-done | bytes 131104 | tf_op jit(solution)/shard_map/ppermute | solution.py:69
  127.2 2.8 %collective-permute-done.16.refs_5_ = bf16[512,128]{1,0:T(8,128)(2,1)S(1)} collective-permute-done((bf16[512,128]{1,0:T(8,128)(2,1)S(1)}, bf16[512,128]{1,0:T(8,128)(2,1)S(1)}, u32[]{:S(2)}, u32[]{:S(2)}) %collective-permute-start.16) | collective-permute-done | bytes 131104 | tf_op jit(solution)/shard_map/ppermute | solution.py:69
  130.4 16.5 %all_to_all.34.columns = bf16[16,64,128]{2,1,0:T(8,128)(2,1)S(1)} all-to-all(bf16[16,64,128]{2,1,0:T(8,128)(2,1)S(1)} %get-tuple-element.80), channel_id=1, replica_groups=mesh['sx'=16,'sy'=16] {'sx'}, dimensions={0} | all-to-all | bytes 524288 | tf_op jit(solution)/shard_map/all_to_all | solution.py:233
  147.6 11.6 %all_to_all.35.parts = bf16[16,64,128]{2,1,0:T(8,128)(2,1)S(1)} all-to-all(bf16[16,64,128]{2,1,0:T(8,128)(2,1)S(1)} %shard_map.63), channel_id=1, replica_groups=mesh['sx'=16,'sy'=16] {'sy'}, dimensions={0} | all-to-all | bytes 524288 | tf_op jit(solution)/shard_map/all_to_all | solution.py:241
  160.1 1.7 %collective-permute-start.22 = (bf16[64,128]{1,0:T(8,128)(2,1)S(1)}, bf16[64,128]{1,0:T(8,128)(2,1)S(1)}, u32[]{:S(2)}, u32[]{:S(2)}) collective-permute-start(bf16[64,128]{1,0:T(8,128)(2,1)S(1)} %shard_map.64.own), channel_id=1, source_target_pairs={{1,2},{3,4},{5,6},{7,8},{9,10},{11,12},{13,14},{15,0},{2,1},{4,3},... | collective-permute-start | bytes 49160 | tf_op jit(solution)/shard_map/ppermute | solution.py:69
  161.8 1.6 collective-permute-start.21
  163.7 1.9 %collective-permute-done.22.refs_6_ = bf16[64,128]{1,0:T(8,128)(2,1)S(1)} collective-permute-done((bf16[64,128]{1,0:T(8,128)(2,1)S(1)}, bf16[64,128]{1,0:T(8,128)(2,1)S(1)}, u32[]{:S(2)}, u32[]{:S(2)}) %collective-permute-start.22) | collective-permute-done | bytes 16416 | tf_op jit(solution)/shard_map/ppermute | solution.py:69
  167.1 1.3 shard_map.65
  (64 shorter events, 25.5 us)
Async XLA Ops:
  0.0 40.4 %copy-start.1 = (bf16[1,1,1024,1024]{3,2,1,0:T(8,128)(2,1)S(1)}, bf16[1,1,1024,1024]{3,2,1,0:T(8,128)(2,1)}, u32[]{:S(2)}) copy-start(bf16[1,1,1024,1024]{3,2,1,0:T(8,128)(2,1)} %param.7) | copy-start | bytes 6291460
  0.0 16.6 %copy-start.2 = (bf16[1,1,64,2048]{3,2,1,0:T(8,128)(2,1)S(1)}, bf16[1,1,64,2048]{3,2,1,0:T(8,128)(2,1)}, u32[]{:S(2)}) copy-start(bf16[1,1,64,2048]{3,2,1,0:T(8,128)(2,1)} %param.6) | copy-start | bytes 786436
  0.0 40.4 %copy-start = (bf16[1,1,2048,2048]{3,2,1,0:T(8,128)(2,1)S(1)}, bf16[1,1,2048,2048]{3,2,1,0:T(8,128)(2,1)}, u32[]{:S(2)}) copy-start(bf16[1,1,2048,2048]{3,2,1,0:T(8,128)(2,1)} %param.4) | copy-start | bytes 25165828
  0.2 1.4 copy-start.3
  3.8 7.1 %collective-permute-start.2 = (bf16[512,128]{1,0:T(8,128)(2,1)}, bf16[512,128]{1,0:T(8,128)(2,1)S(1)}, u32[]{:S(2)}, u32[]{:S(2)}) collective-permute-start(bf16[512,128]{1,0:T(8,128)(2,1)} %get-tuple-element.49), channel_id=1, source_target_pairs={{1,2},{3,4},{5,6},{7,8},{9,10},{11,12},{13,14},{15,0},{2,1},{4,3},... | collective-permute-start | bytes 393224 | tf_op jit(solution)/shard_map/ppermute | solution.py:69
  5.5 5.4 %collective-permute-start.3 = (bf16[512,128]{1,0:T(8,128)(2,1)}, bf16[512,128]{1,0:T(8,128)(2,1)}, u32[]{:S(2)}, u32[]{:S(2)}) collective-permute-start(bf16[512,128]{1,0:T(8,128)(2,1)} %get-tuple-element.50), channel_id=1, source_target_pairs={{0,1},{2,3},{4,5},{6,7},{8,9},{10,11},{12,13},{14,15},{1,0},{3,2},... | collective-permute-start | bytes 393224 | tf_op jit(solution)/shard_map/ppermute | solution.py:69
  7.3 9.3 %collective-permute-start = (bf16[512,128]{1,0:T(8,128)(2,1)S(1)}, bf16[512,128]{1,0:T(8,128)(2,1)S(1)}, u32[]{:S(2)}, u32[]{:S(2)}) collective-permute-start(bf16[512,128]{1,0:T(8,128)(2,1)S(1)} %get-tuple-element.47), channel_id=1, source_target_pairs={{0,16},{32,48},{64,80},{96,112},{128,144},{160,176},{192,208},{224... | collective-permute-start | bytes 393224 | tf_op jit(solution)/shard_map/ppermute | solution.py:69
  8.7 7.9 %collective-permute-start.1 = (bf16[512,128]{1,0:T(8,128)(2,1)S(1)}, bf16[512,128]{1,0:T(8,128)(2,1)S(1)}, u32[]{:S(2)}, u32[]{:S(2)}) collective-permute-start(bf16[512,128]{1,0:T(8,128)(2,1)S(1)} %get-tuple-element.48), channel_id=1, source_target_pairs={{16,32},{48,64},{80,96},{112,128},{144,160},{176,192},{208,224},{2... | collective-permute-start | bytes 393224 | tf_op jit(solution)/shard_map/ppermute | solution.py:69
  16.6 1.0 copy-start.5
  17.6 0.9 copy-start.8
  41.2 21.8 %copy-start.9 = (f32[512,128]{1,0:T(8,128)S(1)}, f32[512,128]{1,0:T(8,128)}, u32[]{:S(2)}) copy-start(f32[512,128]{1,0:T(8,128)} %copy-done.7) | copy-start | bytes 786436
  53.0 6.8 %collective-permute-start.5 = (bf16[320,128]{1,0:T(8,128)(2,1)S(1)}, bf16[320,128]{1,0:T(8,128)(2,1)S(1)}, u32[]{:S(2)}, u32[]{:S(2)}) collective-permute-start(bf16[320,128]{1,0:T(8,128)(2,1)S(1)} %get-tuple-element.54), channel_id=1, source_target_pairs={{16,32},{48,64},{80,96},{112,128},{144,160},{176,192},{208,224},{2... | collective-permute-start | bytes 245768 | tf_op jit(solution)/shard_map/ppermute | solution.py:69
  54.8 6.4 %collective-permute-start.6 = (bf16[320,128]{1,0:T(8,128)(2,1)S(1)}, bf16[320,128]{1,0:T(8,128)(2,1)S(1)}, u32[]{:S(2)}, u32[]{:S(2)}) collective-permute-start(bf16[320,128]{1,0:T(8,128)(2,1)S(1)} %get-tuple-element.55), channel_id=1, source_target_pairs={{1,2},{3,4},{5,6},{7,8},{9,10},{11,12},{13,14},{15,0},{2,1},{4,3},... | collective-permute-start | bytes 245768 | tf_op jit(solution)/shard_map/ppermute | solution.py:69
  56.3 4.9 %collective-permute-start.7 = (bf16[320,128]{1,0:T(8,128)(2,1)S(1)}, bf16[320,128]{1,0:T(8,128)(2,1)S(1)}, u32[]{:S(2)}, u32[]{:S(2)}) collective-permute-start(bf16[320,128]{1,0:T(8,128)(2,1)S(1)} %get-tuple-element.56), channel_id=1, source_target_pairs={{0,1},{2,3},{4,5},{6,7},{8,9},{10,11},{12,13},{14,15},{1,0},{3,2},... | collective-permute-start | bytes 245768 | tf_op jit(solution)/shard_map/ppermute | solution.py:69
  56.3 5.6 %collective-permute-start.4 = (bf16[320,128]{1,0:T(8,128)(2,1)S(1)}, bf16[320,128]{1,0:T(8,128)(2,1)S(1)}, u32[]{:S(2)}, u32[]{:S(2)}) collective-permute-start(bf16[320,128]{1,0:T(8,128)(2,1)S(1)} %get-tuple-element.53.own), channel_id=1, source_target_pairs={{0,16},{32,48},{64,80},{96,112},{128,144},{160,176},{192,208},{224... | collective-permute-start | bytes 245768 | tf_op jit(solution)/shard_map/ppermute | solution.py:69
  61.9 1.9 %copy-start.6 = (f32[512,128]{1,0:T(8,128)S(1)}, f32[512,128]{1,0:T(8,128)}, u32[]{:S(2)}) copy-start(f32[512,128]{1,0:T(8,128)} %copy-done.4) | copy-start | bytes 786436
  65.2 6.6 %collective-permute-start.8 = (bf16[512,128]{1,0:T(8,128)(2,1)S(1)}, bf16[512,128]{1,0:T(8,128)(2,1)S(1)}, u32[]{:S(2)}, u32[]{:S(2)}) collective-permute-start(bf16[512,128]{1,0:T(8,128)(2,1)S(1)} %get-tuple-element.63), channel_id=1, source_target_pairs={{0,16},{32,48},{64,80},{96,112},{128,144},{160,176},{192,208},{224... | collective-permute-start | bytes 393224 | tf_op jit(solution)/shard_map/ppermute | solution.py:69
  67.3 4.5 %collective-permute-start.11 = (bf16[512,128]{1,0:T(8,128)(2,1)S(1)}, bf16[512,128]{1,0:T(8,128)(2,1)S(1)}, u32[]{:S(2)}, u32[]{:S(2)}) collective-permute-start(bf16[512,128]{1,0:T(8,128)(2,1)S(1)} %get-tuple-element.66), channel_id=1, source_target_pairs={{0,1},{2,3},{4,5},{6,7},{8,9},{10,11},{12,13},{14,15},{1,0},{3,2},... | collective-permute-start | bytes 393224 | tf_op jit(solution)/shard_map/ppermute | solution.py:69
  67.3 7.2 %collective-permute-start.10 = (bf16[512,128]{1,0:T(8,128)(2,1)S(1)}, bf16[512,128]{1,0:T(8,128)(2,1)S(1)}, u32[]{:S(2)}, u32[]{:S(2)}) collective-permute-start(bf16[512,128]{1,0:T(8,128)(2,1)S(1)} %get-tuple-element.65), channel_id=1, source_target_pairs={{1,2},{3,4},{5,6},{7,8},{9,10},{11,12},{13,14},{15,0},{2,1},{4,3},... | collective-permute-start | bytes 393224 | tf_op jit(solution)/shard_map/ppermute | solution.py:69
  70.5 6.2 %collective-permute-start.9 = (bf16[512,128]{1,0:T(8,128)(2,1)S(1)}, bf16[512,128]{1,0:T(8,128)(2,1)S(1)}, u32[]{:S(2)}, u32[]{:S(2)}) collective-permute-start(bf16[512,128]{1,0:T(8,128)(2,1)S(1)} %get-tuple-element.64), channel_id=1, source_target_pairs={{16,32},{48,64},{80,96},{112,128},{144,160},{176,192},{208,224},{2... | collective-permute-start | bytes 393224 | tf_op jit(solution)/shard_map/ppermute | solution.py:69
  106.9 4.7 %collective-permute-start.15 = (bf16[64,128]{1,0:T(8,128)(2,1)S(1)}, bf16[64,128]{1,0:T(8,128)(2,1)S(1)}, u32[]{:S(2)}, u32[]{:S(2)}) collective-permute-start(bf16[64,128]{1,0:T(8,128)(2,1)S(1)} %shard_map.57.own), channel_id=1, source_target_pairs={{0,1},{2,3},{4,5},{6,7},{8,9},{10,11},{12,13},{14,15},{1,0},{3,2},... | collective-permute-start | bytes 49160 | tf_op jit(solution)/shard_map/ppermute | solution.py:69
  108.0 5.6 %collective-permute-start.14 = (bf16[64,128]{1,0:T(8,128)(2,1)S(1)}, bf16[64,128]{1,0:T(8,128)(2,1)S(1)}, u32[]{:S(2)}, u32[]{:S(2)}) collective-permute-start(bf16[64,128]{1,0:T(8,128)(2,1)S(1)} %shard_map.57.own), channel_id=1, source_target_pairs={{1,2},{3,4},{5,6},{7,8},{9,10},{11,12},{13,14},{15,0},{2,1},{4,3},... | collective-permute-start | bytes 49160 | tf_op jit(solution)/shard_map/ppermute | solution.py:69
  109.6 4.6 %collective-permute-start.13 = (bf16[64,128]{1,0:T(8,128)(2,1)S(1)}, bf16[64,128]{1,0:T(8,128)(2,1)S(1)}, u32[]{:S(2)}, u32[]{:S(2)}) collective-permute-start(bf16[64,128]{1,0:T(8,128)(2,1)S(1)} %shard_map.57.own), channel_id=1, source_target_pairs={{16,32},{48,64},{80,96},{112,128},{144,160},{176,192},{208,224},{2... | collective-permute-start | bytes 49160 | tf_op jit(solution)/shard_map/ppermute | solution.py:69
  110.9 3.7 %collective-permute-start.12 = (bf16[64,128]{1,0:T(8,128)(2,1)S(1)}, bf16[64,128]{1,0:T(8,128)(2,1)S(1)}, u32[]{:S(2)}, u32[]{:S(2)}) collective-permute-start(bf16[64,128]{1,0:T(8,128)(2,1)S(1)} %shard_map.57.own), channel_id=1, source_target_pairs={{0,16},{32,48},{64,80},{96,112},{128,144},{160,176},{192,208},{224... | collective-permute-start | bytes 49160 | tf_op jit(solution)/shard_map/ppermute | solution.py:69
  117.9 6.9 %collective-permute-start.18 = (bf16[512,128]{1,0:T(8,128)(2,1)S(1)}, bf16[512,128]{1,0:T(8,128)(2,1)S(1)}, u32[]{:S(2)}, u32[]{:S(2)}) collective-permute-start(bf16[512,128]{1,0:T(8,128)(2,1)S(1)} %get-tuple-element.77), channel_id=1, source_target_pairs={{1,2},{3,4},{5,6},{7,8},{9,10},{11,12},{13,14},{15,0},{2,1},{4,3},... | collective-permute-start | bytes 393224 | tf_op jit(solution)/shard_map/ppermute | solution.py:69
  119.0 8.2 %collective-permute-start.17 = (bf16[512,128]{1,0:T(8,128)(2,1)S(1)}, bf16[512,128]{1,0:T(8,128)(2,1)S(1)}, u32[]{:S(2)}, u32[]{:S(2)}) collective-permute-start(bf16[512,128]{1,0:T(8,128)(2,1)S(1)} %get-tuple-element.76), channel_id=1, source_target_pairs={{16,32},{48,64},{80,96},{112,128},{144,160},{176,192},{208,224},{2... | collective-permute-start | bytes 393224 | tf_op jit(solution)/shard_map/ppermute | solution.py:69
  121.6 5.7 %collective-permute-start.19 = (bf16[512,128]{1,0:T(8,128)(2,1)S(1)}, bf16[512,128]{1,0:T(8,128)(2,1)S(1)}, u32[]{:S(2)}, u32[]{:S(2)}) collective-permute-start(bf16[512,128]{1,0:T(8,128)(2,1)S(1)} %get-tuple-element.78), channel_id=1, source_target_pairs={{0,1},{2,3},{4,5},{6,7},{8,9},{10,11},{12,13},{14,15},{1,0},{3,2},... | collective-permute-start | bytes 393224 | tf_op jit(solution)/shard_map/ppermute | solution.py:69
  121.7 8.3 %collective-permute-start.16 = (bf16[512,128]{1,0:T(8,128)(2,1)S(1)}, bf16[512,128]{1,0:T(8,128)(2,1)S(1)}, u32[]{:S(2)}, u32[]{:S(2)}) collective-permute-start(bf16[512,128]{1,0:T(8,128)(2,1)S(1)} %get-tuple-element.75), channel_id=1, source_target_pairs={{0,16},{32,48},{64,80},{96,112},{128,144},{160,176},{192,208},{224... | collective-permute-start | bytes 393224 | tf_op jit(solution)/shard_map/ppermute | solution.py:69
  159.2 4.5 %collective-permute-start.23 = (bf16[64,128]{1,0:T(8,128)(2,1)S(1)}, bf16[64,128]{1,0:T(8,128)(2,1)S(1)}, u32[]{:S(2)}, u32[]{:S(2)}) collective-permute-start(bf16[64,128]{1,0:T(8,128)(2,1)S(1)} %shard_map.64.own), channel_id=1, source_target_pairs={{0,1},{2,3},{4,5},{6,7},{8,9},{10,11},{12,13},{14,15},{1,0},{3,2},... | collective-permute-start | bytes 49160 | tf_op jit(solution)/shard_map/ppermute | solution.py:69
  160.1 5.6 %collective-permute-start.22 = (bf16[64,128]{1,0:T(8,128)(2,1)S(1)}, bf16[64,128]{1,0:T(8,128)(2,1)S(1)}, u32[]{:S(2)}, u32[]{:S(2)}) collective-permute-start(bf16[64,128]{1,0:T(8,128)(2,1)S(1)} %shard_map.64.own), channel_id=1, source_target_pairs={{1,2},{3,4},{5,6},{7,8},{9,10},{11,12},{13,14},{15,0},{2,1},{4,3},... | collective-permute-start | bytes 49160 | tf_op jit(solution)/shard_map/ppermute | solution.py:69
  161.8 4.6 %collective-permute-start.21 = (bf16[64,128]{1,0:T(8,128)(2,1)S(1)}, bf16[64,128]{1,0:T(8,128)(2,1)S(1)}, u32[]{:S(2)}, u32[]{:S(2)}) collective-permute-start(bf16[64,128]{1,0:T(8,128)(2,1)S(1)} %shard_map.64.own), channel_id=1, source_target_pairs={{16,32},{48,64},{80,96},{112,128},{144,160},{176,192},{208,224},{2... | collective-permute-start | bytes 49160 | tf_op jit(solution)/shard_map/ppermute | solution.py:69
  163.4 3.7 %collective-permute-start.20 = (bf16[64,128]{1,0:T(8,128)(2,1)S(1)}, bf16[64,128]{1,0:T(8,128)(2,1)S(1)}, u32[]{:S(2)}, u32[]{:S(2)}) collective-permute-start(bf16[64,128]{1,0:T(8,128)(2,1)S(1)} %shard_map.64.own), channel_id=1, source_target_pairs={{0,16},{32,48},{64,80},{96,112},{128,144},{160,176},{192,208},{224... | collective-permute-start | bytes 49160 | tf_op jit(solution)/shard_map/ppermute | solution.py:69
  (2 other events, 1.4 us)
